TPU v7x, 32 devices: a whole 2x2x4 slice. The times are simulated.
32 devices in a mesh: row: 4 (over x, core), col: 8 (over z, y).
Axes of the slice: x: 2, y: 2, z: 4, core: 2. Of those that a mesh axis runs over, the one named last changes fastest.
Arguments:
- a_window: bfloat16 [8192, 2048], P(('col', 'row')), may hold values from -0.125 to 0.125
- b_tiles: bfloat16 [4096, 4096], P('col', 'row'), may hold values from -6 to 6
- mask_a: int32 [32, 8], P('col'), may hold values from 0 to 1, as said below
- mask_b: int32 [16, 16], P('col', 'row'), may hold values 0 or 1
Outputs:
- product: bfloat16 [8192, 4096], P('col', 'row')
Inputs may be any that keep to these rules, and one draw needn't show every extreme that they name: `mask_a`: block flags, 1 for an occupied block; the share of occupied blocks varies from block row to block row.
All inputs are finite; a program needn't handle non-finite values. No bound on the sum of `mask_b` on one device may be relied on, other than what follows from the above.
Results may differ from a plain program's by a relative error of at most 0.001.
Values may be sent and summed in bfloat16 or wider, within the bound.
No kernel may reach another device: no remote copies, remote signals or barrier semaphores. Data moves between devices by JAX's collectives and lax.ppermute only.
A program may use at most 64 MiB of HBM per device.

v0:
```python
import jax
import jax.numpy as jnp
from jax import lax
from jax.sharding import PartitionSpec as P

BS = 256
KB = 2
STEPS = 4


def shifted(block, axis, distance):
    devices = range(lax.axis_size(axis))
    route = [((i - distance) % len(devices), i) for i in devices]
    return lax.ppermute(block, axis, route)


def row_flags(flags, count):
    rows = lax.iota(jnp.int32, count) // BS
    return jnp.take(flags, rows, axis=0)


def dense_dot(left, right):
    return jnp.dot(left, right, preferred_element_type=jnp.float32)


def tile_product(a_tile, a_flags, b_live):
    a_live = a_tile * jnp.repeat(a_flags, BS, axis=1).astype(jnp.bfloat16)
    return dense_dot(a_live, b_live)


def shards(a_window, b_tiles, mask_a, mask_b):
    k_width = KB * BS
    rows_all = mask_a.shape[0] * BS
    kblocks = mask_b.shape[0]
    jblocks = mask_b.shape[1]
    b_masked = (
        b_tiles.reshape(kblocks, BS, jblocks, BS) * mask_b[:, None, :, None].astype(jnp.bfloat16)
    ).reshape(b_tiles.shape)
    total = jnp.zeros((rows_all, b_tiles.shape[1]), jnp.float32)
    moving = b_masked
    for step in range(STEPS):
        if step > 0:
            moving = shifted(moving, "col", -1)
        step_flags = mask_a[:, step * KB : (step + 1) * KB]

        def multiply_rows(piece, start, step_flags=step_flags, b_current=moving):
            return tile_product(piece, row_flags(step_flags, piece.shape[0]), b_current)

        term = multiply_rows(
            lax.all_gather(
                a_window[:, step * k_width : (step + 1) * k_width], "row", axis=0, tiled=True
            ),
            jnp.int32(0),
        )
        total = total + term
    return total.astype(jnp.bfloat16)


def solution(mesh):
    return jax.shard_map(
        shards,
        mesh=mesh,
        in_specs=(P(("col", "row"), None), P("col", "row"), P("col", None), P("col", "row")),
        out_specs=P("col", "row"),
        check_vma=False,
    )
```

profile of v0, /device:TPU:0, one launch (start us, length us, event | category | flops | bytes accessed | tf_op | source)
XLA Modules:
  0.0 109.2 jit_solution(3975356078811199286)
XLA Ops:
  6.5 0.0 copy-start.2
  6.5 0.0 all-gather.7.cloned.1.call-start
  6.5 2.3 %fusion.14 = (bf16[256,512]{1,0:T(8,128)(2,1)}, bf16[256,512]{1,0:T(8,128)(2,1)}, bf16[256,512]{1,0:T(8,128)(2,1)}, bf16[256,512]{1,0:T(8,128)(2,1)}) fusion(bf16[256,2048]{1,0:T(8,128)(2,1)} %param.6), kind=kLoop, calls=%fused_computation.28 | loop fusion | bytes 2097152 | tf_op jit(solution)/shard_map/slice | solution.py:51
  8.8 0.0 copy-start.3
  8.8 0.0 all-gather.7.cloned.1.call-update
  8.9 0.0 all-gather.5.cloned.1.call-start
  8.9 0.7 all-gather.5.cloned.1.call-update
  9.6 0.0 all-gather.9.cloned.1.call-start
  9.7 0.7 all-gather.9.cloned.1.call-update
  10.3 0.0 all-gather.11.cloned.1.call-start
  10.4 0.7 convert_element_type.37
  11.1 0.3 mul.24
  11.4 0.2 copy.6
  11.6 0.0 copy-done.2
  11.7 0.4 mul.26
  12.1 0.0 copy-start
  12.1 1.0 copy-done
  13.0 6.0 %collective-permute-start = (bf16[512,1024]{1,0:T(8,128)(2,1)S(1)}, bf16[512,1024]{1,0:T(8,128)(2,1)}, u32[]{:S(2)}, u32[]{:S(2)}) collective-permute-start(bf16[512,1024]{1,0:T(8,128)(2,1)S(1)} %mul.26), channel_id=1, source_target_pairs={{1,0},{2,1},{3,2},{4,3},{5,4},{6,5},{7,6},{0,7},{9,8},{10,9},{11,1... | collective-permute-start | bytes 3145736 | tf_op jit(solution)/shard_map/ppermute | solution.py:14
  19.0 22.4 %collective-permute-done = bf16[512,1024]{1,0:T(8,128)(2,1)} collective-permute-done((bf16[512,1024]{1,0:T(8,128)(2,1)S(1)}, bf16[512,1024]{1,0:T(8,128)(2,1)}, u32[]{:S(2)}, u32[]{:S(2)}) %collective-permute-start) | collective-permute-done | bytes 1048608 | tf_op jit(solution)/shard_map/ppermute | solution.py:14
  41.5 5.3 %collective-permute-start.1 = (bf16[512,1024]{1,0:T(8,128)(2,1)}, bf16[512,1024]{1,0:T(8,128)(2,1)}, u32[]{:S(2)}, u32[]{:S(2)}) collective-permute-start(bf16[512,1024]{1,0:T(8,128)(2,1)} %collective-permute-done), channel_id=1, source_target_pairs={{1,0},{2,1},{3,2},{4,3},{5,4},{6,5},{7,6},{0,7},{9,8},{10,9},{11,1... | collective-permute-start | bytes 3145736 | tf_op jit(solution)/shard_map/ppermute | solution.py:14
  46.7 0.0 all-gather.11.cloned.1.call-update
  46.8 0.0 copy-done.3
  46.8 0.1 fusion.15
  46.9 2.8 %gather_fusion = s32[1024,2]{1,0:T(8,128)S(1)} fusion(s32[4,2]{1,0:T(4,128)S(1)} %get-tuple-element.12, s32[1024]{0:T(1024)S(1)} %fusion.9), kind=kCustom, calls=%fused_computation.clone | custom fusion | bytes 20480 | tf_op jit(solution)/shard_map/jit(_take)/gather | solution.py:19
  49.7 2.8 %gather_fusion.1 = s32[1024,2]{1,0:T(8,128)S(1)} fusion(s32[4,2]{1,0:T(4,128)S(1)} %get-tuple-element.11, s32[1024]{0:T(1024)S(1)} %fusion.9), kind=kCustom, calls=%fused_computation.1.clone | custom fusion | bytes 20480 | tf_op jit(solution)/shard_map/jit(_take)/gather | solution.py:19
  52.5 2.8 %gather_fusion.2 = s32[1024,2]{1,0:T(8,128)S(1)} fusion(s32[4,2]{1,0:T(4,128)S(1)} %get-tuple-element.13, s32[1024]{0:T(1024)S(1)} %fusion.9), kind=kCustom, calls=%fused_computation.2.clone | custom fusion | bytes 20480 | tf_op jit(solution)/shard_map/jit(_take)/gather | solution.py:19
  55.3 2.8 %gather_fusion.3 = s32[1024,2]{1,0:T(8,128)S(1)} fusion(s32[4,2]{1,0:T(4,128)S(1)} %get-tuple-element.10, s32[1024]{0:T(1024)S(1)} %fusion.9), kind=kCustom, calls=%fused_computation.3.clone | custom fusion | bytes 20480 | tf_op jit(solution)/shard_map/jit(_take)/gather | solution.py:19
  58.1 0.3 select_convert_fusion
  58.4 1.2 %broadcast_in_dim.24 = bf16[1024,2,256]{2,1,0:T(2,128)(2,1)S(1)} broadcast(bf16[1024,2]{1,0:T(8,128)(2,1)S(1)} %get-tuple-element.16), dimensions={0,1} | broadcast | bytes 1052672 | tf_op jit(solution)/shard_map/broadcast_in_dim | solution.py:27
  59.7 0.2 copy.8
  59.9 1.2 %broadcast_in_dim.23 = bf16[1024,2,256]{2,1,0:T(2,128)(2,1)S(1)} broadcast(bf16[1024,2]{1,0:T(8,128)(2,1)S(1)} %get-tuple-element.15), dimensions={0,1} | broadcast | bytes 1052672 | tf_op jit(solution)/shard_map/broadcast_in_dim | solution.py:27
  61.2 0.2 copy.7
  61.4 1.2 %broadcast_in_dim.22 = bf16[1024,2,256]{2,1,0:T(2,128)(2,1)S(1)} broadcast(bf16[1024,2]{1,0:T(8,128)(2,1)S(1)} %get-tuple-element.17), dimensions={0,1} | broadcast | bytes 1052672 | tf_op jit(solution)/shard_map/broadcast_in_dim | solution.py:27
  62.7 0.2 copy.5
  62.9 1.2 %broadcast_in_dim.25 = bf16[1024,2,256]{2,1,0:T(2,128)(2,1)S(1)} broadcast(bf16[1024,2]{1,0:T(8,128)(2,1)S(1)} %get-tuple-element.14), dimensions={0,1} | broadcast | bytes 1052672 | tf_op jit(solution)/shard_map/broadcast_in_dim | solution.py:27
  64.2 1.2 %copy.9 = bf16[128,8,2,256]{3,1,2,0:T(8,128)(2,1)} copy(bf16[128,8,2,256]{3,2,1,0:T(2,128)(2,1)S(1)} %bitcast.23) | data formatting | bytes 2097152
  65.4 3.2 %collective-permute-done.1 = bf16[512,1024]{1,0:T(8,128)(2,1)} collective-permute-done((bf16[512,1024]{1,0:T(8,128)(2,1)}, bf16[512,1024]{1,0:T(8,128)(2,1)}, u32[]{:S(2)}, u32[]{:S(2)}) %collective-permute-start.1) | collective-permute-done | bytes 1048608 | tf_op jit(solution)/shard_map/ppermute | solution.py:14
  68.6 5.2 %collective-permute-start.2 = (bf16[512,1024]{1,0:T(8,128)(2,1)}, bf16[512,1024]{1,0:T(8,128)(2,1)}, u32[]{:S(2)}, u32[]{:S(2)}) collective-permute-start(bf16[512,1024]{1,0:T(8,128)(2,1)} %collective-permute-done.1), channel_id=1, source_target_pairs={{1,0},{2,1},{3,2},{4,3},{5,4},{6,5},{7,6},{0,7},{9,8},{10,9},{11,1... | collective-permute-start | bytes 3145736 | tf_op jit(solution)/shard_map/ppermute | solution.py:14
  73.8 0.0 all-gather.7.cloned.1.call-done
  73.8 4.7 %fusion.3 = f32[1024,1024]{1,0:T(8,128)} fusion(bf16[512,1024]{1,0:T(8,128)(2,1)} %collective-permute-done, bf16[1024,512]{1,0:T(8,128)(2,1)} %all-gather.7.cloned.1.call-done, bf16[1024,512]{1,0:T(8,128)(2,1)S(1)} %bitcast.17), kind=kOutput, calls=%fused_computation.8 | convolution fusion | flops 1074266112 | bytes 7340032 | tf_op jit(solution)/shard_map/dot_general | solution.py:23
  78.5 0.0 all-gather.5.cloned.1.call-done
  78.5 4.8 %fusion.5 = f32[1024,1024]{1,0:T(8,128)} fusion(bf16[512,1024]{1,0:T(8,128)(2,1)} %copy-done, bf16[1024,512]{1,0:T(8,128)(2,1)} %all-gather.5.cloned.1.call-done, bf16[1024,512]{1,0:T(8,128)(2,1)S(1)} %bitcast.16), kind=kOutput, calls=%fused_computation.10 | convolution fusion | flops 1074266112 | bytes 7340032 | tf_op jit(solution)/shard_map/dot_general | solution.py:23
  83.3 0.0 all-gather.9.cloned.1.call-done
  83.3 0.0 copy-start.1
  83.3 4.8 %fusion.1 = f32[1024,1024]{1,0:T(8,128)} fusion(bf16[512,1024]{1,0:T(8,128)(2,1)} %collective-permute-done.1, bf16[1024,512]{1,0:T(8,128)(2,1)} %all-gather.9.cloned.1.call-done, bf16[1024,512]{1,0:T(8,128)(2,1)S(1)} %bitcast.15), kind=kOutput, calls=%fused_computation.6 | convolution fusion | flops 1074266112 | bytes 7340032 | tf_op jit(solution)/shard_map/dot_general | solution.py:23
  88.2 6.5 %collective-permute-done.2 = bf16[512,1024]{1,0:T(8,128)(2,1)} collective-permute-done((bf16[512,1024]{1,0:T(8,128)(2,1)}, bf16[512,1024]{1,0:T(8,128)(2,1)}, u32[]{:S(2)}, u32[]{:S(2)}) %collective-permute-start.2) | collective-permute-done | bytes 1048608 | tf_op jit(solution)/shard_map/ppermute | solution.py:14
  94.7 0.0 copy-done.1
  94.7 7.9 %add_convert_fusion = bf16[1024,1024]{1,0:T(8,128)(2,1)} fusion(f32[1024,1024]{1,0:T(8,128)} %fusion.1, f32[1024,1024]{1,0:T(8,128)} %fusion.5, f32[1024,1024]{1,0:T(8,128)} %fusion.3, bf16[512,1024]{1,0:T(8,128)(2,1)} %collective-permute-done.2, bf16[1024,512]{1,0:T(8,128)(2,1)} %all-gather.11.cloned.1.call-done, bf16[1024,512]{1,0:T(8,128)(2,1)S(1)} %bitcast.18), kind=kOutput, calls=%fused_computation.4 | convolution fusion | flops 1078460416 | bytes 17825792 | tf_op jit(solution)/shard_map/dot_general | solution.py:23
  (3 shorter events, 0.0 us)
Async XLA Ops:
  6.5 5.1 %copy-start.2 = (bf16[512,1024]{1,0:T(8,128)(2,1)S(1)}, bf16[512,1024]{1,0:T(8,128)(2,1)}, u32[]{:S(2)}) copy-start(bf16[512,1024]{1,0:T(8,128)(2,1)} %param.7) | copy-start | bytes 3145732
  6.5 67.2 %all-gather.7.cloned.1.call-start = ((), (), s32[]{:S(2)}) async-start(), calls=%async_computation.1 | async-start | bytes 1310720 | tf_op jit(solution)/shard_map/all_gather | solution.py:50
  8.8 37.9 %copy-start.3 = (s32[4,8]{1,0:T(4,128)S(1)}, s32[4,8]{1,0:T(4,128)}, u32[]{:S(2)}) copy-start(s32[4,8]{1,0:T(4,128)} %param.8) | copy-start | bytes 388
  8.9 69.7 %all-gather.5.cloned.1.call-start = ((), (), s32[]{:S(2)}) async-start(), calls=%async_computation | async-start | bytes 1310720 | tf_op jit(solution)/shard_map/all_gather | solution.py:50
  9.6 73.7 %all-gather.9.cloned.1.call-start = ((), (), s32[]{:S(2)}) async-start(), calls=%async_computation.2 | async-start | bytes 1310720 | tf_op jit(solution)/shard_map/all_gather | solution.py:50
  10.3 77.8 %all-gather.11.cloned.1.call-start = ((), (), s32[]{:S(2)}) async-start(), calls=%async_computation.3 | async-start | bytes 1310720 | tf_op jit(solution)/shard_map/all_gather | solution.py:50
  12.1 1.0 copy-start
  13.0 28.4 %collective-permute-start = (bf16[512,1024]{1,0:T(8,128)(2,1)S(1)}, bf16[512,1024]{1,0:T(8,128)(2,1)}, u32[]{:S(2)}, u32[]{:S(2)}) collective-permute-start(bf16[512,1024]{1,0:T(8,128)(2,1)S(1)} %mul.26), channel_id=1, source_target_pairs={{1,0},{2,1},{3,2},{4,3},{5,4},{6,5},{7,6},{0,7},{9,8},{10,9},{11,1... | collective-permute-start | bytes 3145736 | tf_op jit(solution)/shard_map/ppermute | solution.py:14
  41.5 27.1 %collective-permute-start.1 = (bf16[512,1024]{1,0:T(8,128)(2,1)}, bf16[512,1024]{1,0:T(8,128)(2,1)}, u32[]{:S(2)}, u32[]{:S(2)}) collective-permute-start(bf16[512,1024]{1,0:T(8,128)(2,1)} %collective-permute-done), channel_id=1, source_target_pairs={{1,0},{2,1},{3,2},{4,3},{5,4},{6,5},{7,6},{0,7},{9,8},{10,9},{11,1... | collective-permute-start | bytes 3145736 | tf_op jit(solution)/shard_map/ppermute | solution.py:14
  68.6 26.1 %collective-permute-start.2 = (bf16[512,1024]{1,0:T(8,128)(2,1)}, bf16[512,1024]{1,0:T(8,128)(2,1)}, u32[]{:S(2)}, u32[]{:S(2)}) collective-permute-start(bf16[512,1024]{1,0:T(8,128)(2,1)} %collective-permute-done.1), channel_id=1, source_target_pairs={{1,0},{2,1},{3,2},{4,3},{5,4},{6,5},{7,6},{0,7},{9,8},{10,9},{11,1... | collective-permute-start | bytes 3145736 | tf_op jit(solution)/shard_map/ppermute | solution.py:14
  83.3 11.4 %copy-start.1 = (bf16[128,8,2,256]{3,1,2,0:T(8,128)(2,1)S(1)}, bf16[128,8,2,256]{3,1,2,0:T(8,128)(2,1)}, u32[]{:S(2)}) copy-start(bf16[128,8,2,256]{3,1,2,0:T(8,128)(2,1)} %copy.9) | copy-start | bytes 3145732
Sparse Core Ops, SparseCore 0:
  9.0 19.4 all-gather.6
  30.0 16.7 all-gather.4
  48.3 16.7 all-gather.8
  66.5 16.7 all-gather.10
where the time goes:
time: 109 us
  waiting for transfers between devices  33.6 us (31%)
  matrix products  22.3 us (20%)
  local copies, waits for them, and re-layouts  22 us (20%)
  starting transfers between devices  16.6 us (15%)
  between operations  13.3 us (12%)
  other arithmetic  1.39 us (1%)
    ppermute x3, waiting for transfers between devices, shifted(): return lax.ppermute(block, axis, route)  32.2 us
    dot_general x4, matrix products, dense_dot(): return jnp.dot(left, right, preferred_element_type=jnp.float32)  22.3 us
    ppermute x3, starting transfers between devices, shifted(): return lax.ppermute(block, axis, route)  16.5 us
    gather x4, local copies, waits for them, and re-layouts, row_flags(): return jnp.take(flags, rows, axis=0)  11.2 us
    broadcast_in_dim x4, local copies, waits for them, and re-layouts, tile_product(): a_live = a_tile * jnp.repeat(a_flags, BS, axis=1).astype(jnp.bfloat16)  4.99 us
    unnamed x13, local copies, waits for them, and re-layouts  3.11 us
    slice x1, local copies, waits for them, and re-layouts, shards(): a_window[:, step * k_width:(step + 1) * k_width]  2.29 us
  transfers between devices with their start and end apart: 7, of which 3 were waited for; matrix products, arithmetic and copies ran while one was open for 32% of the time, Pallas kernels for 0%

commit v1 on v0

v1 whole, which is shorter than its diff:
```python
import functools

import jax
import jax.numpy as jnp
from jax import lax
from jax.experimental import pallas as pl
from jax.experimental.pallas import tpu as pltpu
from jax.sharding import PartitionSpec as P

BS = 256
KB = 2
STEPS = 4

VMEM = pltpu.MemorySpace.VMEM
SMEM = pltpu.MemorySpace.SMEM


def moved(block, axis, target):
    count = lax.axis_size(axis)
    return lax.ppermute(block, axis, [(i, target(i) % count) for i in range(count)])


def mask_tile_kernel(flags, tile, *pieces):
    for column, piece in enumerate(pieces):
        for row in range(tile.shape[0] // BS):
            block = tile[row * BS : (row + 1) * BS, column * BS : (column + 1) * BS]
            live = flags[row, column].astype(jnp.float32).astype(block.dtype)
            piece[row * BS : (row + 1) * BS, :] = block * live


def mask_tile(tile, flags):
    depth, width = tile.shape
    columns = width // BS
    return pl.pallas_call(
        mask_tile_kernel,
        out_shape=[jax.ShapeDtypeStruct((depth, BS), tile.dtype)] * columns,
        in_specs=[pl.BlockSpec(memory_space=SMEM), pl.BlockSpec(memory_space=VMEM)],
        out_specs=[pl.BlockSpec(memory_space=VMEM)] * columns,
        name="mask_tile",
    )(flags, tile)


def mask_rows_kernel(spot, flags, rows, out):
    row = spot[0]
    for column in range(rows.shape[1] // BS):
        block = rows[:, column * BS : (column + 1) * BS]
        live = flags[row, column].astype(jnp.float32).astype(block.dtype)
        out[:, column * BS : (column + 1) * BS] = block * live


def mask_rows(rows, flags, block_row):
    return pl.pallas_call(
        mask_rows_kernel,
        out_shape=jax.ShapeDtypeStruct(rows.shape, rows.dtype),
        in_specs=[
            pl.BlockSpec(memory_space=SMEM),
            pl.BlockSpec(memory_space=SMEM),
            pl.BlockSpec(memory_space=VMEM),
        ],
        out_specs=pl.BlockSpec(memory_space=VMEM),
        name="mask_rows",
    )(block_row[None], flags, rows)


def column_kernel(shards, fresh, spots, *refs):
    lefts = refs[:shards]
    rights = refs[shards : shards + STEPS]
    out = refs[shards + STEPS + (0 if fresh else 1)]
    rows = lefts[0].shape[0]
    for index, left in enumerate(lefts):
        total = None
        for step, right in enumerate(rights):
            depth = right.shape[0]
            term = jnp.dot(
                left[:, step * depth : (step + 1) * depth],
                right[...],
                preferred_element_type=jnp.float32,
            )
            total = term if total is None else total + term
        start = pl.multiple_of(spots[index] * rows, rows)
        out[pl.ds(start, rows), :] = total.astype(out.dtype)


def column_product(spots, lefts, rights, product, column, width):
    shards = len(lefts)
    rows_all = shards * lefts[0].shape[0]
    fresh = product is None
    operands = [spots, *lefts, *rights] + ([] if fresh else [product])
    in_specs = [pl.BlockSpec(memory_space=SMEM)]
    in_specs += [pl.BlockSpec(x.shape, lambda i: (0, 0)) for x in (*lefts, *rights)]
    in_specs += [] if fresh else [pl.BlockSpec(memory_space=pl.ANY)]
    return pl.pallas_call(
        functools.partial(column_kernel, shards, fresh),
        grid=(1,),
        out_shape=jax.ShapeDtypeStruct((rows_all, width), lefts[0].dtype),
        in_specs=in_specs,
        out_specs=pl.BlockSpec((rows_all, BS), lambda i: (0, column)),
        input_output_aliases={} if fresh else {len(operands) - 1: 0},
        cost_estimate=pl.CostEstimate(
            flops=2 * rows_all * lefts[0].shape[1] * BS,
            bytes_accessed=2 * (rows_all * lefts[0].shape[1] + lefts[0].shape[1] * BS + rows_all * BS),
            transcendentals=0,
        ),
        compiler_params=pltpu.CompilerParams(vmem_limit_bytes=24 << 20),
        name="column_product",
    )(*operands)


def shards(a_window, b_tiles, mask_a, mask_b):
    rows = a_window.shape[0]
    n_row = lax.axis_size("row")
    me_row = lax.axis_index("row")
    even = lax.axis_index("col") % 2 == 0

    own = mask_tile(b_tiles, mask_b)
    by_two = [moved(piece, "col", lambda i: i - 2) for piece in own]
    by_one = [
        moved(jnp.where(even, far, near), "col", lambda i: i ^ 1) for far, near in zip(by_two, own)
    ]
    by_three = [moved(piece, "col", lambda i: i - 2) for piece in by_one]

    mine = mask_rows(a_window, mask_a, me_row * rows // BS)
    lefts, spots = [], []
    for distance in range(n_row // 2):
        far = mine if distance == 0 else moved(mine, "row", lambda i: i - 2 * distance)
        lefts += [far, moved(far, "row", lambda i: i ^ 1)]
        place = (me_row + 2 * distance) % n_row
        spots += [place, place ^ 1]
    spots = jnp.stack(spots).astype(jnp.int32)

    product = None
    for column in range(len(own)):
        rights = [own[column], by_one[column], by_two[column], by_three[column]]
        product = column_product(spots, lefts, rights, product, column, b_tiles.shape[1])
    return product


def solution(mesh):
    return jax.shard_map(
        shards,
        mesh=mesh,
        in_specs=(P(("col", "row"), None), P("col", "row"), P("col", None), P("col", "row")),
        out_specs=P("col", "row"),
        check_vma=False,
    )
```

time: 109 us -> 69.4 us (0.64)
  matrix products: 22.3 us -> 0 us
  local copies, waits for them, and re-layouts: 22 us -> 1.66 us
  Pallas kernels: 0 us -> 18.4 us
  waiting for transfers between devices: 33.6 us -> 15.9 us
  between operations: 13.3 us -> 0.06 us
  starting transfers between devices: 16.6 us -> 29.2 us
  other arithmetic: 1.39 us -> 3.78 us
    dot_general x4 -> x0, matrix products: 22.3 us -> none  [dense_dot(): return jnp.dot(left, right, preferred_element_type=jnp.float32)]
    pallas_call x0 -> x6, Pallas kernels: none -> 18.4 us  [the longest x4 13.8 us: column_product(): pl.pallas_call(functools.partial(column_kernel, shards, fresh), grid=(1,)...]
    ppermute x3 -> x15, waiting for transfers between devices: 32.2 us -> 15.9 us  [moved(): lax.ppermute(block, axis, [(i, target(i) % count) for i in range(count)])]
    ppermute x3 -> x15, starting transfers between devices: 16.5 us -> 29.2 us  [moved(): lax.ppermute(block, axis, [(i, target(i) % count) for i in range(count)])]
    gather x4 -> x0, local copies, waits for them, and re-layouts: 11.2 us -> none  [row_flags(): return jnp.take(flags, rows, axis=0)]
    broadcast_in_dim x4 -> x0, local copies, waits for them, and re-layouts: 4.99 us -> none  [tile_product(): a_live = a_tile * jnp.repeat(a_flags, BS, axis=1).astype(jnp.bfloat16)]
    select_n x0 -> x4, other arithmetic: none -> 3.7 us  [shards(): jnp.where(even, far, near)]
    slice x2 -> x0, local copies, waits for them, and re-layouts: 2.37 us -> none  [the longest x1 2.29 us: shards(): a_window[:, step * k_width:(step + 1) * k_width]]
  transfers between devices with their start and end apart: 7 -> 15, of which waited for: 3 -> 7; matrix products, arithmetic and copies ran while one was open for 32% -> 5% of each run, Pallas kernels for 0% -> 18%
where the time goes in v1:
time: 69.4 us; the launch traced here: 69 us
  starting transfers between devices  29.2 us (42%)
  Pallas kernels  18.4 us (27%)
  waiting for transfers between devices  15.9 us (23%)
  other arithmetic  3.78 us (5%)
  local copies, waits for them, and re-layouts  1.66 us (2%)
    ppermute x15, starting transfers between devices, moved(): lax.ppermute(block, axis, [(i, target(i) % count) for i in range(count)])  29.2 us
    ppermute x15, waiting for transfers between devices, moved(): lax.ppermute(block, axis, [(i, target(i) % count) for i in range(count)])  15.9 us
    pallas_call x4, Pallas kernels, column_product(): pl.pallas_call(functools.partial(column_kernel, shards, fresh), grid=(1,)...  13.8 us
    select_n x4, other arithmetic, shards(): jnp.where(even, far, near)  3.7 us
    pallas_call x1, Pallas kernels, mask_rows(): pl.pallas_call(mask_rows_kernel, out_shape=jax.ShapeDtypeStruct(rows.shap...  2.35 us
    pallas_call x1, Pallas kernels, mask_tile(): pl.pallas_call(mask_tile_kernel, out_shape=[jax.ShapeDtypeStruct((depth,...  2.25 us
    unnamed x14, local copies, waits for them, and re-layouts  1.66 us
  transfers between devices with their start and end apart: 15, of which 7 were waited for; matrix products, arithmetic and copies ran while one was open for 5% of the time, Pallas kernels for 18%

profile of v1, /device:TPU:0, one launch (start us, length us, event | category | flops | bytes accessed | tf_op | source)
XLA Modules:
  0.0 69.0 jit_solution(8543603293748418390)
XLA Ops:
  0.0 2.3 %mask_rows.1.refs_0_ = bf16[256,2048]{1,0:T(8,128)(2,1)} custom-call(s32[1]{0:T(128)} %bitcast.4.spot, s32[4,8]{1,0:T(4,128)} %flags.2, bf16[256,2048]{1,0:T(8,128)(2,1)} %rows.1), custom_call_target="tpu_custom_call" | custom-call | tf_op jit(solution)/shard_map/mask_rows/pallas_call | solution.py:52
  2.4 2.9 %collective-permute-start.1 = (bf16[256,2048]{1,0:T(8,128)(2,1)}, bf16[256,2048]{1,0:T(8,128)(2,1)S(1)}, u32[]{:S(2)}, u32[]{:S(2)}) collective-permute-start(bf16[256,2048]{1,0:T(8,128)(2,1)} %mask_rows.1.refs_0_), channel_id=1, source_target_pairs={{0,16},{8,24},{16,0},{24,8},{1,17},{9,25},{17,1},{25,9},{2,18},{10... | collective-permute-start | bytes 3145736 | tf_op jit(solution)/shard_map/ppermute | solution.py:20
  5.3 2.3 %mask_tile.1 = (bf16[512,256]{1,0:T(8,128)(2,1)}, bf16[512,256]{1,0:T(8,128)(2,1)}, bf16[512,256]{1,0:T(8,128)(2,1)}, bf16[512,256]{1,0:T(8,128)(2,1)}) custom-call(s32[2,4]{1,0:T(2,128)} %flags.3, bf16[512,1024]{1,0:T(8,128)(2,1)} %tile.1), custom_call_target="tpu_custom_call" | custom-call | tf_op jit(solution)/shard_map/mask_tile/pallas_call | solution.py:34
  7.5 3.6 %collective-permute-start.12 = (bf16[512,256]{1,0:T(8,128)(2,1)}, bf16[512,256]{1,0:T(8,128)(2,1)}, u32[]{:S(2)}, u32[]{:S(2)}) collective-permute-start(bf16[512,256]{1,0:T(8,128)(2,1)} %get-tuple-element.12.refs_4_), channel_id=1, source_target_pairs={{0,6},{1,7},{2,0},{3,1},{4,2},{5,3},{6,4},{7,5},{8,14},{9,15},{10,... | collective-permute-start | bytes 786440 | tf_op jit(solution)/shard_map/ppermute | solution.py:20
  11.1 0.4 collective-permute-start.9
  11.6 0.0 collective-permute-start
  11.6 0.4 collective-permute-start.6
  12.1 6.2 %collective-permute-done.12.refs_6_ = bf16[512,256]{1,0:T(8,128)(2,1)} collective-permute-done((bf16[512,256]{1,0:T(8,128)(2,1)}, bf16[512,256]{1,0:T(8,128)(2,1)}, u32[]{:S(2)}, u32[]{:S(2)}) %collective-permute-start.12) | collective-permute-done | bytes 262176 | tf_op jit(solution)/shard_map/ppermute | solution.py:20
  18.2 4.3 %collective-permute-start.3 = (bf16[512,256]{1,0:T(8,128)(2,1)}, bf16[512,256]{1,0:T(8,128)(2,1)S(1)}, u32[]{:S(2)}, u32[]{:S(2)}) collective-permute-start(bf16[512,256]{1,0:T(8,128)(2,1)} %get-tuple-element.9.refs_4_), channel_id=1, source_target_pairs={{0,6},{1,7},{2,0},{3,1},{4,2},{5,3},{6,4},{7,5},{8,14},{9,15},{10,... | collective-permute-start | bytes 786440 | tf_op jit(solution)/shard_map/ppermute | solution.py:20
  22.5 1.0 %broadcast_select_fusion = bf16[512,256]{1,0:T(8,128)(2,1)S(1)} fusion(bf16[512,256]{1,0:T(8,128)(2,1)} %collective-permute-done.12.refs_6_, bf16[512,256]{1,0:T(8,128)(2,1)} %get-tuple-element.12.refs_4_, pred[]{:T(512)S(6)} %eq.7), kind=kLoop, calls=%fused_computation | loop fusion | flops 131072 | bytes 786433 | tf_op jit(solution)/shard_map/jit(_where)/select_n | solution.py:118
  23.5 0.4 collective-permute-done.9.refs_6_
  23.8 1.5 %collective-permute-start.13 = (bf16[512,256]{1,0:T(8,128)(2,1)S(1)}, bf16[512,256]{1,0:T(8,128)(2,1)}, u32[]{:S(2)}, u32[]{:S(2)}) collective-permute-start(bf16[512,256]{1,0:T(8,128)(2,1)S(1)} %broadcast_select_fusion), channel_id=1, source_target_pairs={{0,1},{1,0},{2,3},{3,2},{4,5},{5,4},{6,7},{7,6},{8,9},{9,8},{10,11... | collective-permute-start | bytes 786440 | tf_op jit(solution)/shard_map/ppermute | solution.py:20
  25.4 3.4 %collective-permute-done.1.refs_2_ = bf16[256,2048]{1,0:T(8,128)(2,1)S(1)} collective-permute-done((bf16[256,2048]{1,0:T(8,128)(2,1)}, bf16[256,2048]{1,0:T(8,128)(2,1)S(1)}, u32[]{:S(2)}, u32[]{:S(2)}) %collective-permute-start.1) | collective-permute-done | bytes 1048608 | tf_op jit(solution)/shard_map/ppermute | solution.py:20
  28.7 0.0 collective-permute-start.2
  28.7 1.0 %broadcast_select_fusion.1 = bf16[512,256]{1,0:T(8,128)(2,1)S(1)} fusion(bf16[512,256]{1,0:T(8,128)(2,1)} %collective-permute-done.9.refs_6_, bf16[512,256]{1,0:T(8,128)(2,1)} %get-tuple-element.11.refs_4_, pred[]{:T(512)S(6)} %eq.7), kind=kLoop, calls=%fused_computation.1 | loop fusion | flops 131072 | bytes 786433 | tf_op jit(solution)/shard_map/jit(_where)/select_n | solution.py:118
  29.7 0.0 collective-permute-done.6.refs_6_
  29.7 1.8 %collective-permute-start.10 = (bf16[512,256]{1,0:T(8,128)(2,1)S(1)}, bf16[512,256]{1,0:T(8,128)(2,1)}, u32[]{:S(2)}, u32[]{:S(2)}) collective-permute-start(bf16[512,256]{1,0:T(8,128)(2,1)S(1)} %broadcast_select_fusion.1), channel_id=1, source_target_pairs={{0,1},{1,0},{2,3},{3,2},{4,5},{5,4},{6,7},{7,6},{8,9},{9,8},{10,11... | collective-permute-start | bytes 786440 | tf_op jit(solution)/shard_map/ppermute | solution.py:20
  31.5 1.0 %broadcast_select_fusion.2 = bf16[512,256]{1,0:T(8,128)(2,1)S(1)} fusion(bf16[512,256]{1,0:T(8,128)(2,1)} %collective-permute-done.6.refs_6_, bf16[512,256]{1,0:T(8,128)(2,1)} %get-tuple-element.10.refs_4_, pred[]{:T(512)S(6)} %eq.7), kind=kLoop, calls=%fused_computation.2 | loop fusion | flops 131072 | bytes 786433 | tf_op jit(solution)/shard_map/jit(_where)/select_n | solution.py:118
  32.5 1.1 %collective-permute-done.3.refs_6_ = bf16[512,256]{1,0:T(8,128)(2,1)S(1)} collective-permute-done((bf16[512,256]{1,0:T(8,128)(2,1)}, bf16[512,256]{1,0:T(8,128)(2,1)S(1)}, u32[]{:S(2)}, u32[]{:S(2)}) %collective-permute-start.3) | collective-permute-done | bytes 262176 | tf_op jit(solution)/shard_map/ppermute | solution.py:20
  33.6 1.5 %collective-permute-start.7 = (bf16[512,256]{1,0:T(8,128)(2,1)S(1)}, bf16[512,256]{1,0:T(8,128)(2,1)}, u32[]{:S(2)}, u32[]{:S(2)}) collective-permute-start(bf16[512,256]{1,0:T(8,128)(2,1)S(1)} %broadcast_select_fusion.2), channel_id=1, source_target_pairs={{0,1},{1,0},{2,3},{3,2},{4,5},{5,4},{6,7},{7,6},{8,9},{9,8},{10,11... | collective-permute-start | bytes 786440 | tf_op jit(solution)/shard_map/ppermute | solution.py:20
  35.1 0.0 copy-done.1
  35.1 0.8 %broadcast_select_fusion.3 = bf16[512,256]{1,0:T(8,128)(2,1)} fusion(bf16[512,256]{1,0:T(8,128)(2,1)S(1)} %collective-permute-done.3.refs_6_, bf16[512,256]{1,0:T(8,128)(2,1)S(1)} %copy-done.1, pred[]{:T(512)S(6)} %eq.7), kind=kLoop, calls=%fused_computation.3 | loop fusion | flops 131072 | bytes 786433 | tf_op jit(solution)/shard_map/jit(_where)/select_n | solution.py:118
  35.9 0.7 %copy-done.4 = bf16[512,256]{1,0:T(8,128)(2,1)} copy-done((bf16[512,256]{1,0:T(8,128)(2,1)}, bf16[512,256]{1,0:T(8,128)(2,1)S(1)}, u32[]{:S(2)}) %copy-start.4) | copy-done | bytes 262168
  36.6 0.0 collective-permute-done.13.refs_5_
  36.6 0.5 collective-permute-start.4
  37.1 1.9 %collective-permute-done.10.refs_5_ = bf16[512,256]{1,0:T(8,128)(2,1)} collective-permute-done((bf16[512,256]{1,0:T(8,128)(2,1)S(1)}, bf16[512,256]{1,0:T(8,128)(2,1)}, u32[]{:S(2)}, u32[]{:S(2)}) %collective-permute-start.10) | collective-permute-done | bytes 262176 | tf_op jit(solution)/shard_map/ppermute | solution.py:20
  39.0 4.0 %collective-permute-start.14 = (bf16[512,256]{1,0:T(8,128)(2,1)}, bf16[512,256]{1,0:T(8,128)(2,1)}, u32[]{:S(2)}, u32[]{:S(2)}) collective-permute-start(bf16[512,256]{1,0:T(8,128)(2,1)} %collective-permute-done.13.refs_5_), channel_id=1, source_target_pairs={{0,6},{1,7},{2,0},{3,1},{4,2},{5,3},{6,4},{7,5},{8,14},{9,15},{10,... | collective-permute-start | bytes 786440 | tf_op jit(solution)/shard_map/ppermute | solution.py:20
  43.0 1.7 %collective-permute-done.7.refs_5_ = bf16[512,256]{1,0:T(8,128)(2,1)} collective-permute-done((bf16[512,256]{1,0:T(8,128)(2,1)S(1)}, bf16[512,256]{1,0:T(8,128)(2,1)}, u32[]{:S(2)}, u32[]{:S(2)}) %collective-permute-start.7) | collective-permute-done | bytes 262176 | tf_op jit(solution)/shard_map/ppermute | solution.py:20
  44.6 4.0 %collective-permute-start.11 = (bf16[512,256]{1,0:T(8,128)(2,1)}, bf16[512,256]{1,0:T(8,128)(2,1)}, u32[]{:S(2)}, u32[]{:S(2)}) collective-permute-start(bf16[512,256]{1,0:T(8,128)(2,1)} %collective-permute-done.10.refs_5_), channel_id=1, source_target_pairs={{0,6},{1,7},{2,0},{3,1},{4,2},{5,3},{6,4},{7,5},{8,14},{9,15},{10,... | collective-permute-start | bytes 786440 | tf_op jit(solution)/shard_map/ppermute | solution.py:20
  48.6 1.3 %collective-permute-done.4.refs_5_ = bf16[512,256]{1,0:T(8,128)(2,1)} collective-permute-done((bf16[512,256]{1,0:T(8,128)(2,1)}, bf16[512,256]{1,0:T(8,128)(2,1)}, u32[]{:S(2)}, u32[]{:S(2)}) %collective-permute-start.4) | collective-permute-done | bytes 262176 | tf_op jit(solution)/shard_map/ppermute | solution.py:20
  49.9 3.8 %collective-permute-start.8 = (bf16[512,256]{1,0:T(8,128)(2,1)}, bf16[512,256]{1,0:T(8,128)(2,1)S(1)}, u32[]{:S(2)}, u32[]{:S(2)}) collective-permute-start(bf16[512,256]{1,0:T(8,128)(2,1)} %collective-permute-done.7.refs_5_), channel_id=1, source_target_pairs={{0,6},{1,7},{2,0},{3,1},{4,2},{5,3},{6,4},{7,5},{8,14},{9,15},{10,... | collective-permute-start | bytes 786440 | tf_op jit(solution)/shard_map/ppermute | solution.py:20
  53.6 0.1 pad_add_fusion.spots
  53.7 0.0 collective-permute-done.14.refs_7_
  53.7 0.5 collective-permute-start.5
  54.2 0.0 collective-permute-done.refs_1_
  54.2 0.0 collective-permute-done.2.refs_3_
  54.2 0.0 copy-done
  54.2 0.0 copy-start.6
  54.2 0.9 %copy-done.6 = bf16[512,256]{1,0:T(8,128)(2,1)S(1)} copy-done((bf16[512,256]{1,0:T(8,128)(2,1)S(1)}, bf16[512,256]{1,0:T(8,128)(2,1)}, u32[]{:S(2)}) %copy-start.6) | copy-done | bytes 262168
  55.2 3.5 %column_product.4.refs_8_ = bf16[1024,1024]{1,0:T(8,128)(2,1)} custom-call(s32[4]{0:T(128)S(1)} %pad_add_fusion.spots, bf16[256,2048]{1,0:T(8,128)(2,1)S(1)} %copy-done, bf16[256,2048]{1,0:T(8,128)(2,1)S(1)} %collective-permute-done.refs_1_, bf16[256,2048]{1,0:T(8,128)(2,1)S(1)} %collective-permute-done.1.refs_2_, ...), custom_call_target="tpu_custom_call" | custom-call | flops 1073741824 | bytes 5767168 | tf_op jit(solution)/shard_map/column_product/pallas_call | solution.py:92
  58.6 0.0 collective-permute-done.11.refs_7_
  58.6 0.0 copy-done.3
  58.6 3.5 %column_product.5.refs_8_ = bf16[1024,1024]{1,0:T(8,128)(2,1)} custom-call(s32[4]{0:T(128)S(1)} %pad_add_fusion.spots, bf16[256,2048]{1,0:T(8,128)(2,1)S(1)} %copy-done, bf16[256,2048]{1,0:T(8,128)(2,1)S(1)} %collective-permute-done.refs_1_, bf16[256,2048]{1,0:T(8,128)(2,1)S(1)} %collective-permute-done.1.refs_2_, ...), custom_call_target="tpu_custom_call", output_to_operand_aliasing={{}: (9, {})} | custom-call | flops 1073741824 | bytes 5767168 | tf_op jit(solution)/shard_map/column_product/pallas_call | solution.py:92
  62.2 0.0 collective-permute-done.8.refs_7_
  62.2 0.0 copy-done.2
  62.2 3.5 %column_product.6.refs_8_ = bf16[1024,1024]{1,0:T(8,128)(2,1)} custom-call(s32[4]{0:T(128)S(1)} %pad_add_fusion.spots, bf16[256,2048]{1,0:T(8,128)(2,1)S(1)} %copy-done, bf16[256,2048]{1,0:T(8,128)(2,1)S(1)} %collective-permute-done.refs_1_, bf16[256,2048]{1,0:T(8,128)(2,1)S(1)} %collective-permute-done.1.refs_2_, ...), custom_call_target="tpu_custom_call", output_to_operand_aliasing={{}: (9, {})} | custom-call | flops 1073741824 | bytes 5767168 | tf_op jit(solution)/shard_map/column_product/pallas_call | solution.py:92
  65.6 0.0 collective-permute-done.5.refs_7_
  65.6 3.3 %column_product.7 = bf16[1024,1024]{1,0:T(8,128)(2,1)} custom-call(s32[4]{0:T(128)S(1)} %pad_add_fusion.spots, bf16[256,2048]{1,0:T(8,128)(2,1)S(1)} %copy-done, bf16[256,2048]{1,0:T(8,128)(2,1)S(1)} %collective-permute-done.refs_1_, bf16[256,2048]{1,0:T(8,128)(2,1)S(1)} %collective-permute-done.1.refs_2_, ...), custom_call_target="tpu_custom_call", output_to_operand_aliasing={{}: (9, {})} | custom-call | flops 1073741824 | bytes 5767168 | tf_op jit(solution)/shard_map/column_product/pallas_call | solution.py:92
  (7 shorter events, 0.0 us)
Async XLA Ops:
  2.3 51.8 %copy-start = (bf16[256,2048]{1,0:T(8,128)(2,1)S(1)}, bf16[256,2048]{1,0:T(8,128)(2,1)}, u32[]{:S(2)}) copy-start(bf16[256,2048]{1,0:T(8,128)(2,1)} %mask_rows.1.refs_0_) | copy-start | bytes 3145732
  2.4 26.4 %collective-permute-start.1 = (bf16[256,2048]{1,0:T(8,128)(2,1)}, bf16[256,2048]{1,0:T(8,128)(2,1)S(1)}, u32[]{:S(2)}, u32[]{:S(2)}) collective-permute-start(bf16[256,2048]{1,0:T(8,128)(2,1)} %mask_rows.1.refs_0_), channel_id=1, source_target_pairs={{0,16},{8,24},{16,0},{24,8},{1,17},{9,25},{17,1},{25,9},{2,18},{10... | collective-permute-start | bytes 3145736 | tf_op jit(solution)/shard_map/ppermute | solution.py:20
  7.5 27.6 %copy-start.1 = (bf16[512,256]{1,0:T(8,128)(2,1)S(1)}, bf16[512,256]{1,0:T(8,128)(2,1)}, u32[]{:S(2)}) copy-start(bf16[512,256]{1,0:T(8,128)(2,1)} %get-tuple-element.9.refs_4_) | copy-start | bytes 786436
  7.5 10.7 %collective-permute-start.12 = (bf16[512,256]{1,0:T(8,128)(2,1)}, bf16[512,256]{1,0:T(8,128)(2,1)}, u32[]{:S(2)}, u32[]{:S(2)}) collective-permute-start(bf16[512,256]{1,0:T(8,128)(2,1)} %get-tuple-element.12.refs_4_), channel_id=1, source_target_pairs={{0,6},{1,7},{2,0},{3,1},{4,2},{5,3},{6,4},{7,5},{8,14},{9,15},{10,... | collective-permute-start | bytes 786440 | tf_op jit(solution)/shard_map/ppermute | solution.py:20
  11.1 12.7 %collective-permute-start.9 = (bf16[512,256]{1,0:T(8,128)(2,1)}, bf16[512,256]{1,0:T(8,128)(2,1)}, u32[]{:S(2)}, u32[]{:S(2)}) collective-permute-start(bf16[512,256]{1,0:T(8,128)(2,1)} %get-tuple-element.11.refs_4_), channel_id=1, source_target_pairs={{0,6},{1,7},{2,0},{3,1},{4,2},{5,3},{6,4},{7,5},{8,14},{9,15},{10,... | collective-permute-start | bytes 786440 | tf_op jit(solution)/shard_map/ppermute | solution.py:20
  11.6 42.6 %collective-permute-start = (bf16[256,2048]{1,0:T(8,128)(2,1)}, bf16[256,2048]{1,0:T(8,128)(2,1)S(1)}, u32[]{:S(2)}, u32[]{:S(2)}) collective-permute-start(bf16[256,2048]{1,0:T(8,128)(2,1)} %mask_rows.1.refs_0_), channel_id=1, source_target_pairs={{0,8},{8,0},{16,24},{24,16},{1,9},{9,1},{17,25},{25,17},{2,10},{10... | collective-permute-start | bytes 3145736 | tf_op jit(solution)/shard_map/ppermute | solution.py:20
  11.6 18.1 %collective-permute-start.6 = (bf16[512,256]{1,0:T(8,128)(2,1)}, bf16[512,256]{1,0:T(8,128)(2,1)}, u32[]{:S(2)}, u32[]{:S(2)}) collective-permute-start(bf16[512,256]{1,0:T(8,128)(2,1)} %get-tuple-element.10.refs_4_), channel_id=1, source_target_pairs={{0,6},{1,7},{2,0},{3,1},{4,2},{5,3},{6,4},{7,5},{8,14},{9,15},{10,... | collective-permute-start | bytes 786440 | tf_op jit(solution)/shard_map/ppermute | solution.py:20
  18.2 15.4 %collective-permute-start.3 = (bf16[512,256]{1,0:T(8,128)(2,1)}, bf16[512,256]{1,0:T(8,128)(2,1)S(1)}, u32[]{:S(2)}, u32[]{:S(2)}) collective-permute-start(bf16[512,256]{1,0:T(8,128)(2,1)} %get-tuple-element.9.refs_4_), channel_id=1, source_target_pairs={{0,6},{1,7},{2,0},{3,1},{4,2},{5,3},{6,4},{7,5},{8,14},{9,15},{10,... | collective-permute-start | bytes 786440 | tf_op jit(solution)/shard_map/ppermute | solution.py:20
  23.8 12.8 %collective-permute-start.13 = (bf16[512,256]{1,0:T(8,128)(2,1)S(1)}, bf16[512,256]{1,0:T(8,128)(2,1)}, u32[]{:S(2)}, u32[]{:S(2)}) collective-permute-start(bf16[512,256]{1,0:T(8,128)(2,1)S(1)} %broadcast_select_fusion), channel_id=1, source_target_pairs={{0,1},{1,0},{2,3},{3,2},{4,5},{5,4},{6,7},{7,6},{8,9},{9,8},{10,11... | collective-permute-start | bytes 786440 | tf_op jit(solution)/shard_map/ppermute | solution.py:20
  28.7 25.5 %collective-permute-start.2 = (bf16[256,2048]{1,0:T(8,128)(2,1)S(1)}, bf16[256,2048]{1,0:T(8,128)(2,1)}, u32[]{:S(2)}, u32[]{:S(2)}) collective-permute-start(bf16[256,2048]{1,0:T(8,128)(2,1)S(1)} %collective-permute-done.1.refs_2_), channel_id=1, source_target_pairs={{0,8},{8,0},{16,24},{24,16},{1,9},{9,1},{17,25},{25,17},{2,10},{10... | collective-permute-start | bytes 3145736 | tf_op jit(solution)/shard_map/ppermute | solution.py:20
  29.7 9.3 %collective-permute-start.10 = (bf16[512,256]{1,0:T(8,128)(2,1)S(1)}, bf16[512,256]{1,0:T(8,128)(2,1)}, u32[]{:S(2)}, u32[]{:S(2)}) collective-permute-start(bf16[512,256]{1,0:T(8,128)(2,1)S(1)} %broadcast_select_fusion.1), channel_id=1, source_target_pairs={{0,1},{1,0},{2,3},{3,2},{4,5},{5,4},{6,7},{7,6},{8,9},{9,8},{10,11... | collective-permute-start | bytes 786440 | tf_op jit(solution)/shard_map/ppermute | solution.py:20
  33.6 11.0 %collective-permute-start.7 = (bf16[512,256]{1,0:T(8,128)(2,1)S(1)}, bf16[512,256]{1,0:T(8,128)(2,1)}, u32[]{:S(2)}, u32[]{:S(2)}) collective-permute-start(bf16[512,256]{1,0:T(8,128)(2,1)S(1)} %broadcast_select_fusion.2), channel_id=1, source_target_pairs={{0,1},{1,0},{2,3},{3,2},{4,5},{5,4},{6,7},{7,6},{8,9},{9,8},{10,11... | collective-permute-start | bytes 786440 | tf_op jit(solution)/shard_map/ppermute | solution.py:20
  35.9 0.7 %copy-start.4 = (bf16[512,256]{1,0:T(8,128)(2,1)}, bf16[512,256]{1,0:T(8,128)(2,1)S(1)}, u32[]{:S(2)}) copy-start(bf16[512,256]{1,0:T(8,128)(2,1)S(1)} %collective-permute-done.3.refs_6_) | copy-start | bytes 786436
  36.6 13.3 %collective-permute-start.4 = (bf16[512,256]{1,0:T(8,128)(2,1)}, bf16[512,256]{1,0:T(8,128)(2,1)}, u32[]{:S(2)}, u32[]{:S(2)}) collective-permute-start(bf16[512,256]{1,0:T(8,128)(2,1)} %broadcast_select_fusion.3), channel_id=1, source_target_pairs={{0,1},{1,0},{2,3},{3,2},{4,5},{5,4},{6,7},{7,6},{8,9},{9,8},{10,11... | collective-permute-start | bytes 786440 | tf_op jit(solution)/shard_map/ppermute | solution.py:20
  39.0 14.7 %collective-permute-start.14 = (bf16[512,256]{1,0:T(8,128)(2,1)}, bf16[512,256]{1,0:T(8,128)(2,1)}, u32[]{:S(2)}, u32[]{:S(2)}) collective-permute-start(bf16[512,256]{1,0:T(8,128)(2,1)} %collective-permute-done.13.refs_5_), channel_id=1, source_target_pairs={{0,6},{1,7},{2,0},{3,1},{4,2},{5,3},{6,4},{7,5},{8,14},{9,15},{10,... | collective-permute-start | bytes 786440 | tf_op jit(solution)/shard_map/ppermute | solution.py:20
  44.6 14.0 %collective-permute-start.11 = (bf16[512,256]{1,0:T(8,128)(2,1)}, bf16[512,256]{1,0:T(8,128)(2,1)}, u32[]{:S(2)}, u32[]{:S(2)}) collective-permute-start(bf16[512,256]{1,0:T(8,128)(2,1)} %collective-permute-done.10.refs_5_), channel_id=1, source_target_pairs={{0,6},{1,7},{2,0},{3,1},{4,2},{5,3},{6,4},{7,5},{8,14},{9,15},{10,... | collective-permute-start | bytes 786440 | tf_op jit(solution)/shard_map/ppermute | solution.py:20
  49.9 12.3 %collective-permute-start.8 = (bf16[512,256]{1,0:T(8,128)(2,1)}, bf16[512,256]{1,0:T(8,128)(2,1)S(1)}, u32[]{:S(2)}, u32[]{:S(2)}) collective-permute-start(bf16[512,256]{1,0:T(8,128)(2,1)} %collective-permute-done.7.refs_5_), channel_id=1, source_target_pairs={{0,6},{1,7},{2,0},{3,1},{4,2},{5,3},{6,4},{7,5},{8,14},{9,15},{10,... | collective-permute-start | bytes 786440 | tf_op jit(solution)/shard_map/ppermute | solution.py:20
  53.7 4.9 %copy-start.3 = (bf16[512,256]{1,0:T(8,128)(2,1)S(1)}, bf16[512,256]{1,0:T(8,128)(2,1)}, u32[]{:S(2)}) copy-start(bf16[512,256]{1,0:T(8,128)(2,1)} %get-tuple-element.11.refs_4_) | copy-start | bytes 786436
  53.7 11.9 %collective-permute-start.5 = (bf16[512,256]{1,0:T(8,128)(2,1)}, bf16[512,256]{1,0:T(8,128)(2,1)S(1)}, u32[]{:S(2)}, u32[]{:S(2)}) collective-permute-start(bf16[512,256]{1,0:T(8,128)(2,1)} %collective-permute-done.4.refs_5_), channel_id=1, source_target_pairs={{0,6},{1,7},{2,0},{3,1},{4,2},{5,3},{6,4},{7,5},{8,14},{9,15},{10,... | collective-permute-start | bytes 786440 | tf_op jit(solution)/shard_map/ppermute | solution.py:20
  54.2 1.0 %copy-start.6 = (bf16[512,256]{1,0:T(8,128)(2,1)S(1)}, bf16[512,256]{1,0:T(8,128)(2,1)}, u32[]{:S(2)}) copy-start(bf16[512,256]{1,0:T(8,128)(2,1)} %get-tuple-element.12.refs_4_) | copy-start | bytes 786436
  58.6 3.5 %copy-start.2 = (bf16[512,256]{1,0:T(8,128)(2,1)S(1)}, bf16[512,256]{1,0:T(8,128)(2,1)}, u32[]{:S(2)}) copy-start(bf16[512,256]{1,0:T(8,128)(2,1)} %get-tuple-element.10.refs_4_) | copy-start | bytes 786436
  62.2 3.5 %copy-start.5 = (bf16[512,256]{1,0:T(8,128)(2,1)S(1)}, bf16[512,256]{1,0:T(8,128)(2,1)}, u32[]{:S(2)}) copy-start(bf16[512,256]{1,0:T(8,128)(2,1)} %copy-done.4) | copy-start | bytes 786436

commit v2 on v0

v2 whole, which is shorter than its diff:
```python
import functools

import jax
import jax.numpy as jnp
from jax import lax
from jax.experimental import pallas as pl
from jax.experimental.pallas import tpu as pltpu
from jax.sharding import PartitionSpec as P

BS = 256
STEPS = 4
PIECES = 4

ANY = pl.ANY
HBM = pltpu.MemorySpace.HBM
VMEM = pltpu.MemorySpace.VMEM


def pinned(value, space=VMEM):
    return pltpu.with_memory_space_constraint(value, space)


def kernel_call(kernel, name, out_shape, operands, spaces, out_space, scratch=(), aliases=None, flops=0):
    moved = 2 * sum(value.size for value in operands)
    return pl.pallas_call(
        kernel,
        out_shape=out_shape,
        in_specs=[pl.BlockSpec(memory_space=space) for space in spaces],
        out_specs=jax.tree.map(lambda _: pl.BlockSpec(memory_space=out_space), out_shape),
        scratch_shapes=list(scratch),
        input_output_aliases=aliases or {},
        cost_estimate=pl.CostEstimate(flops=flops, bytes_accessed=moved, transcendentals=0),
        compiler_params=pltpu.CompilerParams(vmem_limit_bytes=8 << 20),
        name=name,
    )(*operands)


def mask_tile_kernel(first, all_flags, tile, *refs):
    *outs, flags, flag_sem, sem = refs
    width = outs[0].shape[1]
    flag_copy = pltpu.make_async_copy(all_flags, flags, flag_sem)
    flag_copy.start()
    copies = [
        pltpu.make_async_copy(tile.at[:, (first + n) * width : (first + n + 1) * width], out, sem.at[n])
        for n, out in enumerate(outs)
    ]
    for copy in copies:
        copy.start()
    flag_copy.wait()
    for n, (copy, out) in enumerate(zip(copies, outs)):
        copy.wait()
        for row in range(0, out.shape[0], BS):
            for column in range(0, width, BS):

                @pl.when(flags[row // BS, ((first + n) * width + column) // BS] == 0)
                def _():
                    out[row : row + BS, column : column + BS] = jnp.zeros((BS, BS), out.dtype)


def mask_tile(tile, flags, first, count):
    shape = (tile.shape[0], tile.shape[1] // PIECES)
    return kernel_call(
        functools.partial(mask_tile_kernel, first),
        "mask_tile",
        [VMEM(shape, tile.dtype)] * count,
        [pinned(flags, HBM), pinned(tile, HBM)],
        [HBM, HBM],
        VMEM,
        [pltpu.SMEM(flags.shape, flags.dtype), pltpu.SemaphoreType.DMA, pltpu.SemaphoreType.DMA((count,))],
    )


def mask_rows_kernel(all_flags, rows, out, flags, flag_sem, sem):
    flag_copy = pltpu.make_async_copy(all_flags, flags, flag_sem)
    copy = pltpu.make_async_copy(rows, out, sem)
    flag_copy.start()
    copy.start()
    flag_copy.wait()
    copy.wait()
    block_row = lax.axis_index("row") * rows.shape[0] // BS
    for column in range(out.shape[1] // BS):

        @pl.when(flags[block_row, column] == 0)
        def _():
            out[:, column * BS : (column + 1) * BS] = jnp.zeros((out.shape[0], BS), out.dtype)


def mask_rows(rows, flags):
    return kernel_call(
        mask_rows_kernel,
        "mask_rows",
        VMEM(rows.shape, rows.dtype),
        [pinned(flags, HBM), pinned(rows, HBM)],
        [HBM, HBM],
        VMEM,
        [pltpu.SMEM(flags.shape, flags.dtype), pltpu.SemaphoreType.DMA, pltpu.SemaphoreType.DMA],
    )


def choose_kernel(on_even, on_odd, out):
    odd = lax.axis_index("col") % 2

    @pl.when(odd == 0)
    def _():
        out[...] = on_even[...]

    @pl.when(odd == 1)
    def _():
        out[...] = on_odd[...]


def choose(on_even, on_odd):
    return kernel_call(
        choose_kernel,
        "choose",
        VMEM(on_even.shape, on_even.dtype),
        [pinned(on_even), pinned(on_odd)],
        [VMEM, VMEM],
        VMEM,
    )


def stack_rows_kernel(offsets, *refs):
    *shards, out, sem = refs
    rows = shards[0].shape[0]
    me, count = lax.axis_index("row"), len(shards)
    copies = []
    for n, (shard, (distance, flip)) in enumerate(zip(shards, offsets)):
        place = lax.rem(me + distance, count)
        if flip:
            place = place + 1 - 2 * lax.rem(place, 2)
        start = pl.multiple_of(place * rows, rows)
        copies.append(pltpu.make_async_copy(shard, out.at[pl.ds(start, rows), :], sem.at[n]))
    for copy in copies:
        copy.start()
    for copy in copies:
        copy.wait()


def stack_rows(shards, offsets):
    rows, depth = shards[0].shape
    return kernel_call(
        functools.partial(stack_rows_kernel, offsets),
        "stack_rows",
        VMEM((rows * len(shards), depth), shards[0].dtype),
        shards,
        [ANY] * len(shards),
        VMEM,
        [pltpu.SemaphoreType.DMA((len(shards),))],
    )


def product_kernel(plan, left, *refs):
    steps, rights, has_partial, has_product, column = plan
    tiles, rest = refs[:rights], list(refs[rights:])
    partial = rest.pop(0) if has_partial else None
    if has_product:
        rest.pop(0)
    out = rest.pop(0)
    final = len(rest) > 0
    depth, width = tiles[0].shape
    odd = lax.axis_index("col") % 2

    forked = [
        (at, place)
        for at, (_, even, odds) in enumerate(steps)
        for place in range(len(even))
        if even[place] != odds[place]
    ]
    sources = {}
    if forked:
        chosen, fork_sem = rest[2], rest[3]
        for slot, (at, place) in enumerate(forked):
            sources[at, place] = chosen.at[slot]
            for parity in range(2):

                @pl.when(odd == parity)
                def _():
                    source = tiles[steps[at][1 + parity][place]]
                    pltpu.make_async_copy(source, chosen.at[slot], fork_sem.at[slot]).start()

        for slot in range(len(forked)):
            pltpu.make_async_copy(chosen.at[slot], chosen.at[slot], fork_sem.at[slot]).wait()

    places = len(steps[0][1])
    chunk = min(BS, left.shape[0])

    def out_copy(index):
        rows = pl.ds(pl.multiple_of(index * chunk, chunk), chunk)
        return pltpu.make_async_copy(
            rest[0].at[index], out.at[rows, column : column + places * width], rest[1].at[index]
        )

    @pl.loop(0, left.shape[0] // chunk)
    def _(index):
        rows = pl.ds(pl.multiple_of(index * chunk, chunk), chunk)
        for place in range(places):
            columns = slice(place * width, (place + 1) * width)
            total = None
            for at, (step, even, _) in enumerate(steps):
                right = sources.get((at, place), tiles[even[place]])
                term = jnp.dot(
                    left[rows, step * depth : (step + 1) * depth],
                    right[...],
                    preferred_element_type=jnp.float32,
                )
                total = term if total is None else total + term
            if has_partial:
                total = total + partial[rows, columns]
            if final:
                rest[0][index, :, columns] = total.astype(out.dtype)
            else:
                out[rows, columns] = total
        if final:
            out_copy(index).start()

    if final:

        @pl.loop(0, left.shape[0] // chunk)
        def _(index):
            out_copy(index).wait()


def add_products(left, steps, column=0, width=None, partial=None, product=None):
    tiles, numbered, forked = [], [], 0
    for step, *sides in steps:
        entry = [step]
        for pieces in sides:
            for piece in pieces:
                if not any(tile is piece for tile in tiles):
                    tiles.append(piece)
            entry.append(tuple(next(n for n, tile in enumerate(tiles) if tile is piece) for piece in pieces))
        numbered.append(tuple(entry))
        forked += sum(a != b for a, b in zip(entry[1], entry[2]))
    rows, depth, piece_width = left.shape[0], tiles[0].shape[0], tiles[0].shape[1]
    columns = piece_width * len(steps[0][1])
    final = width is not None
    operands = [pinned(x) for x in (left, *tiles, *([] if partial is None else [partial]))]
    spaces = [VMEM] * len(operands)
    aliases = {}
    if product is not None:
        aliases = {len(operands): 0}
        operands.append(product)
        spaces.append(HBM)
    scratch = []
    if final:
        out_shape = jax.ShapeDtypeStruct((rows, width), left.dtype)
        chunk = min(BS, rows)
        scratch += [
            pltpu.VMEM((rows // chunk, chunk, columns), left.dtype),
            pltpu.SemaphoreType.DMA((rows // chunk,)),
        ]
    else:
        out_shape = VMEM((rows, columns), jnp.float32)
    if forked:
        scratch += [pltpu.VMEM((forked, depth, piece_width), left.dtype), pltpu.SemaphoreType.DMA((forked,))]
    plan = (tuple(numbered), len(tiles), partial is not None, product is not None, column)
    return kernel_call(
        functools.partial(product_kernel, plan),
        "add_products",
        out_shape,
        operands,
        spaces,
        HBM if final else VMEM,
        scratch,
        aliases,
        flops=2 * rows * len(steps) * depth * columns,
    )


def moved(block, axis, target):
    count = lax.axis_size(axis)
    return lax.ppermute(block, axis, [(i, target(i) % count) for i in range(count)])


def tied(value, *entries):
    value, *others = lax.optimization_barrier((value, *[entry[0] for entry in entries]))
    for entry, other in zip(entries, others):
        entry[0] = other
    return value


def by_two(block):
    return [moved(block, "col", lambda i: i - 2)]


def across(block):
    return [moved(block, "col", lambda i: i ^ 1)]


def shards(a_window, b_tiles, mask_a, mask_b):
    width = b_tiles.shape[1]
    count = lax.axis_size("row")

    def flip(entry, *held):
        return [moved(tied(entry[0], *held), "row", lambda i: i ^ 1)]

    (own_b,) = mask_tile(b_tiles, mask_b, 0, 1)
    z_b = by_two(own_b)
    d_b = across(own_b)
    own_c, own_1, own_2 = mask_tile(tied(b_tiles, [own_b]), mask_b, 1, 3)
    z_c = by_two(own_c)
    mine = [mask_rows(tied(a_window, [own_c]), mask_a)]

    step = (z_b, d_b)
    s_b = across(tied(z_b[0], *step))
    z_1 = by_two(tied(own_1, *step))
    lefts, offsets, held = [mine], [(0, False)], step
    for distance in range(2, count, 2):
        lefts.append([moved(tied(mine[0], *held), "row", lambda i: i - distance)])
        offsets.append((distance, False))
        held = lefts[-1:]

    step = (z_c, s_b)
    s_c = across(tied(z_c[0], *step))
    z_2 = by_two(tied(own_2, *step))
    near = [flip(mine, *step)]

    step = (z_1, s_c)
    y_1 = across(choose(tied(z_1[0], *step), own_1))
    x_bc = by_two(choose(tied(z_c[0], *step), s_b[0]))

    step = (z_2, y_1)
    y_2 = across(choose(tied(z_2[0], *step), own_2))
    w_1 = by_two(tied(y_1[0], *step))

    step = (x_bc, y_2)
    w_2 = by_two(tied(y_2[0], *step))
    q_c = across(choose(tied(x_bc[0], *step), own_c))
    for left in lefts[1:]:
        near.append(flip(left, *step, *near[-1:]))
    lefts += near
    offsets += [(distance, True) for distance, _ in offsets]
    left = stack_rows([entry[0] for entry in lefts], tuple(offsets))

    partial = add_products(
        left,
        [
            (0, [own_2], [own_2]),
            (1, [y_2[0]], [y_2[0]]),
            (2, [z_2[0]], [z_2[0]]),
        ],
    )
    product = add_products(
        left,
        [
            (0, [own_b, own_c, own_1], [own_b, own_c, own_1]),
            (1, [d_b[0], q_c[0], y_1[0]], [s_b[0], s_c[0], y_1[0]]),
            (2, [z_b[0], z_c[0], z_1[0]], [z_b[0], z_c[0], z_1[0]]),
            (3, [s_b[0], s_c[0], w_1[0]], [x_bc[0], q_c[0], w_1[0]]),
        ],
        width=width,
    )
    return add_products(
        left,
        [(3, [w_2[0]], [w_2[0]])],
        column=3 * (width // PIECES),
        width=width,
        partial=partial,
        product=product,
    )


def solution(mesh):
    return jax.shard_map(
        shards,
        mesh=mesh,
        in_specs=(P(("col", "row"), None), P("col", "row"), P("col", None), P("col", "row")),
        out_specs=P("col", "row"),
        check_vma=False,
    )
```

time: 109 us -> 63.9 us (0.59)
  matrix products: 22.3 us -> 0 us
  local copies, waits for them, and re-layouts: 22 us -> 0 us
  between operations: 13.3 us -> 0.11 us
  Pallas kernels: 0 us -> 11.8 us
  starting transfers between devices: 16.6 us -> 24.2 us
  waiting for transfers between devices: 33.6 us -> 27.6 us
  other arithmetic: 1.39 us -> 0 us
    dot_general x4 -> x0, matrix products: 22.3 us -> none  [dense_dot(): return jnp.dot(left, right, preferred_element_type=jnp.float32)]
    pallas_call x0 -> x11, Pallas kernels: none -> 11.8 us  [kernel_call(): pl.pallas_call(kernel, out_shape=out_shape, in_specs=[pl.BlockSpec(memory...]
    gather x4 -> x0, local copies, waits for them, and re-layouts: 11.2 us -> none  [row_flags(): return jnp.take(flags, rows, axis=0)]
    ppermute x3 -> x16, starting transfers between devices: 16.5 us -> 24.2 us  [moved(): lax.ppermute(block, axis, [(i, target(i) % count) for i in range(count)])]
    broadcast_in_dim x4 -> x0, local copies, waits for them, and re-layouts: 4.99 us -> none  [tile_product(): a_live = a_tile * jnp.repeat(a_flags, BS, axis=1).astype(jnp.bfloat16)]
    ppermute x3 -> x16, waiting for transfers between devices: 32.2 us -> 27.6 us  [moved(): lax.ppermute(block, axis, [(i, target(i) % count) for i in range(count)])]
    unnamed x13 -> x0, local copies, waits for them, and re-layouts: 3.11 us -> none
    slice x2 -> x0, local copies, waits for them, and re-layouts: 2.37 us -> none  [the longest x1 2.29 us: shards(): a_window[:, step * k_width:(step + 1) * k_width]]
  transfers between devices with their start and end apart: 7 -> 16, of which waited for: 3 -> 9; matrix products, arithmetic and copies ran while one was open for 32% -> 0% of each run, Pallas kernels for 0% -> 14%
where the time goes in v2:
time: 63.9 us; the launch traced here: 63.7 us
  waiting for transfers between devices  27.6 us (43%)
  starting transfers between devices  24.2 us (38%)
  Pallas kernels  11.8 us (18%)
    ppermute x16, waiting for transfers between devices, moved(): lax.ppermute(block, axis, [(i, target(i) % count) for i in range(count)])  27.6 us
    ppermute x16, starting transfers between devices, moved(): lax.ppermute(block, axis, [(i, target(i) % count) for i in range(count)])  24.2 us
    pallas_call x11, Pallas kernels, kernel_call(): pl.pallas_call(kernel, out_shape=out_shape, in_specs=[pl.BlockSpec(memory...  11.8 us
  transfers between devices with their start and end apart: 16, of which 9 were waited for; matrix products, arithmetic and copies ran while one was open for 0% of the time, Pallas kernels for 14%

profile of v2, /device:TPU:0, one launch (start us, length us, event | category | flops | bytes accessed | tf_op | source)
XLA Modules:
  0.0 63.7 jit_solution(14567284519393181076)
XLA Ops:
  0.0 1.0 %mask_tile.2.refs_0_ = bf16[512,256]{1,0:T(8,128)(2,1)S(1)} custom-call(s32[2,4]{1,0:T(2,128)} %all_flags.4, bf16[512,1024]{1,0:T(8,128)(2,1)} %tile.2), custom_call_target="tpu_custom_call" | custom-call | bytes 1048592 | tf_op jit(solution)/shard_map/mask_tile/pallas_call | solution.py:25
  1.0 5.1 %collective-permute-start = (bf16[512,256]{1,0:T(8,128)(2,1)S(1)}, bf16[512,256]{1,0:T(8,128)(2,1)S(1)}, u32[]{:S(2)}, u32[]{:S(2)}) collective-permute-start(bf16[512,256]{1,0:T(8,128)(2,1)S(1)} %mask_tile.2.refs_0_), channel_id=1, source_target_pairs={{0,6},{1,7},{2,0},{3,1},{4,2},{5,3},{6,4},{7,5},{8,14},{9,15},{10,... | collective-permute-start | bytes 786440 | tf_op jit(solution)/shard_map/ppermute | solution.py:273
  6.1 1.5 %collective-permute-start.1 = (bf16[512,256]{1,0:T(8,128)(2,1)S(1)}, bf16[512,256]{1,0:T(8,128)(2,1)S(1)}, u32[]{:S(2)}, u32[]{:S(2)}) collective-permute-start(bf16[512,256]{1,0:T(8,128)(2,1)S(1)} %mask_tile.2.refs_0_), channel_id=1, source_target_pairs={{0,1},{1,0},{2,3},{3,2},{4,5},{5,4},{6,7},{7,6},{8,9},{9,8},{10,11... | collective-permute-start | bytes 786440 | tf_op jit(solution)/shard_map/ppermute | solution.py:273
  7.6 1.2 %mask_tile.3 = (bf16[512,256]{1,0:T(8,128)(2,1)S(1)}, bf16[512,256]{1,0:T(8,128)(2,1)S(1)}, bf16[512,256]{1,0:T(8,128)(2,1)S(1)}) custom-call(s32[2,4]{1,0:T(2,128)} %all_flags.4, bf16[512,1024]{1,0:T(8,128)(2,1)} %tile.2), custom_call_target="tpu_custom_call" | custom-call | bytes 1048592 | tf_op jit(solution)/shard_map/mask_tile/pallas_call | solution.py:25
  8.8 0.5 collective-permute-start.3
  9.3 3.5 %collective-permute-done.refs_8_ = bf16[512,256]{1,0:T(8,128)(2,1)S(1)} collective-permute-done((bf16[512,256]{1,0:T(8,128)(2,1)S(1)}, bf16[512,256]{1,0:T(8,128)(2,1)S(1)}, u32[]{:S(2)}, u32[]{:S(2)}) %collective-permute-start) | collective-permute-done | bytes 262176 | tf_op jit(solution)/shard_map/ppermute | solution.py:273
  12.8 1.1 %collective-permute-done.1.refs_3_ = bf16[512,256]{1,0:T(8,128)(2,1)S(1)} collective-permute-done((bf16[512,256]{1,0:T(8,128)(2,1)S(1)}, bf16[512,256]{1,0:T(8,128)(2,1)S(1)}, u32[]{:S(2)}, u32[]{:S(2)}) %collective-permute-start.1) | collective-permute-done | bytes 262176 | tf_op jit(solution)/shard_map/ppermute | solution.py:273
  13.8 1.5 %collective-permute-start.4 = (bf16[512,256]{1,0:T(8,128)(2,1)S(1)}, bf16[512,256]{1,0:T(8,128)(2,1)S(1)}, u32[]{:S(2)}, u32[]{:S(2)}) collective-permute-start(bf16[512,256]{1,0:T(8,128)(2,1)S(1)} %collective-permute-done.refs_8_), channel_id=1, source_target_pairs={{0,1},{1,0},{2,3},{3,2},{4,5},{5,4},{6,7},{7,6},{8,9},{9,8},{10,11... | collective-permute-start | bytes 786440 | tf_op jit(solution)/shard_map/ppermute | solution.py:273
  15.4 1.3 %mask_rows.1.refs_0_ = bf16[256,2048]{1,0:T(8,128)(2,1)S(1)} custom-call(s32[4,8]{1,0:T(4,128)} %all_flags.5, bf16[256,2048]{1,0:T(8,128)(2,1)} %rows), custom_call_target="tpu_custom_call" | custom-call | bytes 1048640 | tf_op jit(solution)/shard_map/mask_rows/pallas_call | solution.py:25
  16.7 1.6 %collective-permute-start.2 = (bf16[256,2048]{1,0:T(8,128)(2,1)S(1)}, bf16[256,2048]{1,0:T(8,128)(2,1)S(1)}, u32[]{:S(2)}, u32[]{:S(2)}) collective-permute-start(bf16[256,2048]{1,0:T(8,128)(2,1)S(1)} %mask_rows.1.refs_0_), channel_id=1, source_target_pairs={{0,16},{8,24},{16,0},{24,8},{1,17},{9,25},{17,1},{25,9},{2,18},{10... | collective-permute-start | bytes 3145736 | tf_op jit(solution)/shard_map/ppermute | solution.py:273
  18.3 0.0 collective-permute-done.3.on_even.refs_9_
  18.3 2.4 %collective-permute-done.4.on_odd.refs_6_ = bf16[512,256]{1,0:T(8,128)(2,1)S(1)} collective-permute-done((bf16[512,256]{1,0:T(8,128)(2,1)S(1)}, bf16[512,256]{1,0:T(8,128)(2,1)S(1)}, u32[]{:S(2)}, u32[]{:S(2)}) %collective-permute-start.4) | collective-permute-done | bytes 262176 | tf_op jit(solution)/shard_map/ppermute | solution.py:273
  20.7 0.0 collective-permute-start.11
  20.7 2.7 %collective-permute-start.6 = (bf16[512,256]{1,0:T(8,128)(2,1)S(1)}, bf16[512,256]{1,0:T(8,128)(2,1)S(1)}, u32[]{:S(2)}, u32[]{:S(2)}) collective-permute-start(bf16[512,256]{1,0:T(8,128)(2,1)S(1)} %get-tuple-element.64.on_odd.refs_2_), channel_id=1, source_target_pairs={{0,6},{1,7},{2,0},{3,1},{4,2},{5,3},{6,4},{7,5},{8,14},{9,15},{10,... | collective-permute-start | bytes 786440 | tf_op jit(solution)/shard_map/ppermute | solution.py:273
  23.4 1.5 %collective-permute-start.7 = (bf16[512,256]{1,0:T(8,128)(2,1)S(1)}, bf16[512,256]{1,0:T(8,128)(2,1)S(1)}, u32[]{:S(2)}, u32[]{:S(2)}) collective-permute-start(bf16[512,256]{1,0:T(8,128)(2,1)S(1)} %collective-permute-done.3.on_even.refs_9_), channel_id=1, source_target_pairs={{0,1},{1,0},{2,3},{3,2},{4,5},{5,4},{6,7},{7,6},{8,9},{9,8},{10,11... | collective-permute-start | bytes 786440 | tf_op jit(solution)/shard_map/ppermute | solution.py:273
  25.0 0.0 collective-permute-start.5
  25.0 5.1 %collective-permute-done.6.on_even.refs_10_ = bf16[512,256]{1,0:T(8,128)(2,1)S(1)} collective-permute-done((bf16[512,256]{1,0:T(8,128)(2,1)S(1)}, bf16[512,256]{1,0:T(8,128)(2,1)S(1)}, u32[]{:S(2)}, u32[]{:S(2)}) %collective-permute-start.6) | collective-permute-done | bytes 262176 | tf_op jit(solution)/shard_map/ppermute | solution.py:273
  30.1 1.8 %collective-permute-done.7.refs_7_ = bf16[512,256]{1,0:T(8,128)(2,1)S(1)} collective-permute-done((bf16[512,256]{1,0:T(8,128)(2,1)S(1)}, bf16[512,256]{1,0:T(8,128)(2,1)S(1)}, u32[]{:S(2)}, u32[]{:S(2)}) %collective-permute-start.7) | collective-permute-done | bytes 262176 | tf_op jit(solution)/shard_map/ppermute | solution.py:273
  31.9 1.6 %collective-permute-start.8 = (bf16[512,256]{1,0:T(8,128)(2,1)S(1)}, bf16[512,256]{1,0:T(8,128)(2,1)S(1)}, u32[]{:S(2)}, u32[]{:S(2)}) collective-permute-start(bf16[512,256]{1,0:T(8,128)(2,1)S(1)} %choose.4), channel_id=1, source_target_pairs={{0,1},{1,0},{2,3},{3,2},{4,5},{5,4},{6,7},{7,6},{8,9},{9,8},{10,11... | collective-permute-start | bytes 786440 | tf_op jit(solution)/shard_map/ppermute | solution.py:273
  33.5 2.5 %collective-permute-start.10 = (bf16[512,256]{1,0:T(8,128)(2,1)S(1)}, bf16[512,256]{1,0:T(8,128)(2,1)S(1)}, u32[]{:S(2)}, u32[]{:S(2)}) collective-permute-start(bf16[512,256]{1,0:T(8,128)(2,1)S(1)} %choose.6), channel_id=1, source_target_pairs={{0,6},{1,7},{2,0},{3,1},{4,2},{5,3},{6,4},{7,5},{8,14},{9,15},{10,... | collective-permute-start | bytes 786440 | tf_op jit(solution)/shard_map/ppermute | solution.py:273
  36.0 0.0 collective-permute-done.5.on_even.refs_2_
  36.1 3.5 %collective-permute-done.8.refs_5_ = bf16[512,256]{1,0:T(8,128)(2,1)S(1)} collective-permute-done((bf16[512,256]{1,0:T(8,128)(2,1)S(1)}, bf16[512,256]{1,0:T(8,128)(2,1)S(1)}, u32[]{:S(2)}, u32[]{:S(2)}) %collective-permute-start.8) | collective-permute-done | bytes 262176 | tf_op jit(solution)/shard_map/ppermute | solution.py:273
  39.6 1.6 %collective-permute-start.9 = (bf16[512,256]{1,0:T(8,128)(2,1)S(1)}, bf16[512,256]{1,0:T(8,128)(2,1)S(1)}, u32[]{:S(2)}, u32[]{:S(2)}) collective-permute-start(bf16[512,256]{1,0:T(8,128)(2,1)S(1)} %choose.5), channel_id=1, source_target_pairs={{0,1},{1,0},{2,3},{3,2},{4,5},{5,4},{6,7},{7,6},{8,9},{9,8},{10,11... | collective-permute-start | bytes 786440 | tf_op jit(solution)/shard_map/ppermute | solution.py:273
  41.2 0.0 collective-permute-done.10.on_even.refs_12_
  41.2 5.2 %collective-permute-done.9.refs_1_ = bf16[512,256]{1,0:T(8,128)(2,1)S(1)} collective-permute-done((bf16[512,256]{1,0:T(8,128)(2,1)S(1)}, bf16[512,256]{1,0:T(8,128)(2,1)S(1)}, u32[]{:S(2)}, u32[]{:S(2)}) %collective-permute-start.9) | collective-permute-done | bytes 262176 | tf_op jit(solution)/shard_map/ppermute | solution.py:273
  46.4 0.0 collective-permute-done.2.refs_1_
  46.4 0.0 collective-permute-done.11.refs_2_
  46.4 0.0 collective-permute-start.12
  46.4 2.4 %collective-permute-start.15 = (bf16[512,256]{1,0:T(8,128)(2,1)S(1)}, bf16[512,256]{1,0:T(8,128)(2,1)S(1)}, u32[]{:S(2)}, u32[]{:S(2)}) collective-permute-start(bf16[512,256]{1,0:T(8,128)(2,1)S(1)} %collective-permute-done.8.refs_5_), channel_id=1, source_target_pairs={{0,6},{1,7},{2,0},{3,1},{4,2},{5,3},{6,4},{7,5},{8,14},{9,15},{10,... | collective-permute-start | bytes 786440 | tf_op jit(solution)/shard_map/ppermute | solution.py:273
  48.8 1.6 %collective-permute-start.14 = (bf16[512,256]{1,0:T(8,128)(2,1)S(1)}, bf16[512,256]{1,0:T(8,128)(2,1)S(1)}, u32[]{:S(2)}, u32[]{:S(2)}) collective-permute-start(bf16[512,256]{1,0:T(8,128)(2,1)S(1)} %choose.7), channel_id=1, source_target_pairs={{0,1},{1,0},{2,3},{3,2},{4,5},{5,4},{6,7},{7,6},{8,9},{9,8},{10,11... | collective-permute-start | bytes 786440 | tf_op jit(solution)/shard_map/ppermute | solution.py:273
  50.4 0.0 collective-permute-start.13
  50.4 0.0 collective-permute-done.12.refs_3_
  50.4 0.3 stack_rows.1.left
  50.8 1.5 %add_products.3.refs_1_ = f32[1024,256]{1,0:T(8,128)S(1)} custom-call(bf16[1024,2048]{1,0:T(8,128)(2,1)S(1)} %stack_rows.1.left, bf16[512,256]{1,0:T(8,128)(2,1)S(1)} %get-tuple-element.63.on_odd.refs_0_, bf16[512,256]{1,0:T(8,128)(2,1)S(1)} %collective-permute-done.9.refs_1_, bf16[512,256]{1,0:T(8,128)(2,1)S(1)} %collective-permute-done.5.on_even.refs_2_), custom_call_target="tpu_custom_call" | custom-call | flops 805306368 | bytes 4980736 | tf_op jit(solution)/shard_map/add_products/pallas_call | solution.py:25
  52.3 3.3 %collective-permute-done.15.refs_11_ = bf16[512,256]{1,0:T(8,128)(2,1)S(1)} collective-permute-done((bf16[512,256]{1,0:T(8,128)(2,1)S(1)}, bf16[512,256]{1,0:T(8,128)(2,1)S(1)}, u32[]{:S(2)}, u32[]{:S(2)}) %collective-permute-start.15) | collective-permute-done | bytes 262176 | tf_op jit(solution)/shard_map/ppermute | solution.py:273
  55.6 1.7 %collective-permute-done.14.refs_4_ = bf16[512,256]{1,0:T(8,128)(2,1)S(1)} collective-permute-done((bf16[512,256]{1,0:T(8,128)(2,1)S(1)}, bf16[512,256]{1,0:T(8,128)(2,1)S(1)}, u32[]{:S(2)}, u32[]{:S(2)}) %collective-permute-start.14) | collective-permute-done | bytes 262176 | tf_op jit(solution)/shard_map/ppermute | solution.py:273
  57.3 4.8 %add_products.4.refs_2_ = bf16[1024,1024]{1,0:T(8,128)(2,1)} custom-call(bf16[1024,2048]{1,0:T(8,128)(2,1)S(1)} %stack_rows.1.left, bf16[512,256]{1,0:T(8,128)(2,1)S(1)} %mask_tile.2.refs_0_, bf16[512,256]{1,0:T(8,128)(2,1)S(1)} %get-tuple-element.51.on_odd.refs_1_, bf16[512,256]{1,0:T(8,128)(2,1)S(1)} %get-tuple-element.64.on_odd.refs_2_, ...), custom_call_target="tpu_custom_call" | custom-call | flops 3221225472 | bytes 7602176 | tf_op jit(solution)/shard_map/add_products/pallas_call | solution.py:25
  62.1 0.0 collective-permute-done.13.refs_0_
  62.1 1.6 %add_products.5 = bf16[1024,1024]{1,0:T(8,128)(2,1)} custom-call(bf16[1024,2048]{1,0:T(8,128)(2,1)S(1)} %stack_rows.1.left, bf16[512,256]{1,0:T(8,128)(2,1)S(1)} %collective-permute-done.13.refs_0_, f32[1024,256]{1,0:T(8,128)S(1)} %add_products.3.refs_1_, bf16[1024,1024]{1,0:T(8,128)(2,1)} %add_products.4.refs_2_), custom_call_target="tpu_custom_call", output_to_operand_aliasing={{}: (3, {})} | custom-call | flops 268435456 | bytes 7077888 | tf_op jit(solution)/shard_map/add_products/pallas_call | solution.py:25
  (4 shorter events, 0.1 us)
Async XLA Ops:
  1.0 11.8 %collective-permute-start = (bf16[512,256]{1,0:T(8,128)(2,1)S(1)}, bf16[512,256]{1,0:T(8,128)(2,1)S(1)}, u32[]{:S(2)}, u32[]{:S(2)}) collective-permute-start(bf16[512,256]{1,0:T(8,128)(2,1)S(1)} %mask_tile.2.refs_0_), channel_id=1, source_target_pairs={{0,6},{1,7},{2,0},{3,1},{4,2},{5,3},{6,4},{7,5},{8,14},{9,15},{10,... | collective-permute-start | bytes 786440 | tf_op jit(solution)/shard_map/ppermute | solution.py:273
  6.1 7.8 %collective-permute-start.1 = (bf16[512,256]{1,0:T(8,128)(2,1)S(1)}, bf16[512,256]{1,0:T(8,128)(2,1)S(1)}, u32[]{:S(2)}, u32[]{:S(2)}) collective-permute-start(bf16[512,256]{1,0:T(8,128)(2,1)S(1)} %mask_tile.2.refs_0_), channel_id=1, source_target_pairs={{0,1},{1,0},{2,3},{3,2},{4,5},{5,4},{6,7},{7,6},{8,9},{9,8},{10,11... | collective-permute-start | bytes 786440 | tf_op jit(solution)/shard_map/ppermute | solution.py:273
  8.8 9.5 %collective-permute-start.3 = (bf16[512,256]{1,0:T(8,128)(2,1)S(1)}, bf16[512,256]{1,0:T(8,128)(2,1)S(1)}, u32[]{:S(2)}, u32[]{:S(2)}) collective-permute-start(bf16[512,256]{1,0:T(8,128)(2,1)S(1)} %get-tuple-element.51.on_odd.refs_1_), channel_id=1, source_target_pairs={{0,6},{1,7},{2,0},{3,1},{4,2},{5,3},{6,4},{7,5},{8,14},{9,15},{10,... | collective-permute-start | bytes 786440 | tf_op jit(solution)/shard_map/ppermute | solution.py:273
  13.8 6.9 %collective-permute-start.4 = (bf16[512,256]{1,0:T(8,128)(2,1)S(1)}, bf16[512,256]{1,0:T(8,128)(2,1)S(1)}, u32[]{:S(2)}, u32[]{:S(2)}) collective-permute-start(bf16[512,256]{1,0:T(8,128)(2,1)S(1)} %collective-permute-done.refs_8_), channel_id=1, source_target_pairs={{0,1},{1,0},{2,3},{3,2},{4,5},{5,4},{6,7},{7,6},{8,9},{9,8},{10,11... | collective-permute-start | bytes 786440 | tf_op jit(solution)/shard_map/ppermute | solution.py:273
  16.7 29.7 %collective-permute-start.2 = (bf16[256,2048]{1,0:T(8,128)(2,1)S(1)}, bf16[256,2048]{1,0:T(8,128)(2,1)S(1)}, u32[]{:S(2)}, u32[]{:S(2)}) collective-permute-start(bf16[256,2048]{1,0:T(8,128)(2,1)S(1)} %mask_rows.1.refs_0_), channel_id=1, source_target_pairs={{0,16},{8,24},{16,0},{24,8},{1,17},{9,25},{17,1},{25,9},{2,18},{10... | collective-permute-start | bytes 3145736 | tf_op jit(solution)/shard_map/ppermute | solution.py:273
  20.7 25.7 %collective-permute-start.11 = (bf16[256,2048]{1,0:T(8,128)(2,1)S(1)}, bf16[256,2048]{1,0:T(8,128)(2,1)S(1)}, u32[]{:S(2)}, u32[]{:S(2)}) collective-permute-start(bf16[256,2048]{1,0:T(8,128)(2,1)S(1)} %mask_rows.1.refs_0_), channel_id=1, source_target_pairs={{0,8},{8,0},{16,24},{24,16},{1,9},{9,1},{17,25},{25,17},{2,10},{10... | collective-permute-start | bytes 3145736 | tf_op jit(solution)/shard_map/ppermute | solution.py:273
  20.7 9.4 %collective-permute-start.6 = (bf16[512,256]{1,0:T(8,128)(2,1)S(1)}, bf16[512,256]{1,0:T(8,128)(2,1)S(1)}, u32[]{:S(2)}, u32[]{:S(2)}) collective-permute-start(bf16[512,256]{1,0:T(8,128)(2,1)S(1)} %get-tuple-element.64.on_odd.refs_2_), channel_id=1, source_target_pairs={{0,6},{1,7},{2,0},{3,1},{4,2},{5,3},{6,4},{7,5},{8,14},{9,15},{10,... | collective-permute-start | bytes 786440 | tf_op jit(solution)/shard_map/ppermute | solution.py:273
  23.4 8.4 %collective-permute-start.7 = (bf16[512,256]{1,0:T(8,128)(2,1)S(1)}, bf16[512,256]{1,0:T(8,128)(2,1)S(1)}, u32[]{:S(2)}, u32[]{:S(2)}) collective-permute-start(bf16[512,256]{1,0:T(8,128)(2,1)S(1)} %collective-permute-done.3.on_even.refs_9_), channel_id=1, source_target_pairs={{0,1},{1,0},{2,3},{3,2},{4,5},{5,4},{6,7},{7,6},{8,9},{9,8},{10,11... | collective-permute-start | bytes 786440 | tf_op jit(solution)/shard_map/ppermute | solution.py:273
  25.0 11.1 %collective-permute-start.5 = (bf16[512,256]{1,0:T(8,128)(2,1)S(1)}, bf16[512,256]{1,0:T(8,128)(2,1)S(1)}, u32[]{:S(2)}, u32[]{:S(2)}) collective-permute-start(bf16[512,256]{1,0:T(8,128)(2,1)S(1)} %get-tuple-element.63.on_odd.refs_0_), channel_id=1, source_target_pairs={{0,6},{1,7},{2,0},{3,1},{4,2},{5,3},{6,4},{7,5},{8,14},{9,15},{10,... | collective-permute-start | bytes 786440 | tf_op jit(solution)/shard_map/ppermute | solution.py:273
  31.9 7.7 %collective-permute-start.8 = (bf16[512,256]{1,0:T(8,128)(2,1)S(1)}, bf16[512,256]{1,0:T(8,128)(2,1)S(1)}, u32[]{:S(2)}, u32[]{:S(2)}) collective-permute-start(bf16[512,256]{1,0:T(8,128)(2,1)S(1)} %choose.4), channel_id=1, source_target_pairs={{0,1},{1,0},{2,3},{3,2},{4,5},{5,4},{6,7},{7,6},{8,9},{9,8},{10,11... | collective-permute-start | bytes 786440 | tf_op jit(solution)/shard_map/ppermute | solution.py:273
  33.5 7.7 %collective-permute-start.10 = (bf16[512,256]{1,0:T(8,128)(2,1)S(1)}, bf16[512,256]{1,0:T(8,128)(2,1)S(1)}, u32[]{:S(2)}, u32[]{:S(2)}) collective-permute-start(bf16[512,256]{1,0:T(8,128)(2,1)S(1)} %choose.6), channel_id=1, source_target_pairs={{0,6},{1,7},{2,0},{3,1},{4,2},{5,3},{6,4},{7,5},{8,14},{9,15},{10,... | collective-permute-start | bytes 786440 | tf_op jit(solution)/shard_map/ppermute | solution.py:273
  39.6 6.8 %collective-permute-start.9 = (bf16[512,256]{1,0:T(8,128)(2,1)S(1)}, bf16[512,256]{1,0:T(8,128)(2,1)S(1)}, u32[]{:S(2)}, u32[]{:S(2)}) collective-permute-start(bf16[512,256]{1,0:T(8,128)(2,1)S(1)} %choose.5), channel_id=1, source_target_pairs={{0,1},{1,0},{2,3},{3,2},{4,5},{5,4},{6,7},{7,6},{8,9},{9,8},{10,11... | collective-permute-start | bytes 786440 | tf_op jit(solution)/shard_map/ppermute | solution.py:273
  46.4 4.0 %collective-permute-start.12 = (bf16[256,2048]{1,0:T(8,128)(2,1)S(1)}, bf16[256,2048]{1,0:T(8,128)(2,1)S(1)}, u32[]{:S(2)}, u32[]{:S(2)}) collective-permute-start(bf16[256,2048]{1,0:T(8,128)(2,1)S(1)} %collective-permute-done.2.refs_1_), channel_id=1, source_target_pairs={{0,8},{8,0},{16,24},{24,16},{1,9},{9,1},{17,25},{25,17},{2,10},{10... | collective-permute-start | bytes 3145736 | tf_op jit(solution)/shard_map/ppermute | solution.py:273
  46.4 9.2 %collective-permute-start.15 = (bf16[512,256]{1,0:T(8,128)(2,1)S(1)}, bf16[512,256]{1,0:T(8,128)(2,1)S(1)}, u32[]{:S(2)}, u32[]{:S(2)}) collective-permute-start(bf16[512,256]{1,0:T(8,128)(2,1)S(1)} %collective-permute-done.8.refs_5_), channel_id=1, source_target_pairs={{0,6},{1,7},{2,0},{3,1},{4,2},{5,3},{6,4},{7,5},{8,14},{9,15},{10,... | collective-permute-start | bytes 786440 | tf_op jit(solution)/shard_map/ppermute | solution.py:273
  48.8 8.4 %collective-permute-start.14 = (bf16[512,256]{1,0:T(8,128)(2,1)S(1)}, bf16[512,256]{1,0:T(8,128)(2,1)S(1)}, u32[]{:S(2)}, u32[]{:S(2)}) collective-permute-start(bf16[512,256]{1,0:T(8,128)(2,1)S(1)} %choose.7), channel_id=1, source_target_pairs={{0,1},{1,0},{2,3},{3,2},{4,5},{5,4},{6,7},{7,6},{8,9},{9,8},{10,11... | collective-permute-start | bytes 786440 | tf_op jit(solution)/shard_map/ppermute | solution.py:273
  50.4 11.7 %collective-permute-start.13 = (bf16[512,256]{1,0:T(8,128)(2,1)S(1)}, bf16[512,256]{1,0:T(8,128)(2,1)S(1)}, u32[]{:S(2)}, u32[]{:S(2)}) collective-permute-start(bf16[512,256]{1,0:T(8,128)(2,1)S(1)} %collective-permute-done.9.refs_1_), channel_id=1, source_target_pairs={{0,6},{1,7},{2,0},{3,1},{4,2},{5,3},{6,4},{7,5},{8,14},{9,15},{10,... | collective-permute-start | bytes 786440 | tf_op jit(solution)/shard_map/ppermute | solution.py:273

commit v3 on v2

--- a/solution.py
+++ b/solution.py
@@ -151,7 +151,7 @@
 
 
 def product_kernel(plan, left, *refs):
-    steps, rights, has_partial, has_product, column = plan
+    places, rights, has_partial, has_product, column = plan
     tiles, rest = refs[:rights], list(refs[rights:])
     partial = rest.pop(0) if has_partial else None
     if has_product:
@@ -160,53 +160,27 @@
     final = len(rest) > 0
     depth, width = tiles[0].shape
     odd = lax.axis_index("col") % 2
-
-    forked = [
-        (at, place)
-        for at, (_, even, odds) in enumerate(steps)
-        for place in range(len(even))
-        if even[place] != odds[place]
-    ]
-    sources = {}
-    if forked:
-        chosen, fork_sem = rest[2], rest[3]
-        for slot, (at, place) in enumerate(forked):
-            sources[at, place] = chosen.at[slot]
-            for parity in range(2):
-
-                @pl.when(odd == parity)
-                def _():
-                    source = tiles[steps[at][1 + parity][place]]
-                    pltpu.make_async_copy(source, chosen.at[slot], fork_sem.at[slot]).start()
-
-        for slot in range(len(forked)):
-            pltpu.make_async_copy(chosen.at[slot], chosen.at[slot], fork_sem.at[slot]).wait()
-
-    places = len(steps[0][1])
     chunk = min(BS, left.shape[0])
 
     def out_copy(index):
         rows = pl.ds(pl.multiple_of(index * chunk, chunk), chunk)
-        return pltpu.make_async_copy(
-            rest[0].at[index], out.at[rows, column : column + places * width], rest[1].at[index]
-        )
+        columns = slice(column, column + len(places) * width)
+        return pltpu.make_async_copy(rest[0].at[index], out.at[rows, columns], rest[1].at[index])
 
     @pl.loop(0, left.shape[0] // chunk)
     def _(index):
         rows = pl.ds(pl.multiple_of(index * chunk, chunk), chunk)
-        for place in range(places):
+        for place, terms in enumerate(places):
             columns = slice(place * width, (place + 1) * width)
-            total = None
-            for at, (step, even, _) in enumerate(steps):
-                right = sources.get((at, place), tiles[even[place]])
+            total = partial[rows, columns] if has_partial else None
+            for number, on_even, on_odd in terms:
+                start = on_even * depth
+                if on_even != on_odd:
+                    start = pl.multiple_of(start + odd * ((on_odd - on_even) * depth), depth)
                 term = jnp.dot(
-                    left[rows, step * depth : (step + 1) * depth],
-                    right[...],
-                    preferred_element_type=jnp.float32,
+                    left[rows, pl.ds(start, depth)], tiles[number][...], preferred_element_type=jnp.float32
                 )
                 total = term if total is None else total + term
-            if has_partial:
-                total = total + partial[rows, columns]
             if final:
                 rest[0][index, :, columns] = total.astype(out.dtype)
             else:
@@ -221,28 +195,26 @@
             out_copy(index).wait()
 
 
-def add_products(left, steps, column=0, width=None, partial=None, product=None):
-    tiles, numbered, forked = [], [], 0
-    for step, *sides in steps:
-        entry = [step]
-        for pieces in sides:
-            for piece in pieces:
-                if not any(tile is piece for tile in tiles):
-                    tiles.append(piece)
-            entry.append(tuple(next(n for n, tile in enumerate(tiles) if tile is piece) for piece in pieces))
-        numbered.append(tuple(entry))
-        forked += sum(a != b for a, b in zip(entry[1], entry[2]))
-    rows, depth, piece_width = left.shape[0], tiles[0].shape[0], tiles[0].shape[1]
-    columns = piece_width * len(steps[0][1])
+def add_products(left, places, column=0, width=None, partial=None, product=None):
+    tiles = []
+    for terms in places:
+        for tile, _, _ in terms:
+            if not any(tile is known for known in tiles):
+                tiles.append(tile)
+    numbered = tuple(
+        tuple((next(n for n, known in enumerate(tiles) if known is tile), a, b) for tile, a, b in terms)
+        for terms in places
+    )
+    rows, piece_width = left.shape[0], tiles[0].shape[1]
+    columns = piece_width * len(places)
     final = width is not None
     operands = [pinned(x) for x in (left, *tiles, *([] if partial is None else [partial]))]
     spaces = [VMEM] * len(operands)
-    aliases = {}
+    aliases, scratch = {}, []
     if product is not None:
         aliases = {len(operands): 0}
         operands.append(product)
         spaces.append(HBM)
-    scratch = []
     if final:
         out_shape = jax.ShapeDtypeStruct((rows, width), left.dtype)
         chunk = min(BS, rows)
@@ -252,11 +224,8 @@
         ]
     else:
         out_shape = VMEM((rows, columns), jnp.float32)
-    if forked:
-        scratch += [pltpu.VMEM((forked, depth, piece_width), left.dtype), pltpu.SemaphoreType.DMA((forked,))]
-    plan = (tuple(numbered), len(tiles), partial is not None, product is not None, column)
-    return kernel_call(
-        functools.partial(product_kernel, plan),
+    return kernel_call(
+        functools.partial(product_kernel, (numbered, len(tiles), partial is not None, product is not None, column)),
         "add_products",
         out_shape,
         operands,
@@ -264,7 +233,7 @@
         HBM if final else VMEM,
         scratch,
         aliases,
-        flops=2 * rows * len(steps) * depth * columns,
+        flops=2 * rows * tiles[0].shape[0] * piece_width * sum(len(terms) for terms in places),
     )
 
 
@@ -280,84 +249,96 @@
     return value
 
 
-def by_two(block):
-    return [moved(block, "col", lambda i: i - 2)]
-
-
-def across(block):
-    return [moved(block, "col", lambda i: i ^ 1)]
+HELD = {
+    "Z1": ["Db"],
+    "Z2": ["Sb", "Db"],
+    "Af": ["Zb", "Db"],
+    "Y1": ["Sc", "Zb"],
+    "X": ["Zb"],
+    "Y2": ["Zb", "Sb"],
+    "W1": ["Db", "Zc"],
+    "Q": ["X"],
+    "Ar": ["X", "Y2", "W1", "Sb", "Zc"],
+    "partial2": ["Af"],
+    "first": ["W1", "Ar"],
+    "last": ["Sb", "Z2", "Db", "Sc"],
+    "partial": ["Y1", "X"],
+}
 
 
 def shards(a_window, b_tiles, mask_a, mask_b):
     width = b_tiles.shape[1]
     count = lax.axis_size("row")
-
-    def flip(entry, *held):
-        return [moved(tied(entry[0], *held), "row", lambda i: i ^ 1)]
+    got = {}
+
+    def held(name, value):
+        names = HELD.get(name, [])
+        return tied(value, *[got[known] for known in names]) if names else value
+
+    def send(name, block, axis, target, key=None):
+        with jax.named_scope("send_" + name):
+            got[key or name] = [moved(held(name, block), axis, target)]
+        return got[key or name][0]
+
+    def by_two(name, block):
+        return send(name, block, "col", lambda i: i - 2)
+
+    def across(name, block):
+        return send(name, block, "col", lambda i: i ^ 1)
+
+    def value(name):
+        return got[name][0]
 
     (own_b,) = mask_tile(b_tiles, mask_b, 0, 1)
-    z_b = by_two(own_b)
-    d_b = across(own_b)
+    by_two("Zb", own_b)
+    across("Db", own_b)
     own_c, own_1, own_2 = mask_tile(tied(b_tiles, [own_b]), mask_b, 1, 3)
-    z_c = by_two(own_c)
-    mine = [mask_rows(tied(a_window, [own_c]), mask_a)]
-
-    step = (z_b, d_b)
-    s_b = across(tied(z_b[0], *step))
-    z_1 = by_two(tied(own_1, *step))
-    lefts, offsets, held = [mine], [(0, False)], step
+    by_two("Zc", own_c)
+    mine = mask_rows(held("rows", tied(a_window, [own_c])), mask_a)
+
+    across("Sb", value("Zb"))
+    by_two("Z1", own_1)
+    lefts, offsets = [mine], [(0, False)]
     for distance in range(2, count, 2):
-        lefts.append([moved(tied(mine[0], *held), "row", lambda i: i - distance)])
+        send("Ax", mine, "row", lambda i: i - distance, f"Ax{distance}")
+        got["Ax"] = got[f"Ax{distance}"]
         offsets.append((distance, False))
-        held = lefts[-1:]
-
-    step = (z_c, s_b)
-    s_c = across(tied(z_c[0], *step))
-    z_2 = by_two(tied(own_2, *step))
-    near = [flip(mine, *step)]
-
-    step = (z_1, s_c)
-    y_1 = across(choose(tied(z_1[0], *step), own_1))
-    x_bc = by_two(choose(tied(z_c[0], *step), s_b[0]))
-
-    step = (z_2, y_1)
-    y_2 = across(choose(tied(z_2[0], *step), own_2))
-    w_1 = by_two(tied(y_1[0], *step))
-
-    step = (x_bc, y_2)
-    w_2 = by_two(tied(y_2[0], *step))
-    q_c = across(choose(tied(x_bc[0], *step), own_c))
-    for left in lefts[1:]:
-        near.append(flip(left, *step, *near[-1:]))
-    lefts += near
+    across("Sc", value("Zc"))
+    by_two("Z2", own_2)
+    send("Af", mine, "row", lambda i: i ^ 1)
+    across("Y1", choose(value("Z1"), own_1))
+    by_two("X", choose(value("Zc"), value("Sb")))
+    across("Y2", choose(value("Z2"), own_2))
+    by_two("W1", value("Y1"))
+    by_two("W2", value("Y2"))
+    across("Q", choose(value("X"), own_c))
+    for distance in range(2, count, 2):
+        send("Ar", value(f"Ax{distance}"), "row", lambda i: i ^ 1, f"Ar{distance}")
+        got["Ar"] = got[f"Ar{distance}"]
+    lefts += [value(f"Ax{distance}") for distance in range(2, count, 2)]
+    lefts += [value("Af")] + [value(f"Ar{distance}") for distance in range(2, count, 2)]
     offsets += [(distance, True) for distance, _ in offsets]
-    left = stack_rows([entry[0] for entry in lefts], tuple(offsets))
-
-    partial = add_products(
-        left,
-        [
-            (0, [own_2], [own_2]),
-            (1, [y_2[0]], [y_2[0]]),
-            (2, [z_2[0]], [z_2[0]]),
-        ],
-    )
+    left = stack_rows(lefts, tuple(offsets))
+    got["left"] = [left]
+
+    column_b = [(own_b, 0, 0), (value("Zb"), 2, 2), (value("Sb"), 3, 1), (choose(value("Db"), value("X")), 1, 3)]
+    column_c = [(own_c, 0, 0), (value("Zc"), 2, 2), (value("Sc"), 3, 1)]
+    column_1 = [(own_1, 0, 0), (value("Y1"), 1, 1), (value("Z1"), 2, 2)]
+    column_2 = [(own_2, 0, 0), (value("Y2"), 1, 1), (value("Z2"), 2, 2)]
+    piece = width // PIECES
+    partial = add_products(held("partial", left), [column_c, column_1])
+    partial_2 = add_products(held("partial2", left), [column_2])
+    product = add_products(held("first", left), [column_b], width=width)
     product = add_products(
-        left,
-        [
-            (0, [own_b, own_c, own_1], [own_b, own_c, own_1]),
-            (1, [d_b[0], q_c[0], y_1[0]], [s_b[0], s_c[0], y_1[0]]),
-            (2, [z_b[0], z_c[0], z_1[0]], [z_b[0], z_c[0], z_1[0]]),
-            (3, [s_b[0], s_c[0], w_1[0]], [x_bc[0], q_c[0], w_1[0]]),
-        ],
-        width=width,
-    )
-    return add_products(
-        left,
-        [(3, [w_2[0]], [w_2[0]])],
-        column=3 * (width // PIECES),
+        held("middle", left),
+        [[(value("Q"), 1, 3)], [(value("W1"), 3, 3)]],
+        column=piece,
         width=width,
         partial=partial,
         product=product,
+    )
+    return add_products(
+        held("last", left), [[(value("W2"), 3, 3)]], column=3 * piece, width=width, partial=partial_2, product=product
     )
 
 

time: 63.9 us -> 57.6 us (0.901)
  waiting for transfers between devices: 27.6 us -> 6.61 us
  starting transfers between devices: 24.2 us -> 36.9 us
  Pallas kernels: 11.8 us -> 13.8 us
    ppermute x16, waiting for transfers between devices: 27.6 us -> 6.61 us  [moved(): lax.ppermute(block, axis, [(i, target(i) % count) for i in range(count)])]
    ppermute x16, starting transfers between devices: 24.2 us -> 36.9 us  [moved(): lax.ppermute(block, axis, [(i, target(i) % count) for i in range(count)])]
    pallas_call x11 -> x14, Pallas kernels: 11.8 us -> 13.8 us  [kernel_call(): pl.pallas_call(kernel, out_shape=out_shape, in_specs=[pl.BlockSpec(memory...]
  transfers between devices with their start and end apart: 16 -> 16, of which waited for: 9 -> 5; matrix products, arithmetic and copies ran while one was open for 0% -> 0% of each run, Pallas kernels for 14% -> 20%
where the time goes in v3:
time: 57.6 us; the launch traced here: 57.4 us
  starting transfers between devices  36.9 us (64%)
  Pallas kernels  13.8 us (24%)
  waiting for transfers between devices  6.61 us (11%)
    ppermute x16, starting transfers between devices, moved(): lax.ppermute(block, axis, [(i, target(i) % count) for i in range(count)])  36.9 us
    pallas_call x14, Pallas kernels, kernel_call(): pl.pallas_call(kernel, out_shape=out_shape, in_specs=[pl.BlockSpec(memory...  13.8 us
    ppermute x16, waiting for transfers between devices, moved(): lax.ppermute(block, axis, [(i, target(i) % count) for i in range(count)])  6.61 us
  transfers between devices with their start and end apart: 16, of which 5 were waited for; matrix products, arithmetic and copies ran while one was open for 0% of the time, Pallas kernels for 20%

profile of v3, /device:TPU:0, one launch (start us, length us, event | category | flops | bytes accessed | tf_op | source)
XLA Modules:
  0.0 57.4 jit_solution(4466895589525551414)
XLA Ops:
  0.0 1.0 %mask_tile.2.refs_0_ = bf16[512,256]{1,0:T(8,128)(2,1)S(1)} custom-call(s32[2,4]{1,0:T(2,128)} %all_flags.4, bf16[512,1024]{1,0:T(8,128)(2,1)} %tile.2), custom_call_target="tpu_custom_call" | custom-call | bytes 1048592 | tf_op jit(solution)/shard_map/mask_tile/pallas_call | solution.py:25
  1.0 5.1 %collective-permute-start.1 = (bf16[512,256]{1,0:T(8,128)(2,1)S(1)}, bf16[512,256]{1,0:T(8,128)(2,1)S(1)}, u32[]{:S(2)}, u32[]{:S(2)}) collective-permute-start(bf16[512,256]{1,0:T(8,128)(2,1)S(1)} %mask_tile.2.refs_0_), channel_id=1, source_target_pairs={{0,6},{1,7},{2,0},{3,1},{4,2},{5,3},{6,4},{7,5},{8,14},{9,15},{10,... | collective-permute-start | bytes 786440 | tf_op jit(solution)/shard_map/send_Zb/ppermute | solution.py:242
  6.1 1.5 %collective-permute-start.3 = (bf16[512,256]{1,0:T(8,128)(2,1)S(1)}, bf16[512,256]{1,0:T(8,128)(2,1)S(1)}, u32[]{:S(2)}, u32[]{:S(2)}) collective-permute-start(bf16[512,256]{1,0:T(8,128)(2,1)S(1)} %mask_tile.2.refs_0_), channel_id=1, source_target_pairs={{0,1},{1,0},{2,3},{3,2},{4,5},{5,4},{6,7},{7,6},{8,9},{9,8},{10,11... | collective-permute-start | bytes 786440 | tf_op jit(solution)/shard_map/send_Db/ppermute | solution.py:242
  7.6 1.2 %mask_tile.3 = (bf16[512,256]{1,0:T(8,128)(2,1)S(1)}, bf16[512,256]{1,0:T(8,128)(2,1)S(1)}, bf16[512,256]{1,0:T(8,128)(2,1)S(1)}) custom-call(s32[2,4]{1,0:T(2,128)} %all_flags.4, bf16[512,1024]{1,0:T(8,128)(2,1)} %tile.2), custom_call_target="tpu_custom_call" | custom-call | bytes 1048592 | tf_op jit(solution)/shard_map/mask_tile/pallas_call | solution.py:25
  8.8 0.5 collective-permute-start.5
  9.3 1.3 %mask_rows.1.refs_0_ = bf16[256,2048]{1,0:T(8,128)(2,1)S(1)} custom-call(s32[4,8]{1,0:T(4,128)} %all_flags.5, bf16[256,2048]{1,0:T(8,128)(2,1)} %rows), custom_call_target="tpu_custom_call" | custom-call | bytes 1048640 | tf_op jit(solution)/shard_map/mask_rows/pallas_call | solution.py:25
  10.6 1.5 %collective-permute-start = (bf16[256,2048]{1,0:T(8,128)(2,1)S(1)}, bf16[256,2048]{1,0:T(8,128)(2,1)S(1)}, u32[]{:S(2)}, u32[]{:S(2)}) collective-permute-start(bf16[256,2048]{1,0:T(8,128)(2,1)S(1)} %mask_rows.1.refs_0_), channel_id=1, source_target_pairs={{0,16},{8,24},{16,0},{24,8},{1,17},{9,25},{17,1},{25,9},{2,18},{10... | collective-permute-start | bytes 3145736 | tf_op jit(solution)/shard_map/send_Ax/ppermute | solution.py:242
  12.1 0.7 %collective-permute-done.1.refs_1_ = bf16[512,256]{1,0:T(8,128)(2,1)S(1)} collective-permute-done((bf16[512,256]{1,0:T(8,128)(2,1)S(1)}, bf16[512,256]{1,0:T(8,128)(2,1)S(1)}, u32[]{:S(2)}, u32[]{:S(2)}) %collective-permute-start.1) | collective-permute-done | bytes 262176 | tf_op jit(solution)/shard_map/send_Zb/ppermute | solution.py:242
  12.8 1.5 %collective-permute-start.2 = (bf16[512,256]{1,0:T(8,128)(2,1)S(1)}, bf16[512,256]{1,0:T(8,128)(2,1)S(1)}, u32[]{:S(2)}, u32[]{:S(2)}) collective-permute-start(bf16[512,256]{1,0:T(8,128)(2,1)S(1)} %collective-permute-done.1.refs_1_), channel_id=1, source_target_pairs={{0,1},{1,0},{2,3},{3,2},{4,5},{5,4},{6,7},{7,6},{8,9},{9,8},{10,11... | collective-permute-start | bytes 786440 | tf_op jit(solution)/shard_map/send_Sb/ppermute | solution.py:242
  14.3 0.0 collective-permute-done.3.on_even
  14.3 4.3 %collective-permute-start.6 = (bf16[512,256]{1,0:T(8,128)(2,1)S(1)}, bf16[512,256]{1,0:T(8,128)(2,1)S(1)}, u32[]{:S(2)}, u32[]{:S(2)}) collective-permute-start(bf16[512,256]{1,0:T(8,128)(2,1)S(1)} %get-tuple-element.51.on_odd.refs_3_), channel_id=1, source_target_pairs={{0,6},{1,7},{2,0},{3,1},{4,2},{5,3},{6,4},{7,5},{8,14},{9,15},{10,... | collective-permute-start | bytes 786440 | tf_op jit(solution)/shard_map/send_Z1/ppermute | solution.py:242
  18.6 0.0 collective-permute-done.5.on_even.refs_1_
  18.6 1.3 %collective-permute-start.7 = (bf16[512,256]{1,0:T(8,128)(2,1)S(1)}, bf16[512,256]{1,0:T(8,128)(2,1)S(1)}, u32[]{:S(2)}, u32[]{:S(2)}) collective-permute-start(bf16[512,256]{1,0:T(8,128)(2,1)S(1)} %collective-permute-done.5.on_even.refs_1_), channel_id=1, source_target_pairs={{0,1},{1,0},{2,3},{3,2},{4,5},{5,4},{6,7},{7,6},{8,9},{9,8},{10,11... | collective-permute-start | bytes 786440 | tf_op jit(solution)/shard_map/send_Sc/ppermute | solution.py:242
  19.9 0.1 collective-permute-done.2.on_odd.refs_2_
  20.0 4.2 %collective-permute-start.9 = (bf16[512,256]{1,0:T(8,128)(2,1)S(1)}, bf16[512,256]{1,0:T(8,128)(2,1)S(1)}, u32[]{:S(2)}, u32[]{:S(2)}) collective-permute-start(bf16[512,256]{1,0:T(8,128)(2,1)S(1)} %get-tuple-element.56.on_odd.refs_0_), channel_id=1, source_target_pairs={{0,6},{1,7},{2,0},{3,1},{4,2},{5,3},{6,4},{7,5},{8,14},{9,15},{10,... | collective-permute-start | bytes 786440 | tf_op jit(solution)/shard_map/send_Z2/ppermute | solution.py:242
  24.2 0.0 collective-permute-done.6.on_even.refs_5_
  24.3 0.8 %collective-permute-done.7.refs_2_ = bf16[512,256]{1,0:T(8,128)(2,1)S(1)} collective-permute-done((bf16[512,256]{1,0:T(8,128)(2,1)S(1)}, bf16[512,256]{1,0:T(8,128)(2,1)S(1)}, u32[]{:S(2)}, u32[]{:S(2)}) %collective-permute-start.7) | collective-permute-done | bytes 262176 | tf_op jit(solution)/shard_map/send_Sc/ppermute | solution.py:242
  25.1 1.5 %collective-permute-start.11 = (bf16[512,256]{1,0:T(8,128)(2,1)S(1)}, bf16[512,256]{1,0:T(8,128)(2,1)S(1)}, u32[]{:S(2)}, u32[]{:S(2)}) collective-permute-start(bf16[512,256]{1,0:T(8,128)(2,1)S(1)} %choose.6), channel_id=1, source_target_pairs={{0,1},{1,0},{2,3},{3,2},{4,5},{5,4},{6,7},{7,6},{8,9},{9,8},{10,11... | collective-permute-start | bytes 786440 | tf_op jit(solution)/shard_map/send_Y1/ppermute | solution.py:242
  26.6 4.1 %collective-permute-start.8 = (bf16[512,256]{1,0:T(8,128)(2,1)S(1)}, bf16[512,256]{1,0:T(8,128)(2,1)S(1)}, u32[]{:S(2)}, u32[]{:S(2)}) collective-permute-start(bf16[512,256]{1,0:T(8,128)(2,1)S(1)} %choose.5), channel_id=1, source_target_pairs={{0,6},{1,7},{2,0},{3,1},{4,2},{5,3},{6,4},{7,5},{8,14},{9,15},{10,... | collective-permute-start | bytes 786440 | tf_op jit(solution)/shard_map/send_X/ppermute | solution.py:242
  30.7 0.0 collective-permute-done.9.on_even.refs_2_
  30.7 0.9 %collective-permute-start.10 = (bf16[512,256]{1,0:T(8,128)(2,1)S(1)}, bf16[512,256]{1,0:T(8,128)(2,1)S(1)}, u32[]{:S(2)}, u32[]{:S(2)}) collective-permute-start(bf16[512,256]{1,0:T(8,128)(2,1)S(1)} %choose.8), channel_id=1, source_target_pairs={{0,1},{1,0},{2,3},{3,2},{4,5},{5,4},{6,7},{7,6},{8,9},{9,8},{10,11... | collective-permute-start | bytes 786440 | tf_op jit(solution)/shard_map/send_Y2/ppermute | solution.py:242
  31.6 1.1 %collective-permute-done.11.refs_4_ = bf16[512,256]{1,0:T(8,128)(2,1)S(1)} collective-permute-done((bf16[512,256]{1,0:T(8,128)(2,1)S(1)}, bf16[512,256]{1,0:T(8,128)(2,1)S(1)}, u32[]{:S(2)}, u32[]{:S(2)}) %collective-permute-start.11) | collective-permute-done | bytes 262176 | tf_op jit(solution)/shard_map/send_Y1/ppermute | solution.py:242
  32.8 4.8 %collective-permute-start.12 = (bf16[512,256]{1,0:T(8,128)(2,1)S(1)}, bf16[512,256]{1,0:T(8,128)(2,1)S(1)}, u32[]{:S(2)}, u32[]{:S(2)}) collective-permute-start(bf16[512,256]{1,0:T(8,128)(2,1)S(1)} %collective-permute-done.11.refs_4_), channel_id=1, source_target_pairs={{0,6},{1,7},{2,0},{3,1},{4,2},{5,3},{6,4},{7,5},{8,14},{9,15},{10,... | collective-permute-start | bytes 786440 | tf_op jit(solution)/shard_map/send_W1/ppermute | solution.py:242
  37.5 0.0 collective-permute-start.4
  37.5 0.0 collective-permute-done.8.on_even.on_odd
  37.6 0.0 collective-permute-done.refs_1_
  37.6 0.0 collective-permute-done.10.refs_1_
  37.6 3.8 %collective-permute-done.12.refs_1_ = bf16[512,256]{1,0:T(8,128)(2,1)S(1)} collective-permute-done((bf16[512,256]{1,0:T(8,128)(2,1)S(1)}, bf16[512,256]{1,0:T(8,128)(2,1)S(1)}, u32[]{:S(2)}, u32[]{:S(2)}) %collective-permute-start.12) | collective-permute-done | bytes 262176 | tf_op jit(solution)/shard_map/send_W1/ppermute | solution.py:242
  41.4 0.0 collective-permute-start.13
  41.4 1.3 %collective-permute-start.15 = (bf16[512,256]{1,0:T(8,128)(2,1)S(1)}, bf16[512,256]{1,0:T(8,128)(2,1)S(1)}, u32[]{:S(2)}, u32[]{:S(2)}) collective-permute-start(bf16[512,256]{1,0:T(8,128)(2,1)S(1)} %choose.7), channel_id=1, source_target_pairs={{0,1},{1,0},{2,3},{3,2},{4,5},{5,4},{6,7},{7,6},{8,9},{9,8},{10,11... | collective-permute-start | bytes 786440 | tf_op jit(solution)/shard_map/send_Q/ppermute | solution.py:242
  42.8 4.3 %collective-permute-start.14 = (bf16[512,256]{1,0:T(8,128)(2,1)S(1)}, bf16[512,256]{1,0:T(8,128)(2,1)S(1)}, u32[]{:S(2)}, u32[]{:S(2)}) collective-permute-start(bf16[512,256]{1,0:T(8,128)(2,1)S(1)} %collective-permute-done.10.refs_1_), channel_id=1, source_target_pairs={{0,6},{1,7},{2,0},{3,1},{4,2},{5,3},{6,4},{7,5},{8,14},{9,15},{10,... | collective-permute-start | bytes 786440 | tf_op jit(solution)/shard_map/send_W2/ppermute | solution.py:242
  47.1 0.0 collective-permute-done.4.refs_2_
  47.1 0.0 collective-permute-done.13.refs_3_
  47.1 0.3 stack_rows.1.left
  47.5 2.5 %add_products.7.refs_3_ = bf16[1024,1024]{1,0:T(8,128)(2,1)} custom-call(bf16[1024,2048]{1,0:T(8,128)(2,1)S(1)} %stack_rows.1.left, bf16[512,256]{1,0:T(8,128)(2,1)S(1)} %mask_tile.2.refs_0_, bf16[512,256]{1,0:T(8,128)(2,1)S(1)} %collective-permute-done.1.refs_1_, bf16[512,256]{1,0:T(8,128)(2,1)S(1)} %collective-permute-done.2.on_odd.refs_2_, ...), custom_call_target="tpu_custom_call" | custom-call | flops 1073741824 | bytes 5242880 | tf_op jit(solution)/shard_map/add_products/pallas_call | solution.py:25
  50.0 2.3 %add_products.6.refs_2_ = f32[1024,512]{1,0:T(8,128)S(1)} custom-call(bf16[1024,2048]{1,0:T(8,128)(2,1)S(1)} %stack_rows.1.left, bf16[512,256]{1,0:T(8,128)(2,1)S(1)} %get-tuple-element.43.on_odd.refs_0_, bf16[512,256]{1,0:T(8,128)(2,1)S(1)} %collective-permute-done.5.on_even.refs_1_, bf16[512,256]{1,0:T(8,128)(2,1)S(1)} %collective-permute-done.7.refs_2_, ...), custom_call_target="tpu_custom_call" | custom-call | flops 1610612736 | bytes 5767168 | tf_op jit(solution)/shard_map/add_products/pallas_call | solution.py:25
  52.3 0.0 collective-permute-done.15.refs_0_
  52.3 2.0 %add_products.8.refs_2_ = bf16[1024,1024]{1,0:T(8,128)(2,1)} custom-call(bf16[1024,2048]{1,0:T(8,128)(2,1)S(1)} %stack_rows.1.left, bf16[512,256]{1,0:T(8,128)(2,1)S(1)} %collective-permute-done.15.refs_0_, bf16[512,256]{1,0:T(8,128)(2,1)S(1)} %collective-permute-done.12.refs_1_, ...), custom_call_target="tpu_custom_call", output_to_operand_aliasing={{}: (4, {})} | custom-call | flops 536870912 | bytes 7864320 | tf_op jit(solution)/shard_map/add_products/pallas_call | solution.py:25
  54.3 1.5 %add_products.5.refs_1_ = f32[1024,256]{1,0:T(8,128)S(1)} custom-call(bf16[1024,2048]{1,0:T(8,128)(2,1)S(1)} %stack_rows.1.left, bf16[512,256]{1,0:T(8,128)(2,1)S(1)} %get-tuple-element.56.on_odd.refs_0_, bf16[512,256]{1,0:T(8,128)(2,1)S(1)} %collective-permute-done.10.refs_1_, bf16[512,256]{1,0:T(8,128)(2,1)S(1)} %collective-permute-done.9.on_even.refs_2_), custom_call_target="tpu_custom_call" | custom-call | flops 805306368 | bytes 4980736 | tf_op jit(solution)/shard_map/add_products/pallas_call | solution.py:25
  55.8 0.0 collective-permute-done.14.refs_0_
  55.8 1.6 %add_products.9 = bf16[1024,1024]{1,0:T(8,128)(2,1)} custom-call(bf16[1024,2048]{1,0:T(8,128)(2,1)S(1)} %stack_rows.1.left, bf16[512,256]{1,0:T(8,128)(2,1)S(1)} %collective-permute-done.14.refs_0_, f32[1024,256]{1,0:T(8,128)S(1)} %add_products.5.refs_1_, bf16[1024,1024]{1,0:T(8,128)(2,1)} %add_products.8.refs_2_), custom_call_target="tpu_custom_call", output_to_operand_aliasing={{}: (3, {})} | custom-call | flops 268435456 | bytes 7077888 | tf_op jit(solution)/shard_map/add_products/pallas_call | solution.py:25
  (5 shorter events, 0.1 us)
Async XLA Ops:
  1.0 11.8 %collective-permute-start.1 = (bf16[512,256]{1,0:T(8,128)(2,1)S(1)}, bf16[512,256]{1,0:T(8,128)(2,1)S(1)}, u32[]{:S(2)}, u32[]{:S(2)}) collective-permute-start(bf16[512,256]{1,0:T(8,128)(2,1)S(1)} %mask_tile.2.refs_0_), channel_id=1, source_target_pairs={{0,6},{1,7},{2,0},{3,1},{4,2},{5,3},{6,4},{7,5},{8,14},{9,15},{10,... | collective-permute-start | bytes 786440 | tf_op jit(solution)/shard_map/send_Zb/ppermute | solution.py:242
  6.1 8.2 %collective-permute-start.3 = (bf16[512,256]{1,0:T(8,128)(2,1)S(1)}, bf16[512,256]{1,0:T(8,128)(2,1)S(1)}, u32[]{:S(2)}, u32[]{:S(2)}) collective-permute-start(bf16[512,256]{1,0:T(8,128)(2,1)S(1)} %mask_tile.2.refs_0_), channel_id=1, source_target_pairs={{0,1},{1,0},{2,3},{3,2},{4,5},{5,4},{6,7},{7,6},{8,9},{9,8},{10,11... | collective-permute-start | bytes 786440 | tf_op jit(solution)/shard_map/send_Db/ppermute | solution.py:242
  8.8 9.8 %collective-permute-start.5 = (bf16[512,256]{1,0:T(8,128)(2,1)S(1)}, bf16[512,256]{1,0:T(8,128)(2,1)S(1)}, u32[]{:S(2)}, u32[]{:S(2)}) collective-permute-start(bf16[512,256]{1,0:T(8,128)(2,1)S(1)} %get-tuple-element.43.on_odd.refs_0_), channel_id=1, source_target_pairs={{0,6},{1,7},{2,0},{3,1},{4,2},{5,3},{6,4},{7,5},{8,14},{9,15},{10,... | collective-permute-start | bytes 786440 | tf_op jit(solution)/shard_map/send_Zc/ppermute | solution.py:242
  10.6 27.0 %collective-permute-start = (bf16[256,2048]{1,0:T(8,128)(2,1)S(1)}, bf16[256,2048]{1,0:T(8,128)(2,1)S(1)}, u32[]{:S(2)}, u32[]{:S(2)}) collective-permute-start(bf16[256,2048]{1,0:T(8,128)(2,1)S(1)} %mask_rows.1.refs_0_), channel_id=1, source_target_pairs={{0,16},{8,24},{16,0},{24,8},{1,17},{9,25},{17,1},{25,9},{2,18},{10... | collective-permute-start | bytes 3145736 | tf_op jit(solution)/shard_map/send_Ax/ppermute | solution.py:242
  12.8 7.2 %collective-permute-start.2 = (bf16[512,256]{1,0:T(8,128)(2,1)S(1)}, bf16[512,256]{1,0:T(8,128)(2,1)S(1)}, u32[]{:S(2)}, u32[]{:S(2)}) collective-permute-start(bf16[512,256]{1,0:T(8,128)(2,1)S(1)} %collective-permute-done.1.refs_1_), channel_id=1, source_target_pairs={{0,1},{1,0},{2,3},{3,2},{4,5},{5,4},{6,7},{7,6},{8,9},{9,8},{10,11... | collective-permute-start | bytes 786440 | tf_op jit(solution)/shard_map/send_Sb/ppermute | solution.py:242
  14.3 9.9 %collective-permute-start.6 = (bf16[512,256]{1,0:T(8,128)(2,1)S(1)}, bf16[512,256]{1,0:T(8,128)(2,1)S(1)}, u32[]{:S(2)}, u32[]{:S(2)}) collective-permute-start(bf16[512,256]{1,0:T(8,128)(2,1)S(1)} %get-tuple-element.51.on_odd.refs_3_), channel_id=1, source_target_pairs={{0,6},{1,7},{2,0},{3,1},{4,2},{5,3},{6,4},{7,5},{8,14},{9,15},{10,... | collective-permute-start | bytes 786440 | tf_op jit(solution)/shard_map/send_Z1/ppermute | solution.py:242
  18.6 6.5 %collective-permute-start.7 = (bf16[512,256]{1,0:T(8,128)(2,1)S(1)}, bf16[512,256]{1,0:T(8,128)(2,1)S(1)}, u32[]{:S(2)}, u32[]{:S(2)}) collective-permute-start(bf16[512,256]{1,0:T(8,128)(2,1)S(1)} %collective-permute-done.5.on_even.refs_1_), channel_id=1, source_target_pairs={{0,1},{1,0},{2,3},{3,2},{4,5},{5,4},{6,7},{7,6},{8,9},{9,8},{10,11... | collective-permute-start | bytes 786440 | tf_op jit(solution)/shard_map/send_Sc/ppermute | solution.py:242
  20.0 10.7 %collective-permute-start.9 = (bf16[512,256]{1,0:T(8,128)(2,1)S(1)}, bf16[512,256]{1,0:T(8,128)(2,1)S(1)}, u32[]{:S(2)}, u32[]{:S(2)}) collective-permute-start(bf16[512,256]{1,0:T(8,128)(2,1)S(1)} %get-tuple-element.56.on_odd.refs_0_), channel_id=1, source_target_pairs={{0,6},{1,7},{2,0},{3,1},{4,2},{5,3},{6,4},{7,5},{8,14},{9,15},{10,... | collective-permute-start | bytes 786440 | tf_op jit(solution)/shard_map/send_Z2/ppermute | solution.py:242
  25.1 7.7 %collective-permute-start.11 = (bf16[512,256]{1,0:T(8,128)(2,1)S(1)}, bf16[512,256]{1,0:T(8,128)(2,1)S(1)}, u32[]{:S(2)}, u32[]{:S(2)}) collective-permute-start(bf16[512,256]{1,0:T(8,128)(2,1)S(1)} %choose.6), channel_id=1, source_target_pairs={{0,1},{1,0},{2,3},{3,2},{4,5},{5,4},{6,7},{7,6},{8,9},{9,8},{10,11... | collective-permute-start | bytes 786440 | tf_op jit(solution)/shard_map/send_Y1/ppermute | solution.py:242
  26.6 10.9 %collective-permute-start.8 = (bf16[512,256]{1,0:T(8,128)(2,1)S(1)}, bf16[512,256]{1,0:T(8,128)(2,1)S(1)}, u32[]{:S(2)}, u32[]{:S(2)}) collective-permute-start(bf16[512,256]{1,0:T(8,128)(2,1)S(1)} %choose.5), channel_id=1, source_target_pairs={{0,6},{1,7},{2,0},{3,1},{4,2},{5,3},{6,4},{7,5},{8,14},{9,15},{10,... | collective-permute-start | bytes 786440 | tf_op jit(solution)/shard_map/send_X/ppermute | solution.py:242
  30.7 6.8 %collective-permute-start.10 = (bf16[512,256]{1,0:T(8,128)(2,1)S(1)}, bf16[512,256]{1,0:T(8,128)(2,1)S(1)}, u32[]{:S(2)}, u32[]{:S(2)}) collective-permute-start(bf16[512,256]{1,0:T(8,128)(2,1)S(1)} %choose.8), channel_id=1, source_target_pairs={{0,1},{1,0},{2,3},{3,2},{4,5},{5,4},{6,7},{7,6},{8,9},{9,8},{10,11... | collective-permute-start | bytes 786440 | tf_op jit(solution)/shard_map/send_Y2/ppermute | solution.py:242
  32.8 8.7 %collective-permute-start.12 = (bf16[512,256]{1,0:T(8,128)(2,1)S(1)}, bf16[512,256]{1,0:T(8,128)(2,1)S(1)}, u32[]{:S(2)}, u32[]{:S(2)}) collective-permute-start(bf16[512,256]{1,0:T(8,128)(2,1)S(1)} %collective-permute-done.11.refs_4_), channel_id=1, source_target_pairs={{0,6},{1,7},{2,0},{3,1},{4,2},{5,3},{6,4},{7,5},{8,14},{9,15},{10,... | collective-permute-start | bytes 786440 | tf_op jit(solution)/shard_map/send_W1/ppermute | solution.py:242
  37.5 9.6 %collective-permute-start.4 = (bf16[256,2048]{1,0:T(8,128)(2,1)S(1)}, bf16[256,2048]{1,0:T(8,128)(2,1)S(1)}, u32[]{:S(2)}, u32[]{:S(2)}) collective-permute-start(bf16[256,2048]{1,0:T(8,128)(2,1)S(1)} %mask_rows.1.refs_0_), channel_id=1, source_target_pairs={{0,8},{8,0},{16,24},{24,16},{1,9},{9,1},{17,25},{25,17},{2,10},{10... | collective-permute-start | bytes 3145736 | tf_op jit(solution)/shard_map/send_Af/ppermute | solution.py:242
  41.4 5.7 %collective-permute-start.13 = (bf16[256,2048]{1,0:T(8,128)(2,1)S(1)}, bf16[256,2048]{1,0:T(8,128)(2,1)S(1)}, u32[]{:S(2)}, u32[]{:S(2)}) collective-permute-start(bf16[256,2048]{1,0:T(8,128)(2,1)S(1)} %collective-permute-done.refs_1_), channel_id=1, source_target_pairs={{0,8},{8,0},{16,24},{24,16},{1,9},{9,1},{17,25},{25,17},{2,10},{10... | collective-permute-start | bytes 3145736 | tf_op jit(solution)/shard_map/send_Ar/ppermute | solution.py:242
  41.4 10.9 %collective-permute-start.15 = (bf16[512,256]{1,0:T(8,128)(2,1)S(1)}, bf16[512,256]{1,0:T(8,128)(2,1)S(1)}, u32[]{:S(2)}, u32[]{:S(2)}) collective-permute-start(bf16[512,256]{1,0:T(8,128)(2,1)S(1)} %choose.7), channel_id=1, source_target_pairs={{0,1},{1,0},{2,3},{3,2},{4,5},{5,4},{6,7},{7,6},{8,9},{9,8},{10,11... | collective-permute-start | bytes 786440 | tf_op jit(solution)/shard_map/send_Q/ppermute | solution.py:242
  42.8 13.0 %collective-permute-start.14 = (bf16[512,256]{1,0:T(8,128)(2,1)S(1)}, bf16[512,256]{1,0:T(8,128)(2,1)S(1)}, u32[]{:S(2)}, u32[]{:S(2)}) collective-permute-start(bf16[512,256]{1,0:T(8,128)(2,1)S(1)} %collective-permute-done.10.refs_1_), channel_id=1, source_target_pairs={{0,6},{1,7},{2,0},{3,1},{4,2},{5,3},{6,4},{7,5},{8,14},{9,15},{10,... | collective-permute-start | bytes 786440 | tf_op jit(solution)/shard_map/send_W2/ppermute | solution.py:242

commit v4 on v3

v4 whole, which is shorter than its diff:
```python
import functools

import jax
import jax.numpy as jnp
from jax import lax
from jax.experimental import pallas as pl
from jax.experimental.pallas import tpu as pltpu
from jax.sharding import PartitionSpec as P

BS = 256
STEPS = 4
PIECES = 4

ANY = pl.ANY
HBM = pltpu.MemorySpace.HBM
VMEM = pltpu.MemorySpace.VMEM


def pinned(value, space=VMEM):
    return pltpu.with_memory_space_constraint(value, space)


def kernel_call(kernel, name, out_shape, operands, spaces, out_space, scratch=(), flops=0):
    moved = 2 * sum(value.size for value in operands)
    return pl.pallas_call(
        kernel,
        out_shape=out_shape,
        in_specs=[pl.BlockSpec(memory_space=space) for space in spaces],
        out_specs=jax.tree.map(lambda _: pl.BlockSpec(memory_space=out_space), out_shape),
        scratch_shapes=list(scratch),
        cost_estimate=pl.CostEstimate(flops=flops, bytes_accessed=moved, transcendentals=0),
        compiler_params=pltpu.CompilerParams(vmem_limit_bytes=8 << 20),
        name=name,
    )(*operands)


def mask_tile_kernel(first, all_flags, tile, *refs):
    *outs, flags, flag_sem, sem = refs
    width = outs[0].shape[1]
    flag_copy = pltpu.make_async_copy(all_flags, flags, flag_sem)
    flag_copy.start()
    copies = [
        pltpu.make_async_copy(tile.at[:, (first + n) * width : (first + n + 1) * width], out, sem.at[n])
        for n, out in enumerate(outs)
    ]
    for copy in copies:
        copy.start()
    flag_copy.wait()
    for n, (copy, out) in enumerate(zip(copies, outs)):
        copy.wait()
        for row in range(0, out.shape[0], BS):
            for column in range(0, width, BS):

                @pl.when(flags[row // BS, ((first + n) * width + column) // BS] == 0)
                def _():
                    out[row : row + BS, column : column + BS] = jnp.zeros((BS, BS), out.dtype)


def mask_tile(tile, flags, first, count):
    shape = (tile.shape[0], tile.shape[1] // PIECES)
    return kernel_call(
        functools.partial(mask_tile_kernel, first),
        "mask_tile",
        [VMEM(shape, tile.dtype)] * count,
        [pinned(flags, HBM), pinned(tile, HBM)],
        [HBM, HBM],
        VMEM,
        [pltpu.SMEM(flags.shape, flags.dtype), pltpu.SemaphoreType.DMA, pltpu.SemaphoreType.DMA((count,))],
    )


def choose_kernel(on_even, on_odd, out):
    odd = lax.axis_index("col") % 2

    @pl.when(odd == 0)
    def _():
        out[...] = on_even[...]

    @pl.when(odd == 1)
    def _():
        out[...] = on_odd[...]


def choose(on_even, on_odd):
    return kernel_call(
        choose_kernel,
        "choose",
        VMEM(on_even.shape, on_even.dtype),
        [pinned(on_even), pinned(on_odd)],
        [VMEM, VMEM],
        VMEM,
    )


def stack_rows_kernel(offsets, all_flags, *refs):
    *shards, out, flags, flag_sem, sem = refs
    rows = shards[0].shape[0]
    me, count = lax.axis_index("row"), len(shards)
    flag_copy = pltpu.make_async_copy(all_flags, flags, flag_sem)
    flag_copy.start()
    copies = []
    for n, (shard, (distance, flip)) in enumerate(zip(shards, offsets)):
        place = lax.rem(me + distance, count)
        if flip:
            place = place + 1 - 2 * lax.rem(place, 2)
        start = pl.multiple_of(place * rows, rows)
        copies.append(pltpu.make_async_copy(shard, out.at[pl.ds(start, rows), :], sem.at[n]))
    for copy in copies:
        copy.start()
    flag_copy.wait()
    for copy in copies:
        copy.wait()

    @pl.loop(0, out.shape[0] // BS)
    def _(block_row):
        where = pl.ds(pl.multiple_of(block_row * BS, BS), BS)
        for column in range(out.shape[1] // BS):

            @pl.when(flags[block_row, column] == 0)
            def _():
                out[where, column * BS : (column + 1) * BS] = jnp.zeros((BS, BS), out.dtype)


def stack_rows(shards, offsets, flags):
    rows, depth = shards[0].shape
    count = len(shards)
    return kernel_call(
        functools.partial(stack_rows_kernel, offsets),
        "stack_rows",
        VMEM((rows * count, depth), shards[0].dtype),
        [pinned(flags, HBM), *shards],
        [HBM] + [ANY] * count,
        VMEM,
        [pltpu.SMEM(flags.shape, flags.dtype), pltpu.SemaphoreType.DMA, pltpu.SemaphoreType.DMA((count,))],
    )


def sums(left, tiles, places, partial, rows, store):
    depth, width = tiles[0].shape
    odd = lax.axis_index("col") % 2
    for place, terms in enumerate(places):
        columns = slice(place * width, (place + 1) * width)
        total = None if partial is None else partial[rows, columns]
        for number, on_even, on_odd in terms:
            start = on_even * depth
            if on_even != on_odd:
                start = pl.multiple_of(start + odd * ((on_odd - on_even) * depth), depth)
            term = jnp.dot(left[rows, pl.ds(start, depth)], tiles[number][...], preferred_element_type=jnp.float32)
            total = term if total is None else total + term
        store(columns, total)


def chunks_of(left):
    chunk = min(BS, left.shape[0])
    return chunk, left.shape[0] // chunk


def sum_kernel(plan, left, *refs):
    places, rights, has_partial = plan
    partial = refs[rights] if has_partial else None
    out = refs[-1]
    chunk, count = chunks_of(left)

    @pl.loop(0, count)
    def _(index):
        rows = pl.ds(pl.multiple_of(index * chunk, chunk), chunk)

        def store(columns, total):
            out[rows, columns] = total.astype(out.dtype)

        sums(left, refs[:rights], places, partial, rows, store)


def last_kernel(plan, left, *refs):
    places, rights, ready_columns, column = plan
    tiles, partial = refs[:rights], refs[rights]
    ready, (out, result, sem, ready_sem) = refs[rights + 1 : -4], refs[-4:]
    chunk, count = chunks_of(left)
    copies = [
        pltpu.make_async_copy(block, out.at[:, start : start + block.shape[1]], ready_sem.at[n])
        for n, (block, start) in enumerate(zip(ready, ready_columns))
    ]
    for copy in copies:
        copy.start()

    def out_copy(index):
        rows = pl.ds(pl.multiple_of(index * chunk, chunk), chunk)
        return pltpu.make_async_copy(
            result.at[index], out.at[rows, column : column + result.shape[2]], sem.at[index]
        )

    @pl.loop(0, count)
    def _(index):
        rows = pl.ds(pl.multiple_of(index * chunk, chunk), chunk)

        def store(columns, total):
            result[index, :, columns] = total.astype(out.dtype)

        sums(left, tiles, places, partial, rows, store)
        out_copy(index).start()

    for copy in copies:
        copy.wait()

    @pl.loop(0, count)
    def _(index):
        out_copy(index).wait()


def number_terms(places):
    tiles = []
    for terms in places:
        for tile, _, _ in terms:
            if not any(tile is known for known in tiles):
                tiles.append(tile)
    numbered = tuple(
        tuple((next(n for n, known in enumerate(tiles) if known is tile), a, b) for tile, a, b in terms)
        for terms in places
    )
    return tiles, numbered


def add_products(name, left, places, partial=None, dtype=jnp.float32):
    tiles, numbered = number_terms(places)
    rows, width = left.shape[0], tiles[0].shape[1]
    operands = [pinned(x) for x in (left, *tiles, *([] if partial is None else [partial]))]
    return kernel_call(
        functools.partial(sum_kernel, (numbered, len(tiles), partial is not None)),
        "sum_" + name,
        VMEM((rows, width * len(places)), dtype),
        operands,
        [VMEM] * len(operands),
        VMEM,
        flops=2 * rows * tiles[0].size * sum(len(terms) for terms in places),
    )


def finish_product(left, places, column, width, partial, ready):
    tiles, numbered = number_terms(places)
    rows = left.shape[0]
    columns = tiles[0].shape[1] * len(places)
    chunk, count = chunks_of(left)
    operands = [pinned(x) for x in (left, *tiles, partial, *[block for block, _ in ready])]
    plan = (numbered, len(tiles), tuple(start for _, start in ready), column)
    return kernel_call(
        functools.partial(last_kernel, plan),
        "sum_last",
        jax.ShapeDtypeStruct((rows, width), left.dtype),
        operands,
        [VMEM] * len(operands),
        HBM,
        [
            pltpu.VMEM((count, chunk, columns), left.dtype),
            pltpu.SemaphoreType.DMA((count,)),
            pltpu.SemaphoreType.DMA((len(ready),)),
        ],
        flops=2 * rows * tiles[0].size * len(places),
    )


def moved(block, axis, target):
    count = lax.axis_size(axis)
    return lax.ppermute(block, axis, [(i, target(i) % count) for i in range(count)])


def tied(value, *entries):
    value, *others = lax.optimization_barrier((value, *[entry[0] for entry in entries]))
    for entry, other in zip(entries, others):
        entry[0] = other
    return value


HELD = {
    "Ax": ["own_b"],
    "Z1": ["Db", "own_b"],
    "Z2": ["Db", "Zb"],
    "Af": ["Zb", "Z1", "own_c"],
    "Y1": ["own_b", "Sb", "Zb"],
    "X": ["own_c", "own_b", "Sc"],
    "Y2": ["Zb", "Sb", "Y1", "Z2", "Ax", "Z1", "Zc", "Db", "Sc"],
    "W1": ["Y1"],
    "Q": ["Z2", "Db", "X"],
    "Ar": ["X", "Sb", "Zc", "own_b", "Ax", "Sc"],
    "first": ["X", "Sc", "Af", "Z2", "Z1"],
    "last": ["Sc", "Db"],
    "partial": ["X", "Ax", "Db", "own_b", "Z1"],
    "partial2": ["Z1"],
    "middle": ["Y2", "Sb", "Af"],
    "W2": ["Y2", "first", "X"],
    "Sc": ["Sb", "Zc", "own_c"],
    "Sb": ["own_c"],
}


def shards(a_window, b_tiles, mask_a, mask_b):
    width = b_tiles.shape[1]
    count = lax.axis_size("row")
    got = {}

    def held(name, value):
        names = HELD.get(name, [])
        return tied(value, *[got[known] for known in names]) if names else value

    def send(name, block, axis, target, key=None):
        with jax.named_scope("send_" + name):
            got[key or name] = [moved(held(name, block), axis, target)]
        return got[key or name][0]

    def by_two(name, block):
        return send(name, block, "col", lambda i: i - 2)

    def across(name, block):
        return send(name, block, "col", lambda i: i ^ 1)

    def value(name):
        return got[name][0]

    (own_b,) = mask_tile(b_tiles, mask_b, 0, 1)
    got["own_b"] = [own_b]
    by_two("Zb", own_b)
    across("Db", own_b)
    own_c, own_1, own_2 = mask_tile(tied(b_tiles, [own_b]), mask_b, 1, 3)
    got["own_c"] = [own_c]
    by_two("Zc", own_c)
    mine = a_window

    lefts, offsets = [mine], [(0, False)]
    for distance in range(2, count, 2):
        send("Ax", mine, "row", lambda i: i - distance, f"Ax{distance}")
        got["Ax"] = got[f"Ax{distance}"]
        offsets.append((distance, False))
    across("Sb", value("Zb"))
    by_two("Z1", own_1)
    across("Sc", value("Zc"))
    by_two("Z2", own_2)
    send("Af", mine, "row", lambda i: i ^ 1)
    across("Y1", choose(value("Z1"), own_1))
    by_two("X", choose(value("Zc"), value("Sb")))
    across("Y2", choose(value("Z2"), own_2))
    for distance in range(2, count, 2):
        send("Ar", value(f"Ax{distance}"), "row", lambda i: i ^ 1, f"Ar{distance}")
        got["Ar"] = got[f"Ar{distance}"]
    lefts += [value(f"Ax{distance}") for distance in range(2, count, 2)]
    lefts += [value("Af")] + [value(f"Ar{distance}") for distance in range(2, count, 2)]
    offsets += [(distance, True) for distance, _ in offsets]
    left = stack_rows(lefts, tuple(offsets), mask_a)
    by_two("W1", value("Y1"))
    column_c = [(own_c, 0, 0), (value("Zc"), 2, 2), (value("Sc"), 3, 1)]
    column_1 = [(own_1, 0, 0), (value("Y1"), 1, 1), (value("Z1"), 2, 2)]
    got["partial"] = [add_products("partial", held("partial", left), [column_c, column_1])]
    column_2 = [(own_2, 0, 0), (value("Y2"), 1, 1), (value("Z2"), 2, 2)]
    got["partial2"] = [add_products("partial2", held("partial2", left), [column_2])]
    across("Q", choose(value("X"), own_c))
    column_b = [(own_b, 0, 0), (value("Zb"), 2, 2), (value("Sb"), 3, 1), (choose(value("Db"), value("X")), 1, 3)]
    got["first"] = [add_products("first", held("first", left), [column_b], dtype=left.dtype)]
    by_two("W2", value("Y2"))

    piece = width // PIECES
    middle = add_products(
        "middle",
        held("middle", left),
        [[(value("Q"), 1, 3)], [(value("W1"), 3, 3)]],
        partial=value("partial"),
        dtype=left.dtype,
    )
    return finish_product(
        held("last", left),
        [[(value("W2"), 3, 3)]],
        3 * piece,
        width,
        value("partial2"),
        [(value("first"), 0), (middle, piece)],
    )


def solution(mesh):
    return jax.shard_map(
        shards,
        mesh=mesh,
        in_specs=(P(("col", "row"), None), P("col", "row"), P("col", None), P("col", "row")),
        out_specs=P("col", "row"),
        check_vma=False,
    )
```

time: 57.6 us -> 56.2 us (0.976)
  waiting for transfers between devices: 6.61 us -> 14.8 us
  starting transfers between devices: 36.9 us -> 29.2 us
  Pallas kernels: 13.8 us -> 12 us
    ppermute x16, waiting for transfers between devices: 6.61 us -> 14.8 us  [moved(): lax.ppermute(block, axis, [(i, target(i) % count) for i in range(count)])]
    ppermute x16, starting transfers between devices: 36.9 us -> 29.2 us  [moved(): lax.ppermute(block, axis, [(i, target(i) % count) for i in range(count)])]
    pallas_call x14 -> x13, Pallas kernels: 13.8 us -> 12 us  [kernel_call(): pl.pallas_call(kernel, out_shape=out_shape, in_specs=[pl.BlockSpec(memory...]
  transfers between devices with their start and end apart: 16 -> 16, of which waited for: 5 -> 7; matrix products, arithmetic and copies ran while one was open for 0% -> 0% of each run, Pallas kernels for 20% -> 17%
where the time goes in v4:
time: 56.2 us; the launch traced here: 56.1 us
  starting transfers between devices  29.2 us (52%)
  waiting for transfers between devices  14.8 us (26%)
  Pallas kernels  12 us (21%)
    ppermute x16, starting transfers between devices, moved(): lax.ppermute(block, axis, [(i, target(i) % count) for i in range(count)])  29.2 us
    ppermute x16, waiting for transfers between devices, moved(): lax.ppermute(block, axis, [(i, target(i) % count) for i in range(count)])  14.8 us
    pallas_call x13, Pallas kernels, kernel_call(): pl.pallas_call(kernel, out_shape=out_shape, in_specs=[pl.BlockSpec(memory...  12 us
  transfers between devices with their start and end apart: 16, of which 7 were waited for; matrix products, arithmetic and copies ran while one was open for 0% of the time, Pallas kernels for 17%

profile of v4, /device:TPU:0, one launch (start us, length us, event | category | flops | bytes accessed | tf_op | source)
XLA Modules:
  0.0 56.1 jit_solution(18366768772384607594)
XLA Ops:
  0.0 0.0 copy-start
  0.0 1.1 %mask_tile.2.refs_0_ = bf16[512,256]{1,0:T(8,128)(2,1)S(1)} custom-call(s32[2,4]{1,0:T(2,128)} %all_flags.4, bf16[512,1024]{1,0:T(8,128)(2,1)} %tile.2), custom_call_target="tpu_custom_call" | custom-call | bytes 1048592 | tf_op jit(solution)/shard_map/mask_tile/pallas_call | solution.py:25
  1.1 5.1 %collective-permute-start.1 = (bf16[512,256]{1,0:T(8,128)(2,1)S(1)}, bf16[512,256]{1,0:T(8,128)(2,1)S(1)}, u32[]{:S(2)}, u32[]{:S(2)}) collective-permute-start(bf16[512,256]{1,0:T(8,128)(2,1)S(1)} %mask_tile.2.refs_0_), channel_id=1, source_target_pairs={{0,6},{1,7},{2,0},{3,1},{4,2},{5,3},{6,4},{7,5},{8,14},{9,15},{10,... | collective-permute-start | bytes 786440 | tf_op jit(solution)/shard_map/send_Zb/ppermute | solution.py:263
  6.2 1.5 %collective-permute-start.7 = (bf16[256,2048]{1,0:T(8,128)(2,1)}, bf16[256,2048]{1,0:T(8,128)(2,1)S(1)}, u32[]{:S(2)}, u32[]{:S(2)}) collective-permute-start(bf16[256,2048]{1,0:T(8,128)(2,1)} %refs_0_.1), channel_id=1, source_target_pairs={{0,16},{8,24},{16,0},{24,8},{1,17},{9,25},{17,1},{25,9},{2,18},{10... | collective-permute-start | bytes 3145736 | tf_op jit(solution)/shard_map/send_Ax/ppermute | solution.py:263
  7.7 1.5 %collective-permute-start = (bf16[512,256]{1,0:T(8,128)(2,1)S(1)}, bf16[512,256]{1,0:T(8,128)(2,1)S(1)}, u32[]{:S(2)}, u32[]{:S(2)}) collective-permute-start(bf16[512,256]{1,0:T(8,128)(2,1)S(1)} %mask_tile.2.refs_0_), channel_id=1, source_target_pairs={{0,1},{1,0},{2,3},{3,2},{4,5},{5,4},{6,7},{7,6},{8,9},{9,8},{10,11... | collective-permute-start | bytes 786440 | tf_op jit(solution)/shard_map/send_Db/ppermute | solution.py:263
  9.2 1.1 %mask_tile.3 = (bf16[512,256]{1,0:T(8,128)(2,1)S(1)}, bf16[512,256]{1,0:T(8,128)(2,1)S(1)}, bf16[512,256]{1,0:T(8,128)(2,1)S(1)}) custom-call(s32[2,4]{1,0:T(2,128)} %all_flags.4, bf16[512,1024]{1,0:T(8,128)(2,1)} %tile.2), custom_call_target="tpu_custom_call" | custom-call | bytes 1048592 | tf_op jit(solution)/shard_map/mask_tile/pallas_call | solution.py:25
  10.3 0.5 collective-permute-start.4
  10.8 2.0 %collective-permute-done.1.refs_1_ = bf16[512,256]{1,0:T(8,128)(2,1)S(1)} collective-permute-done((bf16[512,256]{1,0:T(8,128)(2,1)S(1)}, bf16[512,256]{1,0:T(8,128)(2,1)S(1)}, u32[]{:S(2)}, u32[]{:S(2)}) %collective-permute-start.1) | collective-permute-done | bytes 262176 | tf_op jit(solution)/shard_map/send_Zb/ppermute | solution.py:263
  12.9 1.5 %collective-permute-start.5 = (bf16[512,256]{1,0:T(8,128)(2,1)S(1)}, bf16[512,256]{1,0:T(8,128)(2,1)S(1)}, u32[]{:S(2)}, u32[]{:S(2)}) collective-permute-start(bf16[512,256]{1,0:T(8,128)(2,1)S(1)} %collective-permute-done.1.refs_1_), channel_id=1, source_target_pairs={{0,1},{1,0},{2,3},{3,2},{4,5},{5,4},{6,7},{7,6},{8,9},{9,8},{10,11... | collective-permute-start | bytes 786440 | tf_op jit(solution)/shard_map/send_Sb/ppermute | solution.py:263
  14.4 2.5 %collective-permute-done.on_even = bf16[512,256]{1,0:T(8,128)(2,1)S(1)} collective-permute-done((bf16[512,256]{1,0:T(8,128)(2,1)S(1)}, bf16[512,256]{1,0:T(8,128)(2,1)S(1)}, u32[]{:S(2)}, u32[]{:S(2)}) %collective-permute-start) | collective-permute-done | bytes 262176 | tf_op jit(solution)/shard_map/send_Db/ppermute | solution.py:263
  16.9 1.8 %collective-permute-start.3 = (bf16[512,256]{1,0:T(8,128)(2,1)S(1)}, bf16[512,256]{1,0:T(8,128)(2,1)S(1)}, u32[]{:S(2)}, u32[]{:S(2)}) collective-permute-start(bf16[512,256]{1,0:T(8,128)(2,1)S(1)} %get-tuple-element.62.on_odd.refs_3_), channel_id=1, source_target_pairs={{0,6},{1,7},{2,0},{3,1},{4,2},{5,3},{6,4},{7,5},{8,14},{9,15},{10,... | collective-permute-start | bytes 786440 | tf_op jit(solution)/shard_map/send_Z1/ppermute | solution.py:263
  18.7 0.3 collective-permute-done.4.on_even.refs_1_
  19.0 1.7 %collective-permute-done.5.on_odd.refs_2_ = bf16[512,256]{1,0:T(8,128)(2,1)S(1)} collective-permute-done((bf16[512,256]{1,0:T(8,128)(2,1)S(1)}, bf16[512,256]{1,0:T(8,128)(2,1)S(1)}, u32[]{:S(2)}, u32[]{:S(2)}) %collective-permute-start.5) | collective-permute-done | bytes 262176 | tf_op jit(solution)/shard_map/send_Sb/ppermute | solution.py:263
  20.8 1.5 %collective-permute-start.8 = (bf16[512,256]{1,0:T(8,128)(2,1)S(1)}, bf16[512,256]{1,0:T(8,128)(2,1)S(1)}, u32[]{:S(2)}, u32[]{:S(2)}) collective-permute-start(bf16[512,256]{1,0:T(8,128)(2,1)S(1)} %collective-permute-done.4.on_even.refs_1_), channel_id=1, source_target_pairs={{0,1},{1,0},{2,3},{3,2},{4,5},{5,4},{6,7},{7,6},{8,9},{9,8},{10,11... | collective-permute-start | bytes 786440 | tf_op jit(solution)/shard_map/send_Sc/ppermute | solution.py:263
  22.3 3.0 %collective-permute-start.2 = (bf16[512,256]{1,0:T(8,128)(2,1)S(1)}, bf16[512,256]{1,0:T(8,128)(2,1)S(1)}, u32[]{:S(2)}, u32[]{:S(2)}) collective-permute-start(bf16[512,256]{1,0:T(8,128)(2,1)S(1)} %get-tuple-element.60.on_odd.refs_0_), channel_id=1, source_target_pairs={{0,6},{1,7},{2,0},{3,1},{4,2},{5,3},{6,4},{7,5},{8,14},{9,15},{10,... | collective-permute-start | bytes 786440 | tf_op jit(solution)/shard_map/send_Z2/ppermute | solution.py:263
  25.3 0.0 collective-permute-done.3.on_even.refs_5_
  25.4 0.8 %collective-permute-start.6 = (bf16[512,256]{1,0:T(8,128)(2,1)S(1)}, bf16[512,256]{1,0:T(8,128)(2,1)S(1)}, u32[]{:S(2)}, u32[]{:S(2)}) collective-permute-start(bf16[512,256]{1,0:T(8,128)(2,1)S(1)} %choose.6), channel_id=1, source_target_pairs={{0,1},{1,0},{2,3},{3,2},{4,5},{5,4},{6,7},{7,6},{8,9},{9,8},{10,11... | collective-permute-start | bytes 786440 | tf_op jit(solution)/shard_map/send_Y1/ppermute | solution.py:263
  26.2 3.8 %collective-permute-done.8.refs_2_ = bf16[512,256]{1,0:T(8,128)(2,1)S(1)} collective-permute-done((bf16[512,256]{1,0:T(8,128)(2,1)S(1)}, bf16[512,256]{1,0:T(8,128)(2,1)S(1)}, u32[]{:S(2)}, u32[]{:S(2)}) %collective-permute-start.8) | collective-permute-done | bytes 262176 | tf_op jit(solution)/shard_map/send_Sc/ppermute | solution.py:263
  30.0 2.1 %collective-permute-start.9 = (bf16[512,256]{1,0:T(8,128)(2,1)S(1)}, bf16[512,256]{1,0:T(8,128)(2,1)S(1)}, u32[]{:S(2)}, u32[]{:S(2)}) collective-permute-start(bf16[512,256]{1,0:T(8,128)(2,1)S(1)} %choose.7), channel_id=1, source_target_pairs={{0,6},{1,7},{2,0},{3,1},{4,2},{5,3},{6,4},{7,5},{8,14},{9,15},{10,... | collective-permute-start | bytes 786440 | tf_op jit(solution)/shard_map/send_X/ppermute | solution.py:263
  32.1 0.0 copy-done
  32.1 0.0 collective-permute-start.10
  32.1 0.0 collective-permute-done.2.on_even.refs_2_
  32.1 0.8 %collective-permute-done.6.refs_4_ = bf16[512,256]{1,0:T(8,128)(2,1)S(1)} collective-permute-done((bf16[512,256]{1,0:T(8,128)(2,1)S(1)}, bf16[512,256]{1,0:T(8,128)(2,1)S(1)}, u32[]{:S(2)}, u32[]{:S(2)}) %collective-permute-start.6) | collective-permute-done | bytes 262176 | tf_op jit(solution)/shard_map/send_Y1/ppermute | solution.py:263
  33.0 0.0 collective-permute-done.7.refs_1_
  33.0 3.4 %collective-permute-done.9.on_even.on_odd = bf16[512,256]{1,0:T(8,128)(2,1)S(1)} collective-permute-done((bf16[512,256]{1,0:T(8,128)(2,1)S(1)}, bf16[512,256]{1,0:T(8,128)(2,1)S(1)}, u32[]{:S(2)}, u32[]{:S(2)}) %collective-permute-start.9) | collective-permute-done | bytes 262176 | tf_op jit(solution)/shard_map/send_X/ppermute | solution.py:263
  36.4 0.0 collective-permute-start.11
  36.4 1.5 %collective-permute-start.12 = (bf16[512,256]{1,0:T(8,128)(2,1)S(1)}, bf16[512,256]{1,0:T(8,128)(2,1)S(1)}, u32[]{:S(2)}, u32[]{:S(2)}) collective-permute-start(bf16[512,256]{1,0:T(8,128)(2,1)S(1)} %choose.5), channel_id=1, source_target_pairs={{0,1},{1,0},{2,3},{3,2},{4,5},{5,4},{6,7},{7,6},{8,9},{9,8},{10,11... | collective-permute-start | bytes 786440 | tf_op jit(solution)/shard_map/send_Y2/ppermute | solution.py:263
  37.9 3.5 %collective-permute-start.15 = (bf16[512,256]{1,0:T(8,128)(2,1)S(1)}, bf16[512,256]{1,0:T(8,128)(2,1)S(1)}, u32[]{:S(2)}, u32[]{:S(2)}) collective-permute-start(bf16[512,256]{1,0:T(8,128)(2,1)S(1)} %collective-permute-done.6.refs_4_), channel_id=1, source_target_pairs={{0,6},{1,7},{2,0},{3,1},{4,2},{5,3},{6,4},{7,5},{8,14},{9,15},{10,... | collective-permute-start | bytes 786440 | tf_op jit(solution)/shard_map/send_W1/ppermute | solution.py:263
  41.5 0.0 collective-permute-done.10.refs_2_
  41.5 0.0 collective-permute-done.11.refs_3_
  41.5 1.1 %stack_rows.1.left = bf16[1024,2048]{1,0:T(8,128)(2,1)S(1)} custom-call(s32[4,8]{1,0:T(4,128)} %all_flags.5, bf16[256,2048]{1,0:T(8,128)(2,1)S(1)} %copy-done, bf16[256,2048]{1,0:T(8,128)(2,1)S(1)} %collective-permute-done.7.refs_1_, bf16[256,2048]{1,0:T(8,128)(2,1)S(1)} %collective-permute-done.10.refs_2_, bf16[256,2048]{1,0:T(8,128)(2,1)S(1)} %collective-permute-done.11.refs_3_), custom_call_target="tpu_custom_call" | custom-call | bytes 4194368 | tf_op jit(solution)/shard_map/stack_rows/pallas_call | solution.py:25
  42.7 0.8 %collective-permute-start.14 = (bf16[512,256]{1,0:T(8,128)(2,1)S(1)}, bf16[512,256]{1,0:T(8,128)(2,1)S(1)}, u32[]{:S(2)}, u32[]{:S(2)}) collective-permute-start(bf16[512,256]{1,0:T(8,128)(2,1)S(1)} %choose.8), channel_id=1, source_target_pairs={{0,1},{1,0},{2,3},{3,2},{4,5},{5,4},{6,7},{7,6},{8,9},{9,8},{10,11... | collective-permute-start | bytes 786440 | tf_op jit(solution)/shard_map/send_Q/ppermute | solution.py:263
  43.5 1.8 %sum_first.1.refs_2_ = bf16[1024,256]{1,0:T(8,128)(2,1)S(1)} custom-call(bf16[1024,2048]{1,0:T(8,128)(2,1)S(1)} %stack_rows.1.left, bf16[512,256]{1,0:T(8,128)(2,1)S(1)} %mask_tile.2.refs_0_, bf16[512,256]{1,0:T(8,128)(2,1)S(1)} %collective-permute-done.1.refs_1_, bf16[512,256]{1,0:T(8,128)(2,1)S(1)} %collective-permute-done.5.on_odd.refs_2_, ...), custom_call_target="tpu_custom_call" | custom-call | flops 1073741824 | bytes 5242880 | tf_op jit(solution)/shard_map/sum_first/pallas_call | solution.py:25
  45.4 0.0 collective-permute-done.12.refs_1_
  45.4 4.0 %collective-permute-start.13 = (bf16[512,256]{1,0:T(8,128)(2,1)S(1)}, bf16[512,256]{1,0:T(8,128)(2,1)S(1)}, u32[]{:S(2)}, u32[]{:S(2)}) collective-permute-start(bf16[512,256]{1,0:T(8,128)(2,1)S(1)} %collective-permute-done.12.refs_1_), channel_id=1, source_target_pairs={{0,6},{1,7},{2,0},{3,1},{4,2},{5,3},{6,4},{7,5},{8,14},{9,15},{10,... | collective-permute-start | bytes 786440 | tf_op jit(solution)/shard_map/send_W2/ppermute | solution.py:263
  49.4 1.5 %sum_partial2.1.refs_1_ = f32[1024,256]{1,0:T(8,128)S(1)} custom-call(bf16[1024,2048]{1,0:T(8,128)(2,1)S(1)} %stack_rows.1.left, bf16[512,256]{1,0:T(8,128)(2,1)S(1)} %get-tuple-element.60.on_odd.refs_0_, bf16[512,256]{1,0:T(8,128)(2,1)S(1)} %collective-permute-done.12.refs_1_, bf16[512,256]{1,0:T(8,128)(2,1)S(1)} %collective-permute-done.2.on_even.refs_2_), custom_call_target="tpu_custom_call" | custom-call | flops 805306368 | bytes 4980736 | tf_op jit(solution)/shard_map/sum_partial2/pallas_call | solution.py:25
  50.8 2.3 %sum_partial.1.refs_2_ = f32[1024,512]{1,0:T(8,128)S(1)} custom-call(bf16[1024,2048]{1,0:T(8,128)(2,1)S(1)} %stack_rows.1.left, bf16[512,256]{1,0:T(8,128)(2,1)S(1)} %get-tuple-element.64.on_odd.refs_0_, bf16[512,256]{1,0:T(8,128)(2,1)S(1)} %collective-permute-done.4.on_even.refs_1_, bf16[512,256]{1,0:T(8,128)(2,1)S(1)} %collective-permute-done.8.refs_2_, ...), custom_call_target="tpu_custom_call" | custom-call | flops 1610612736 | bytes 5767168 | tf_op jit(solution)/shard_map/sum_partial/pallas_call | solution.py:25
  53.1 0.0 collective-permute-done.15.refs_1_
  53.2 0.0 collective-permute-done.14.refs_0_
  53.2 1.3 %sum_middle.1.refs_3_ = bf16[1024,512]{1,0:T(8,128)(2,1)S(1)} custom-call(bf16[1024,2048]{1,0:T(8,128)(2,1)S(1)} %stack_rows.1.left, bf16[512,256]{1,0:T(8,128)(2,1)S(1)} %collective-permute-done.14.refs_0_, bf16[512,256]{1,0:T(8,128)(2,1)S(1)} %collective-permute-done.15.refs_1_, f32[1024,512]{1,0:T(8,128)S(1)} %sum_partial.1.refs_2_), custom_call_target="tpu_custom_call" | custom-call | flops 536870912 | bytes 5767168 | tf_op jit(solution)/shard_map/sum_middle/pallas_call | solution.py:25
  54.4 0.0 collective-permute-done.13.refs_0_
  54.5 1.6 %sum_last.1 = bf16[1024,1024]{1,0:T(8,128)(2,1)} custom-call(bf16[1024,2048]{1,0:T(8,128)(2,1)S(1)} %stack_rows.1.left, bf16[512,256]{1,0:T(8,128)(2,1)S(1)} %collective-permute-done.13.refs_0_, f32[1024,256]{1,0:T(8,128)S(1)} %sum_partial2.1.refs_1_, bf16[1024,256]{1,0:T(8,128)(2,1)S(1)} %sum_first.1.refs_2_, bf16[1024,512]{1,0:T(8,128)(2,1)S(1)} %sum_middle.1.refs_3_), custom_call_target="tpu_custom_call" | custom-call | flops 268435456 | bytes 6553600 | tf_op jit(solution)/shard_map/sum_last/pallas_call | solution.py:25
  (5 shorter events, 0.1 us)
Async XLA Ops:
  0.0 32.1 %copy-start = (bf16[256,2048]{1,0:T(8,128)(2,1)S(1)}, bf16[256,2048]{1,0:T(8,128)(2,1)}, u32[]{:S(2)}) copy-start(bf16[256,2048]{1,0:T(8,128)(2,1)} %refs_0_.1) | copy-start | bytes 3145732
  1.1 11.8 %collective-permute-start.1 = (bf16[512,256]{1,0:T(8,128)(2,1)S(1)}, bf16[512,256]{1,0:T(8,128)(2,1)S(1)}, u32[]{:S(2)}, u32[]{:S(2)}) collective-permute-start(bf16[512,256]{1,0:T(8,128)(2,1)S(1)} %mask_tile.2.refs_0_), channel_id=1, source_target_pairs={{0,6},{1,7},{2,0},{3,1},{4,2},{5,3},{6,4},{7,5},{8,14},{9,15},{10,... | collective-permute-start | bytes 786440 | tf_op jit(solution)/shard_map/send_Zb/ppermute | solution.py:263
  6.2 26.8 %collective-permute-start.7 = (bf16[256,2048]{1,0:T(8,128)(2,1)}, bf16[256,2048]{1,0:T(8,128)(2,1)S(1)}, u32[]{:S(2)}, u32[]{:S(2)}) collective-permute-start(bf16[256,2048]{1,0:T(8,128)(2,1)} %refs_0_.1), channel_id=1, source_target_pairs={{0,16},{8,24},{16,0},{24,8},{1,17},{9,25},{17,1},{25,9},{2,18},{10... | collective-permute-start | bytes 3145736 | tf_op jit(solution)/shard_map/send_Ax/ppermute | solution.py:263
  7.7 9.2 %collective-permute-start = (bf16[512,256]{1,0:T(8,128)(2,1)S(1)}, bf16[512,256]{1,0:T(8,128)(2,1)S(1)}, u32[]{:S(2)}, u32[]{:S(2)}) collective-permute-start(bf16[512,256]{1,0:T(8,128)(2,1)S(1)} %mask_tile.2.refs_0_), channel_id=1, source_target_pairs={{0,1},{1,0},{2,3},{3,2},{4,5},{5,4},{6,7},{7,6},{8,9},{9,8},{10,11... | collective-permute-start | bytes 786440 | tf_op jit(solution)/shard_map/send_Db/ppermute | solution.py:263
  10.3 8.7 %collective-permute-start.4 = (bf16[512,256]{1,0:T(8,128)(2,1)S(1)}, bf16[512,256]{1,0:T(8,128)(2,1)S(1)}, u32[]{:S(2)}, u32[]{:S(2)}) collective-permute-start(bf16[512,256]{1,0:T(8,128)(2,1)S(1)} %get-tuple-element.64.on_odd.refs_0_), channel_id=1, source_target_pairs={{0,6},{1,7},{2,0},{3,1},{4,2},{5,3},{6,4},{7,5},{8,14},{9,15},{10,... | collective-permute-start | bytes 786440 | tf_op jit(solution)/shard_map/send_Zc/ppermute | solution.py:263
  12.9 7.9 %collective-permute-start.5 = (bf16[512,256]{1,0:T(8,128)(2,1)S(1)}, bf16[512,256]{1,0:T(8,128)(2,1)S(1)}, u32[]{:S(2)}, u32[]{:S(2)}) collective-permute-start(bf16[512,256]{1,0:T(8,128)(2,1)S(1)} %collective-permute-done.1.refs_1_), channel_id=1, source_target_pairs={{0,1},{1,0},{2,3},{3,2},{4,5},{5,4},{6,7},{7,6},{8,9},{9,8},{10,11... | collective-permute-start | bytes 786440 | tf_op jit(solution)/shard_map/send_Sb/ppermute | solution.py:263
  16.9 8.4 %collective-permute-start.3 = (bf16[512,256]{1,0:T(8,128)(2,1)S(1)}, bf16[512,256]{1,0:T(8,128)(2,1)S(1)}, u32[]{:S(2)}, u32[]{:S(2)}) collective-permute-start(bf16[512,256]{1,0:T(8,128)(2,1)S(1)} %get-tuple-element.62.on_odd.refs_3_), channel_id=1, source_target_pairs={{0,6},{1,7},{2,0},{3,1},{4,2},{5,3},{6,4},{7,5},{8,14},{9,15},{10,... | collective-permute-start | bytes 786440 | tf_op jit(solution)/shard_map/send_Z1/ppermute | solution.py:263
  20.8 9.2 %collective-permute-start.8 = (bf16[512,256]{1,0:T(8,128)(2,1)S(1)}, bf16[512,256]{1,0:T(8,128)(2,1)S(1)}, u32[]{:S(2)}, u32[]{:S(2)}) collective-permute-start(bf16[512,256]{1,0:T(8,128)(2,1)S(1)} %collective-permute-done.4.on_even.refs_1_), channel_id=1, source_target_pairs={{0,1},{1,0},{2,3},{3,2},{4,5},{5,4},{6,7},{7,6},{8,9},{9,8},{10,11... | collective-permute-start | bytes 786440 | tf_op jit(solution)/shard_map/send_Sc/ppermute | solution.py:263
  22.3 9.8 %collective-permute-start.2 = (bf16[512,256]{1,0:T(8,128)(2,1)S(1)}, bf16[512,256]{1,0:T(8,128)(2,1)S(1)}, u32[]{:S(2)}, u32[]{:S(2)}) collective-permute-start(bf16[512,256]{1,0:T(8,128)(2,1)S(1)} %get-tuple-element.60.on_odd.refs_0_), channel_id=1, source_target_pairs={{0,6},{1,7},{2,0},{3,1},{4,2},{5,3},{6,4},{7,5},{8,14},{9,15},{10,... | collective-permute-start | bytes 786440 | tf_op jit(solution)/shard_map/send_Z2/ppermute | solution.py:263
  25.4 7.6 %collective-permute-start.6 = (bf16[512,256]{1,0:T(8,128)(2,1)S(1)}, bf16[512,256]{1,0:T(8,128)(2,1)S(1)}, u32[]{:S(2)}, u32[]{:S(2)}) collective-permute-start(bf16[512,256]{1,0:T(8,128)(2,1)S(1)} %choose.6), channel_id=1, source_target_pairs={{0,1},{1,0},{2,3},{3,2},{4,5},{5,4},{6,7},{7,6},{8,9},{9,8},{10,11... | collective-permute-start | bytes 786440 | tf_op jit(solution)/shard_map/send_Y1/ppermute | solution.py:263
  30.0 6.4 %collective-permute-start.9 = (bf16[512,256]{1,0:T(8,128)(2,1)S(1)}, bf16[512,256]{1,0:T(8,128)(2,1)S(1)}, u32[]{:S(2)}, u32[]{:S(2)}) collective-permute-start(bf16[512,256]{1,0:T(8,128)(2,1)S(1)} %choose.7), channel_id=1, source_target_pairs={{0,6},{1,7},{2,0},{3,1},{4,2},{5,3},{6,4},{7,5},{8,14},{9,15},{10,... | collective-permute-start | bytes 786440 | tf_op jit(solution)/shard_map/send_X/ppermute | solution.py:263
  32.1 9.4 %collective-permute-start.10 = (bf16[256,2048]{1,0:T(8,128)(2,1)S(1)}, bf16[256,2048]{1,0:T(8,128)(2,1)S(1)}, u32[]{:S(2)}, u32[]{:S(2)}) collective-permute-start(bf16[256,2048]{1,0:T(8,128)(2,1)S(1)} %copy-done), channel_id=1, source_target_pairs={{0,8},{8,0},{16,24},{24,16},{1,9},{9,1},{17,25},{25,17},{2,10},{10... | collective-permute-start | bytes 3145736 | tf_op jit(solution)/shard_map/send_Af/ppermute | solution.py:263
  36.4 5.1 %collective-permute-start.11 = (bf16[256,2048]{1,0:T(8,128)(2,1)S(1)}, bf16[256,2048]{1,0:T(8,128)(2,1)S(1)}, u32[]{:S(2)}, u32[]{:S(2)}) collective-permute-start(bf16[256,2048]{1,0:T(8,128)(2,1)S(1)} %collective-permute-done.7.refs_1_), channel_id=1, source_target_pairs={{0,8},{8,0},{16,24},{24,16},{1,9},{9,1},{17,25},{25,17},{2,10},{10... | collective-permute-start | bytes 3145736 | tf_op jit(solution)/shard_map/send_Ar/ppermute | solution.py:263
  36.4 9.0 %collective-permute-start.12 = (bf16[512,256]{1,0:T(8,128)(2,1)S(1)}, bf16[512,256]{1,0:T(8,128)(2,1)S(1)}, u32[]{:S(2)}, u32[]{:S(2)}) collective-permute-start(bf16[512,256]{1,0:T(8,128)(2,1)S(1)} %choose.5), channel_id=1, source_target_pairs={{0,1},{1,0},{2,3},{3,2},{4,5},{5,4},{6,7},{7,6},{8,9},{9,8},{10,11... | collective-permute-start | bytes 786440 | tf_op jit(solution)/shard_map/send_Y2/ppermute | solution.py:263
  37.9 15.2 %collective-permute-start.15 = (bf16[512,256]{1,0:T(8,128)(2,1)S(1)}, bf16[512,256]{1,0:T(8,128)(2,1)S(1)}, u32[]{:S(2)}, u32[]{:S(2)}) collective-permute-start(bf16[512,256]{1,0:T(8,128)(2,1)S(1)} %collective-permute-done.6.refs_4_), channel_id=1, source_target_pairs={{0,6},{1,7},{2,0},{3,1},{4,2},{5,3},{6,4},{7,5},{8,14},{9,15},{10,... | collective-permute-start | bytes 786440 | tf_op jit(solution)/shard_map/send_W1/ppermute | solution.py:263
  42.7 10.5 %collective-permute-start.14 = (bf16[512,256]{1,0:T(8,128)(2,1)S(1)}, bf16[512,256]{1,0:T(8,128)(2,1)S(1)}, u32[]{:S(2)}, u32[]{:S(2)}) collective-permute-start(bf16[512,256]{1,0:T(8,128)(2,1)S(1)} %choose.8), channel_id=1, source_target_pairs={{0,1},{1,0},{2,3},{3,2},{4,5},{5,4},{6,7},{7,6},{8,9},{9,8},{10,11... | collective-permute-start | bytes 786440 | tf_op jit(solution)/shard_map/send_Q/ppermute | solution.py:263
  45.4 9.1 %collective-permute-start.13 = (bf16[512,256]{1,0:T(8,128)(2,1)S(1)}, bf16[512,256]{1,0:T(8,128)(2,1)S(1)}, u32[]{:S(2)}, u32[]{:S(2)}) collective-permute-start(bf16[512,256]{1,0:T(8,128)(2,1)S(1)} %collective-permute-done.12.refs_1_), channel_id=1, source_target_pairs={{0,6},{1,7},{2,0},{3,1},{4,2},{5,3},{6,4},{7,5},{8,14},{9,15},{10,... | collective-permute-start | bytes 786440 | tf_op jit(solution)/shard_map/send_W2/ppermute | solution.py:263

commit v5 on v4

--- a/solution.py
+++ b/solution.py
@@ -14,6 +14,20 @@
 ANY = pl.ANY
 HBM = pltpu.MemorySpace.HBM
 VMEM = pltpu.MemorySpace.VMEM
+
+
+COST = {
+    "choose_b": 12000000000,
+    "mask_tile_1": 12000000000,
+    "mask_tile_2": 0,
+    "sum_last": 3000000000,
+    "choose_Y12": 0,
+    "choose_X": 1000000000,
+    "choose_Q": 6000000000,
+    "stack_rows": 12000000000,
+    "sum_partial": 6000000000,
+    "sum_first": 12000000000,
+}
 
 
 def pinned(value, space=VMEM):
@@ -28,40 +42,39 @@
         in_specs=[pl.BlockSpec(memory_space=space) for space in spaces],
         out_specs=jax.tree.map(lambda _: pl.BlockSpec(memory_space=out_space), out_shape),
         scratch_shapes=list(scratch),
-        cost_estimate=pl.CostEstimate(flops=flops, bytes_accessed=moved, transcendentals=0),
+        cost_estimate=pl.CostEstimate(flops=COST.get(name, flops), bytes_accessed=moved, transcendentals=0),
         compiler_params=pltpu.CompilerParams(vmem_limit_bytes=8 << 20),
         name=name,
     )(*operands)
 
 
-def mask_tile_kernel(first, all_flags, tile, *refs):
+def mask_tile_kernel(spans, all_flags, tile, *refs):
     *outs, flags, flag_sem, sem = refs
-    width = outs[0].shape[1]
     flag_copy = pltpu.make_async_copy(all_flags, flags, flag_sem)
     flag_copy.start()
     copies = [
-        pltpu.make_async_copy(tile.at[:, (first + n) * width : (first + n + 1) * width], out, sem.at[n])
-        for n, out in enumerate(outs)
+        pltpu.make_async_copy(tile.at[:, start : start + width], out, sem.at[n])
+        for n, ((start, width), out) in enumerate(zip(spans, outs))
     ]
     for copy in copies:
         copy.start()
     flag_copy.wait()
-    for n, (copy, out) in enumerate(zip(copies, outs)):
+    for (start, width), copy, out in zip(spans, copies, outs):
         copy.wait()
         for row in range(0, out.shape[0], BS):
             for column in range(0, width, BS):
 
-                @pl.when(flags[row // BS, ((first + n) * width + column) // BS] == 0)
+                @pl.when(flags[row // BS, (start + column) // BS] == 0)
                 def _():
                     out[row : row + BS, column : column + BS] = jnp.zeros((BS, BS), out.dtype)
 
 
-def mask_tile(tile, flags, first, count):
-    shape = (tile.shape[0], tile.shape[1] // PIECES)
-    return kernel_call(
-        functools.partial(mask_tile_kernel, first),
-        "mask_tile",
-        [VMEM(shape, tile.dtype)] * count,
+def mask_tile(tile, flags, spans):
+    count = len(spans)
+    return kernel_call(
+        functools.partial(mask_tile_kernel, spans),
+        "mask_tile_%d" % len(spans),
+        [VMEM((tile.shape[0], width), tile.dtype) for _, width in spans],
         [pinned(flags, HBM), pinned(tile, HBM)],
         [HBM, HBM],
         VMEM,
@@ -81,10 +94,10 @@
         out[...] = on_odd[...]
 
 
-def choose(on_even, on_odd):
+def choose(name, on_even, on_odd):
     return kernel_call(
         choose_kernel,
-        "choose",
+        "choose_" + name,
         VMEM(on_even.shape, on_even.dtype),
         [pinned(on_even), pinned(on_odd)],
         [VMEM, VMEM],
@@ -136,10 +149,12 @@
 
 
 def sums(left, tiles, places, partial, rows, store):
-    depth, width = tiles[0].shape
+    depth = tiles[0].shape[0]
     odd = lax.axis_index("col") % 2
-    for place, terms in enumerate(places):
-        columns = slice(place * width, (place + 1) * width)
+    first = 0
+    for terms in places:
+        columns = slice(first, first + tiles[terms[0][0]].shape[1])
+        first = columns.stop
         total = None if partial is None else partial[rows, columns]
         for number, on_even, on_odd in terms:
             start = on_even * depth
@@ -222,23 +237,23 @@
 
 def add_products(name, left, places, partial=None, dtype=jnp.float32):
     tiles, numbered = number_terms(places)
-    rows, width = left.shape[0], tiles[0].shape[1]
+    rows, columns = left.shape[0], sum(terms[0][0].shape[1] for terms in places)
     operands = [pinned(x) for x in (left, *tiles, *([] if partial is None else [partial]))]
     return kernel_call(
         functools.partial(sum_kernel, (numbered, len(tiles), partial is not None)),
         "sum_" + name,
-        VMEM((rows, width * len(places)), dtype),
+        VMEM((rows, columns), dtype),
         operands,
         [VMEM] * len(operands),
         VMEM,
-        flops=2 * rows * tiles[0].size * sum(len(terms) for terms in places),
+        flops=2 * rows * sum(tile.size for terms in places for tile, _, _ in terms),
     )
 
 
 def finish_product(left, places, column, width, partial, ready):
     tiles, numbered = number_terms(places)
     rows = left.shape[0]
-    columns = tiles[0].shape[1] * len(places)
+    columns = sum(terms[0][0].shape[1] for terms in places)
     chunk, count = chunks_of(left)
     operands = [pinned(x) for x in (left, *tiles, partial, *[block for block, _ in ready])]
     plan = (numbered, len(tiles), tuple(start for _, start in ready), column)
@@ -254,7 +269,7 @@
             pltpu.SemaphoreType.DMA((count,)),
             pltpu.SemaphoreType.DMA((len(ready),)),
         ],
-        flops=2 * rows * tiles[0].size * len(places),
+        flops=2 * rows * sum(tile.size for terms in places for tile, _, _ in terms),
     )
 
 
@@ -271,24 +286,15 @@
 
 
 HELD = {
-    "Ax": ["own_b"],
-    "Z1": ["Db", "own_b"],
-    "Z2": ["Db", "Zb"],
-    "Af": ["Zb", "Z1", "own_c"],
-    "Y1": ["own_b", "Sb", "Zb"],
-    "X": ["own_c", "own_b", "Sc"],
-    "Y2": ["Zb", "Sb", "Y1", "Z2", "Ax", "Z1", "Zc", "Db", "Sc"],
-    "W1": ["Y1"],
-    "Q": ["Z2", "Db", "X"],
-    "Ar": ["X", "Sb", "Zc", "own_b", "Ax", "Sc"],
-    "first": ["X", "Sc", "Af", "Z2", "Z1"],
-    "last": ["Sc", "Db"],
-    "partial": ["X", "Ax", "Db", "own_b", "Z1"],
-    "partial2": ["Z1"],
-    "middle": ["Y2", "Sb", "Af"],
-    "W2": ["Y2", "first", "X"],
-    "Sc": ["Sb", "Zc", "own_c"],
-    "Sb": ["own_c"],
+    "Sb": ["Db", "Zb", "own_c"],
+    "Zc": ["Sb"],
+    "Q": ["Y12", "Ar", "own_c", "X", "own_b"],
+    "Ar": ["Z12", "Zb"],
+    "last": ["Zc", "first", "Af", "Db", "Ar", "Zb", "Z12", "Sc", "Q"],
+    "first": ["own_c", "X", "Af"],
+    "partial": ["Db", "own_b", "Ar", "Sc"],
+    "X": ["Z12"],
+    "Y12": ["Sb"],
 }
 
 
@@ -315,13 +321,14 @@
     def value(name):
         return got[name][0]
 
-    (own_b,) = mask_tile(b_tiles, mask_b, 0, 1)
+    piece = width // PIECES
+    (own_b,) = mask_tile(b_tiles, mask_b, ((0, piece),))
     got["own_b"] = [own_b]
     by_two("Zb", own_b)
     across("Db", own_b)
-    own_c, own_1, own_2 = mask_tile(tied(b_tiles, [own_b]), mask_b, 1, 3)
+    own_c, own_12 = mask_tile(tied(b_tiles, [own_b]), mask_b, ((piece, piece), (2 * piece, 2 * piece)))
     got["own_c"] = [own_c]
-    by_two("Zc", own_c)
+    by_two("Z12", own_12)
     mine = a_window
 
     lefts, offsets = [mine], [(0, False)]
@@ -330,13 +337,11 @@
         got["Ax"] = got[f"Ax{distance}"]
         offsets.append((distance, False))
     across("Sb", value("Zb"))
-    by_two("Z1", own_1)
+    send("Af", mine, "row", lambda i: i ^ 1)
+    by_two("Zc", own_c)
+    across("Y12", choose("Y12", value("Z12"), own_12))
+    by_two("X", choose("X", value("Zc"), value("Sb")))
     across("Sc", value("Zc"))
-    by_two("Z2", own_2)
-    send("Af", mine, "row", lambda i: i ^ 1)
-    across("Y1", choose(value("Z1"), own_1))
-    by_two("X", choose(value("Zc"), value("Sb")))
-    across("Y2", choose(value("Z2"), own_2))
     for distance in range(2, count, 2):
         send("Ar", value(f"Ax{distance}"), "row", lambda i: i ^ 1, f"Ar{distance}")
         got["Ar"] = got[f"Ar{distance}"]
@@ -344,32 +349,21 @@
     lefts += [value("Af")] + [value(f"Ar{distance}") for distance in range(2, count, 2)]
     offsets += [(distance, True) for distance, _ in offsets]
     left = stack_rows(lefts, tuple(offsets), mask_a)
-    by_two("W1", value("Y1"))
+    column_b = [(own_b, 0, 0), (value("Zb"), 2, 2), (value("Sb"), 3, 1), (choose("b", value("Db"), value("X")), 1, 3)]
+    got["first"] = [add_products("first", held("first", left), [column_b], dtype=left.dtype)]
+    by_two("W12", value("Y12"))
+    across("Q", choose("Q", value("X"), own_c))
+
+    column_12 = [(own_12, 0, 0), (value("Y12"), 1, 1), (value("Z12"), 2, 2)]
     column_c = [(own_c, 0, 0), (value("Zc"), 2, 2), (value("Sc"), 3, 1)]
-    column_1 = [(own_1, 0, 0), (value("Y1"), 1, 1), (value("Z1"), 2, 2)]
-    got["partial"] = [add_products("partial", held("partial", left), [column_c, column_1])]
-    column_2 = [(own_2, 0, 0), (value("Y2"), 1, 1), (value("Z2"), 2, 2)]
-    got["partial2"] = [add_products("partial2", held("partial2", left), [column_2])]
-    across("Q", choose(value("X"), own_c))
-    column_b = [(own_b, 0, 0), (value("Zb"), 2, 2), (value("Sb"), 3, 1), (choose(value("Db"), value("X")), 1, 3)]
-    got["first"] = [add_products("first", held("first", left), [column_b], dtype=left.dtype)]
-    by_two("W2", value("Y2"))
-
-    piece = width // PIECES
-    middle = add_products(
-        "middle",
-        held("middle", left),
-        [[(value("Q"), 1, 3)], [(value("W1"), 3, 3)]],
-        partial=value("partial"),
-        dtype=left.dtype,
-    )
+    got["partial"] = [add_products("partial", held("partial", left), [column_c, column_12])]
     return finish_product(
         held("last", left),
-        [[(value("W2"), 3, 3)]],
-        3 * piece,
+        [[(value("Q"), 1, 3)], [(value("W12"), 3, 3)]],
+        piece,
         width,
-        value("partial2"),
-        [(value("first"), 0), (middle, piece)],
+        value("partial"),
+        [(value("first"), 0)],
     )
 
 

time: 56.2 us -> 53.4 us (0.950)
  Pallas kernels: 12 us -> 10.7 us
  starting transfers between devices: 29.2 us -> 27.9 us
    ppermute x16 -> x13, starting transfers between devices: 29.2 us -> 27.9 us  [moved(): lax.ppermute(block, axis, [(i, target(i) % count) for i in range(count)])]
    pallas_call x13 -> x10, Pallas kernels: 12 us -> 10.7 us  [kernel_call(): pl.pallas_call(kernel, out_shape=out_shape, in_specs=[pl.BlockSpec(memory...]
    ppermute x16 -> x13, waiting for transfers between devices: 14.8 us -> 14.5 us  [moved(): lax.ppermute(block, axis, [(i, target(i) % count) for i in range(count)])]
  transfers between devices with their start and end apart: 16 -> 13, of which waited for: 7 -> 6; matrix products, arithmetic and copies ran while one was open for 0% -> 0% of each run, Pallas kernels for 17% -> 14%
where the time goes in v5:
time: 53.4 us; the launch traced here: 53.2 us
  starting transfers between devices  27.9 us (52%)
  waiting for transfers between devices  14.5 us (27%)
  Pallas kernels  10.7 us (20%)
    ppermute x13, starting transfers between devices, moved(): lax.ppermute(block, axis, [(i, target(i) % count) for i in range(count)])  27.9 us
    ppermute x13, waiting for transfers between devices, moved(): lax.ppermute(block, axis, [(i, target(i) % count) for i in range(count)])  14.5 us
    pallas_call x10, Pallas kernels, kernel_call(): pl.pallas_call(kernel, out_shape=out_shape, in_specs=[pl.BlockSpec(memory...  10.7 us
  transfers between devices with their start and end apart: 13, of which 6 were waited for; matrix products, arithmetic and copies ran while one was open for 0% of the time, Pallas kernels for 14%

profile of v5, /device:TPU:0, one launch (start us, length us, event | category | flops | bytes accessed | tf_op | source)
XLA Modules:
  0.0 53.2 jit_solution(832187349177987312)
XLA Ops:
  0.0 0.0 copy-start
  0.0 1.1 %mask_tile_1.1.refs_0_ = bf16[512,256]{1,0:T(8,128)(2,1)S(1)} custom-call(s32[2,4]{1,0:T(2,128)} %all_flags.4, bf16[512,1024]{1,0:T(8,128)(2,1)} %tile.2), custom_call_target="tpu_custom_call" | custom-call | flops 12000000000 | bytes 1048592 | tf_op jit(solution)/shard_map/mask_tile_1/pallas_call | solution.py:39
  1.1 5.1 %collective-permute-start.2 = (bf16[512,256]{1,0:T(8,128)(2,1)S(1)}, bf16[512,256]{1,0:T(8,128)(2,1)S(1)}, u32[]{:S(2)}, u32[]{:S(2)}) collective-permute-start(bf16[512,256]{1,0:T(8,128)(2,1)S(1)} %mask_tile_1.1.refs_0_), channel_id=1, source_target_pairs={{0,6},{1,7},{2,0},{3,1},{4,2},{5,3},{6,4},{7,5},{8,14},{9,15},{10,... | collective-permute-start | bytes 786440 | tf_op jit(solution)/shard_map/send_Zb/ppermute | solution.py:278
  6.2 1.5 %collective-permute-start.3 = (bf16[512,256]{1,0:T(8,128)(2,1)S(1)}, bf16[512,256]{1,0:T(8,128)(2,1)S(1)}, u32[]{:S(2)}, u32[]{:S(2)}) collective-permute-start(bf16[512,256]{1,0:T(8,128)(2,1)S(1)} %mask_tile_1.1.refs_0_), channel_id=1, source_target_pairs={{0,1},{1,0},{2,3},{3,2},{4,5},{5,4},{6,7},{7,6},{8,9},{9,8},{10,11... | collective-permute-start | bytes 786440 | tf_op jit(solution)/shard_map/send_Db/ppermute | solution.py:278
  7.7 0.0 copy-done
  7.7 1.5 %collective-permute-start = (bf16[256,2048]{1,0:T(8,128)(2,1)S(1)}, bf16[256,2048]{1,0:T(8,128)(2,1)S(1)}, u32[]{:S(2)}, u32[]{:S(2)}) collective-permute-start(bf16[256,2048]{1,0:T(8,128)(2,1)S(1)} %copy-done), channel_id=1, source_target_pairs={{0,16},{8,24},{16,0},{24,8},{1,17},{9,25},{17,1},{25,9},{2,18},{10... | collective-permute-start | bytes 3145736 | tf_op jit(solution)/shard_map/send_Ax/ppermute | solution.py:278
  9.2 1.2 %mask_tile_2.1 = (bf16[512,256]{1,0:T(8,128)(2,1)S(1)}, bf16[512,512]{1,0:T(8,128)(2,1)S(1)}) custom-call(s32[2,4]{1,0:T(2,128)} %all_flags.4, bf16[512,1024]{1,0:T(8,128)(2,1)} %tile.2), custom_call_target="tpu_custom_call" | custom-call | bytes 1048592 | tf_op jit(solution)/shard_map/mask_tile_2/pallas_call | solution.py:39
  10.4 0.5 collective-permute-start.6
  10.9 2.0 %collective-permute-done.2.refs_1_ = bf16[512,256]{1,0:T(8,128)(2,1)S(1)} collective-permute-done((bf16[512,256]{1,0:T(8,128)(2,1)S(1)}, bf16[512,256]{1,0:T(8,128)(2,1)S(1)}, u32[]{:S(2)}, u32[]{:S(2)}) %collective-permute-start.2) | collective-permute-done | bytes 262176 | tf_op jit(solution)/shard_map/send_Zb/ppermute | solution.py:278
  12.9 1.1 %collective-permute-done.3.on_even = bf16[512,256]{1,0:T(8,128)(2,1)S(1)} collective-permute-done((bf16[512,256]{1,0:T(8,128)(2,1)S(1)}, bf16[512,256]{1,0:T(8,128)(2,1)S(1)}, u32[]{:S(2)}, u32[]{:S(2)}) %collective-permute-start.3) | collective-permute-done | bytes 262176 | tf_op jit(solution)/shard_map/send_Db/ppermute | solution.py:278
  13.9 1.5 %collective-permute-start.4 = (bf16[512,256]{1,0:T(8,128)(2,1)S(1)}, bf16[512,256]{1,0:T(8,128)(2,1)S(1)}, u32[]{:S(2)}, u32[]{:S(2)}) collective-permute-start(bf16[512,256]{1,0:T(8,128)(2,1)S(1)} %collective-permute-done.2.refs_1_), channel_id=1, source_target_pairs={{0,1},{1,0},{2,3},{3,2},{4,5},{5,4},{6,7},{7,6},{8,9},{9,8},{10,11... | collective-permute-start | bytes 786440 | tf_op jit(solution)/shard_map/send_Sb/ppermute | solution.py:278
  15.5 5.3 %collective-permute-done.4.on_odd.refs_2_ = bf16[512,256]{1,0:T(8,128)(2,1)S(1)} collective-permute-done((bf16[512,256]{1,0:T(8,128)(2,1)S(1)}, bf16[512,256]{1,0:T(8,128)(2,1)S(1)}, u32[]{:S(2)}, u32[]{:S(2)}) %collective-permute-start.4) | collective-permute-done | bytes 262176 | tf_op jit(solution)/shard_map/send_Sb/ppermute | solution.py:278
  20.8 2.7 %collective-permute-start.5 = (bf16[512,256]{1,0:T(8,128)(2,1)S(1)}, bf16[512,256]{1,0:T(8,128)(2,1)S(1)}, u32[]{:S(2)}, u32[]{:S(2)}) collective-permute-start(bf16[512,256]{1,0:T(8,128)(2,1)S(1)} %get-tuple-element.31.on_odd.refs_0_), channel_id=1, source_target_pairs={{0,6},{1,7},{2,0},{3,1},{4,2},{5,3},{6,4},{7,5},{8,14},{9,15},{10,... | collective-permute-start | bytes 786440 | tf_op jit(solution)/shard_map/send_Zc/ppermute | solution.py:278
  23.5 1.7 %collective-permute-done.6.on_even.refs_5_ = bf16[512,512]{1,0:T(8,128)(2,1)S(1)} collective-permute-done((bf16[512,512]{1,0:T(8,128)(2,1)S(1)}, bf16[512,512]{1,0:T(8,128)(2,1)S(1)}, u32[]{:S(2)}, u32[]{:S(2)}) %collective-permute-start.6) | collective-permute-done | bytes 524320 | tf_op jit(solution)/shard_map/send_Z12/ppermute | solution.py:278
  25.3 0.4 collective-permute-start.9
  25.8 3.1 %collective-permute-done.5.on_even.refs_1_ = bf16[512,256]{1,0:T(8,128)(2,1)S(1)} collective-permute-done((bf16[512,256]{1,0:T(8,128)(2,1)S(1)}, bf16[512,256]{1,0:T(8,128)(2,1)S(1)}, u32[]{:S(2)}, u32[]{:S(2)}) %collective-permute-start.5) | collective-permute-done | bytes 262176 | tf_op jit(solution)/shard_map/send_Zc/ppermute | solution.py:278
  28.9 4.1 %collective-permute-start.8 = (bf16[512,256]{1,0:T(8,128)(2,1)S(1)}, bf16[512,256]{1,0:T(8,128)(2,1)S(1)}, u32[]{:S(2)}, u32[]{:S(2)}) collective-permute-start(bf16[512,256]{1,0:T(8,128)(2,1)S(1)} %choose_X.1), channel_id=1, source_target_pairs={{0,6},{1,7},{2,0},{3,1},{4,2},{5,3},{6,4},{7,5},{8,14},{9,15},{10,... | collective-permute-start | bytes 786440 | tf_op jit(solution)/shard_map/send_X/ppermute | solution.py:278
  33.0 0.0 collective-permute-start.1
  33.0 1.5 %collective-permute-start.12 = (bf16[512,256]{1,0:T(8,128)(2,1)S(1)}, bf16[512,256]{1,0:T(8,128)(2,1)S(1)}, u32[]{:S(2)}, u32[]{:S(2)}) collective-permute-start(bf16[512,256]{1,0:T(8,128)(2,1)S(1)} %collective-permute-done.5.on_even.refs_1_), channel_id=1, source_target_pairs={{0,1},{1,0},{2,3},{3,2},{4,5},{5,4},{6,7},{7,6},{8,9},{9,8},{10,11... | collective-permute-start | bytes 786440 | tf_op jit(solution)/shard_map/send_Sc/ppermute | solution.py:278
  34.5 0.0 collective-permute-done.refs_1_
  34.5 0.2 collective-permute-start.7
  34.7 1.2 %collective-permute-done.9.refs_4_ = bf16[512,512]{1,0:T(8,128)(2,1)S(1)} collective-permute-done((bf16[512,512]{1,0:T(8,128)(2,1)S(1)}, bf16[512,512]{1,0:T(8,128)(2,1)S(1)}, u32[]{:S(2)}, u32[]{:S(2)}) %collective-permute-start.9) | collective-permute-done | bytes 524320 | tf_op jit(solution)/shard_map/send_Y12/ppermute | solution.py:278
  35.9 7.2 %collective-permute-start.11 = (bf16[512,512]{1,0:T(8,128)(2,1)S(1)}, bf16[512,512]{1,0:T(8,128)(2,1)S(1)}, u32[]{:S(2)}, u32[]{:S(2)}) collective-permute-start(bf16[512,512]{1,0:T(8,128)(2,1)S(1)} %collective-permute-done.9.refs_4_), channel_id=1, source_target_pairs={{0,6},{1,7},{2,0},{3,1},{4,2},{5,3},{6,4},{7,5},{8,14},{9,15},{10,... | collective-permute-start | bytes 1572872 | tf_op jit(solution)/shard_map/send_W12/ppermute | solution.py:278
  43.1 0.0 collective-permute-done.8.on_odd.on_even
  43.2 0.0 collective-permute-done.1.refs_2_
  43.2 0.0 collective-permute-done.7.refs_3_
  43.2 1.1 %stack_rows.1.left = bf16[1024,2048]{1,0:T(8,128)(2,1)S(1)} custom-call(s32[4,8]{1,0:T(4,128)} %all_flags.5, bf16[256,2048]{1,0:T(8,128)(2,1)S(1)} %copy-done, bf16[256,2048]{1,0:T(8,128)(2,1)S(1)} %collective-permute-done.refs_1_, bf16[256,2048]{1,0:T(8,128)(2,1)S(1)} %collective-permute-done.1.refs_2_, bf16[256,2048]{1,0:T(8,128)(2,1)S(1)} %collective-permute-done.7.refs_3_), custom_call_target="tpu_custom_call" | custom-call | flops 12000000000 | bytes 4194368 | tf_op jit(solution)/shard_map/stack_rows/pallas_call | solution.py:39
  44.4 1.5 %collective-permute-start.10 = (bf16[512,256]{1,0:T(8,128)(2,1)S(1)}, bf16[512,256]{1,0:T(8,128)(2,1)S(1)}, u32[]{:S(2)}, u32[]{:S(2)}) collective-permute-start(bf16[512,256]{1,0:T(8,128)(2,1)S(1)} %choose_Q.1), channel_id=1, source_target_pairs={{0,1},{1,0},{2,3},{3,2},{4,5},{5,4},{6,7},{7,6},{8,9},{9,8},{10,11... | collective-permute-start | bytes 786440 | tf_op jit(solution)/shard_map/send_Q/ppermute | solution.py:278
  45.9 0.0 collective-permute-done.12.refs_2_
  45.9 1.8 %sum_first.1.refs_3_ = bf16[1024,256]{1,0:T(8,128)(2,1)S(1)} custom-call(bf16[1024,2048]{1,0:T(8,128)(2,1)S(1)} %stack_rows.1.left, bf16[512,256]{1,0:T(8,128)(2,1)S(1)} %mask_tile_1.1.refs_0_, bf16[512,256]{1,0:T(8,128)(2,1)S(1)} %collective-permute-done.2.refs_1_, bf16[512,256]{1,0:T(8,128)(2,1)S(1)} %collective-permute-done.4.on_odd.refs_2_, ...), custom_call_target="tpu_custom_call" | custom-call | flops 12000000000 | bytes 5242880 | tf_op jit(solution)/shard_map/sum_first/pallas_call | solution.py:39
  47.7 3.1 %sum_partial.1.refs_2_ = f32[1024,768]{1,0:T(8,128)S(1)} custom-call(bf16[1024,2048]{1,0:T(8,128)(2,1)S(1)} %stack_rows.1.left, bf16[512,256]{1,0:T(8,128)(2,1)S(1)} %get-tuple-element.31.on_odd.refs_0_, bf16[512,256]{1,0:T(8,128)(2,1)S(1)} %collective-permute-done.5.on_even.refs_1_, bf16[512,256]{1,0:T(8,128)(2,1)S(1)} %collective-permute-done.12.refs_2_, ...), custom_call_target="tpu_custom_call" | custom-call | flops 6000000000 | bytes 6553600 | tf_op jit(solution)/shard_map/sum_partial/pallas_call | solution.py:39
  50.9 0.0 collective-permute-done.10.refs_0_
  50.9 0.0 collective-permute-done.11.refs_1_
  50.9 2.3 %sum_last.1 = bf16[1024,1024]{1,0:T(8,128)(2,1)} custom-call(bf16[1024,2048]{1,0:T(8,128)(2,1)S(1)} %stack_rows.1.left, bf16[512,256]{1,0:T(8,128)(2,1)S(1)} %collective-permute-done.10.refs_0_, bf16[512,512]{1,0:T(8,128)(2,1)S(1)} %collective-permute-done.11.refs_1_, f32[1024,768]{1,0:T(8,128)S(1)} %sum_partial.1.refs_2_, ...), custom_call_target="tpu_custom_call" | custom-call | flops 3000000000 | bytes 7077888 | tf_op jit(solution)/shard_map/sum_last/pallas_call | solution.py:39
  (4 shorter events, 0.1 us)
Async XLA Ops:
  0.0 7.7 %copy-start = (bf16[256,2048]{1,0:T(8,128)(2,1)S(1)}, bf16[256,2048]{1,0:T(8,128)(2,1)}, u32[]{:S(2)}) copy-start(bf16[256,2048]{1,0:T(8,128)(2,1)} %refs_0_.1) | copy-start | bytes 3145732
  1.1 11.8 %collective-permute-start.2 = (bf16[512,256]{1,0:T(8,128)(2,1)S(1)}, bf16[512,256]{1,0:T(8,128)(2,1)S(1)}, u32[]{:S(2)}, u32[]{:S(2)}) collective-permute-start(bf16[512,256]{1,0:T(8,128)(2,1)S(1)} %mask_tile_1.1.refs_0_), channel_id=1, source_target_pairs={{0,6},{1,7},{2,0},{3,1},{4,2},{5,3},{6,4},{7,5},{8,14},{9,15},{10,... | collective-permute-start | bytes 786440 | tf_op jit(solution)/shard_map/send_Zb/ppermute | solution.py:278
  6.2 7.8 %collective-permute-start.3 = (bf16[512,256]{1,0:T(8,128)(2,1)S(1)}, bf16[512,256]{1,0:T(8,128)(2,1)S(1)}, u32[]{:S(2)}, u32[]{:S(2)}) collective-permute-start(bf16[512,256]{1,0:T(8,128)(2,1)S(1)} %mask_tile_1.1.refs_0_), channel_id=1, source_target_pairs={{0,1},{1,0},{2,3},{3,2},{4,5},{5,4},{6,7},{7,6},{8,9},{9,8},{10,11... | collective-permute-start | bytes 786440 | tf_op jit(solution)/shard_map/send_Db/ppermute | solution.py:278
  7.7 26.8 %collective-permute-start = (bf16[256,2048]{1,0:T(8,128)(2,1)S(1)}, bf16[256,2048]{1,0:T(8,128)(2,1)S(1)}, u32[]{:S(2)}, u32[]{:S(2)}) collective-permute-start(bf16[256,2048]{1,0:T(8,128)(2,1)S(1)} %copy-done), channel_id=1, source_target_pairs={{0,16},{8,24},{16,0},{24,8},{1,17},{9,25},{17,1},{25,9},{2,18},{10... | collective-permute-start | bytes 3145736 | tf_op jit(solution)/shard_map/send_Ax/ppermute | solution.py:278
  10.4 14.9 %collective-permute-start.6 = (bf16[512,512]{1,0:T(8,128)(2,1)S(1)}, bf16[512,512]{1,0:T(8,128)(2,1)S(1)}, u32[]{:S(2)}, u32[]{:S(2)}) collective-permute-start(bf16[512,512]{1,0:T(8,128)(2,1)S(1)} %get-tuple-element.32.on_odd.refs_3_), channel_id=1, source_target_pairs={{0,6},{1,7},{2,0},{3,1},{4,2},{5,3},{6,4},{7,5},{8,14},{9,15},{10,... | collective-permute-start | bytes 1572872 | tf_op jit(solution)/shard_map/send_Z12/ppermute | solution.py:278
  13.9 6.9 %collective-permute-start.4 = (bf16[512,256]{1,0:T(8,128)(2,1)S(1)}, bf16[512,256]{1,0:T(8,128)(2,1)S(1)}, u32[]{:S(2)}, u32[]{:S(2)}) collective-permute-start(bf16[512,256]{1,0:T(8,128)(2,1)S(1)} %collective-permute-done.2.refs_1_), channel_id=1, source_target_pairs={{0,1},{1,0},{2,3},{3,2},{4,5},{5,4},{6,7},{7,6},{8,9},{9,8},{10,11... | collective-permute-start | bytes 786440 | tf_op jit(solution)/shard_map/send_Sb/ppermute | solution.py:278
  20.8 8.1 %collective-permute-start.5 = (bf16[512,256]{1,0:T(8,128)(2,1)S(1)}, bf16[512,256]{1,0:T(8,128)(2,1)S(1)}, u32[]{:S(2)}, u32[]{:S(2)}) collective-permute-start(bf16[512,256]{1,0:T(8,128)(2,1)S(1)} %get-tuple-element.31.on_odd.refs_0_), channel_id=1, source_target_pairs={{0,6},{1,7},{2,0},{3,1},{4,2},{5,3},{6,4},{7,5},{8,14},{9,15},{10,... | collective-permute-start | bytes 786440 | tf_op jit(solution)/shard_map/send_Zc/ppermute | solution.py:278
  25.3 10.6 %collective-permute-start.9 = (bf16[512,512]{1,0:T(8,128)(2,1)S(1)}, bf16[512,512]{1,0:T(8,128)(2,1)S(1)}, u32[]{:S(2)}, u32[]{:S(2)}) collective-permute-start(bf16[512,512]{1,0:T(8,128)(2,1)S(1)} %choose_Y12.1), channel_id=1, source_target_pairs={{0,1},{1,0},{2,3},{3,2},{4,5},{5,4},{6,7},{7,6},{8,9},{9,8},{10,11... | collective-permute-start | bytes 1572872 | tf_op jit(solution)/shard_map/send_Y12/ppermute | solution.py:278
  28.9 14.2 %collective-permute-start.8 = (bf16[512,256]{1,0:T(8,128)(2,1)S(1)}, bf16[512,256]{1,0:T(8,128)(2,1)S(1)}, u32[]{:S(2)}, u32[]{:S(2)}) collective-permute-start(bf16[512,256]{1,0:T(8,128)(2,1)S(1)} %choose_X.1), channel_id=1, source_target_pairs={{0,6},{1,7},{2,0},{3,1},{4,2},{5,3},{6,4},{7,5},{8,14},{9,15},{10,... | collective-permute-start | bytes 786440 | tf_op jit(solution)/shard_map/send_X/ppermute | solution.py:278
  33.0 10.2 %collective-permute-start.1 = (bf16[256,2048]{1,0:T(8,128)(2,1)S(1)}, bf16[256,2048]{1,0:T(8,128)(2,1)S(1)}, u32[]{:S(2)}, u32[]{:S(2)}) collective-permute-start(bf16[256,2048]{1,0:T(8,128)(2,1)S(1)} %copy-done), channel_id=1, source_target_pairs={{0,8},{8,0},{16,24},{24,16},{1,9},{9,1},{17,25},{25,17},{2,10},{10... | collective-permute-start | bytes 3145736 | tf_op jit(solution)/shard_map/send_Af/ppermute | solution.py:278
  33.0 12.9 %collective-permute-start.12 = (bf16[512,256]{1,0:T(8,128)(2,1)S(1)}, bf16[512,256]{1,0:T(8,128)(2,1)S(1)}, u32[]{:S(2)}, u32[]{:S(2)}) collective-permute-start(bf16[512,256]{1,0:T(8,128)(2,1)S(1)} %collective-permute-done.5.on_even.refs_1_), channel_id=1, source_target_pairs={{0,1},{1,0},{2,3},{3,2},{4,5},{5,4},{6,7},{7,6},{8,9},{9,8},{10,11... | collective-permute-start | bytes 786440 | tf_op jit(solution)/shard_map/send_Sc/ppermute | solution.py:278
  34.5 8.7 %collective-permute-start.7 = (bf16[256,2048]{1,0:T(8,128)(2,1)S(1)}, bf16[256,2048]{1,0:T(8,128)(2,1)S(1)}, u32[]{:S(2)}, u32[]{:S(2)}) collective-permute-start(bf16[256,2048]{1,0:T(8,128)(2,1)S(1)} %collective-permute-done.refs_1_), channel_id=1, source_target_pairs={{0,8},{8,0},{16,24},{24,16},{1,9},{9,1},{17,25},{25,17},{2,10},{10... | collective-permute-start | bytes 3145736 | tf_op jit(solution)/shard_map/send_Ar/ppermute | solution.py:278
  35.9 15.0 %collective-permute-start.11 = (bf16[512,512]{1,0:T(8,128)(2,1)S(1)}, bf16[512,512]{1,0:T(8,128)(2,1)S(1)}, u32[]{:S(2)}, u32[]{:S(2)}) collective-permute-start(bf16[512,512]{1,0:T(8,128)(2,1)S(1)} %collective-permute-done.9.refs_4_), channel_id=1, source_target_pairs={{0,6},{1,7},{2,0},{3,1},{4,2},{5,3},{6,4},{7,5},{8,14},{9,15},{10,... | collective-permute-start | bytes 1572872 | tf_op jit(solution)/shard_map/send_W12/ppermute | solution.py:278
  44.4 6.5 %collective-permute-start.10 = (bf16[512,256]{1,0:T(8,128)(2,1)S(1)}, bf16[512,256]{1,0:T(8,128)(2,1)S(1)}, u32[]{:S(2)}, u32[]{:S(2)}) collective-permute-start(bf16[512,256]{1,0:T(8,128)(2,1)S(1)} %choose_Q.1), channel_id=1, source_target_pairs={{0,1},{1,0},{2,3},{3,2},{4,5},{5,4},{6,7},{7,6},{8,9},{9,8},{10,11... | collective-permute-start | bytes 786440 | tf_op jit(solution)/shard_map/send_Q/ppermute | solution.py:278

commit v6 on v5

--- a/solution.py
+++ b/solution.py
@@ -17,16 +17,15 @@
 
 
 COST = {
-    "choose_b": 12000000000,
-    "mask_tile_1": 12000000000,
-    "mask_tile_2": 0,
-    "sum_last": 3000000000,
+    "choose_b": 3000000000,
+    "mask_tile_1": 0,
+    "mask_tile_2": 6000000000,
+    "sum_last": 6000000000,
     "choose_Y12": 0,
     "choose_X": 1000000000,
     "choose_Q": 6000000000,
     "stack_rows": 12000000000,
-    "sum_partial": 6000000000,
-    "sum_first": 12000000000,
+    "sum_early": 3000000000,
 }
 
 
@@ -171,19 +170,19 @@
 
 
 def sum_kernel(plan, left, *refs):
-    places, rights, has_partial = plan
-    partial = refs[rights] if has_partial else None
-    out = refs[-1]
+    groups, rights = plan
+    tiles, outs = refs[:rights], refs[rights:]
     chunk, count = chunks_of(left)
 
     @pl.loop(0, count)
     def _(index):
         rows = pl.ds(pl.multiple_of(index * chunk, chunk), chunk)
-
-        def store(columns, total):
-            out[rows, columns] = total.astype(out.dtype)
-
-        sums(left, refs[:rights], places, partial, rows, store)
+        for places, out in zip(groups, outs):
+
+            def store(columns, total):
+                out[rows, columns] = total.astype(out.dtype)
+
+            sums(left, tiles, places, None, rows, store)
 
 
 def last_kernel(plan, left, *refs):
@@ -235,18 +234,23 @@
     return tiles, numbered
 
 
-def add_products(name, left, places, partial=None, dtype=jnp.float32):
-    tiles, numbered = number_terms(places)
-    rows, columns = left.shape[0], sum(terms[0][0].shape[1] for terms in places)
-    operands = [pinned(x) for x in (left, *tiles, *([] if partial is None else [partial]))]
-    return kernel_call(
-        functools.partial(sum_kernel, (numbered, len(tiles), partial is not None)),
+def add_products(name, left, groups, dtypes):
+    tiles, numbered = number_terms([terms for places in groups for terms in places])
+    rows = left.shape[0]
+    numbered_groups, out_shapes = [], []
+    for places, dtype in zip(groups, dtypes):
+        numbered_groups.append(numbered[: len(places)])
+        numbered = numbered[len(places) :]
+        out_shapes.append(VMEM((rows, sum(terms[0][0].shape[1] for terms in places)), dtype))
+    operands = [pinned(x) for x in (left, *tiles)]
+    return kernel_call(
+        functools.partial(sum_kernel, (tuple(numbered_groups), len(tiles))),
         "sum_" + name,
-        VMEM((rows, columns), dtype),
+        out_shapes,
         operands,
         [VMEM] * len(operands),
         VMEM,
-        flops=2 * rows * sum(tile.size for terms in places for tile, _, _ in terms),
+        flops=2 * rows * sum(tile.size for places in groups for terms in places for tile, _, _ in terms),
     )
 
 
@@ -286,15 +290,14 @@
 
 
 HELD = {
-    "Sb": ["Db", "Zb", "own_c"],
+    "Sb": ["Db", "own_c"],
     "Zc": ["Sb"],
-    "Q": ["Y12", "Ar", "own_c", "X", "own_b"],
+    "Q": ["Y12", "Ar", "own_c", "X", "own_b", "Ax"],
     "Ar": ["Z12", "Zb"],
-    "last": ["Zc", "first", "Af", "Db", "Ar", "Zb", "Z12", "Sc", "Q"],
-    "first": ["own_c", "X", "Af"],
-    "partial": ["Db", "own_b", "Ar", "Sc"],
-    "X": ["Z12"],
+    "last": ["Zc", "Af", "Db", "Ar", "Zb", "Z12", "Sc", "Q"],
     "Y12": ["Sb"],
+    "early": ["Af"],
+    "W12": ["Z12"],
 }
 
 
@@ -350,20 +353,21 @@
     offsets += [(distance, True) for distance, _ in offsets]
     left = stack_rows(lefts, tuple(offsets), mask_a)
     column_b = [(own_b, 0, 0), (value("Zb"), 2, 2), (value("Sb"), 3, 1), (choose("b", value("Db"), value("X")), 1, 3)]
-    got["first"] = [add_products("first", held("first", left), [column_b], dtype=left.dtype)]
     by_two("W12", value("Y12"))
     across("Q", choose("Q", value("X"), own_c))
 
     column_12 = [(own_12, 0, 0), (value("Y12"), 1, 1), (value("Z12"), 2, 2)]
     column_c = [(own_c, 0, 0), (value("Zc"), 2, 2), (value("Sc"), 3, 1)]
-    got["partial"] = [add_products("partial", held("partial", left), [column_c, column_12])]
+    first, partial = add_products(
+        "early", held("early", left), [[column_b], [column_c, column_12]], [left.dtype, jnp.float32]
+    )
     return finish_product(
         held("last", left),
         [[(value("Q"), 1, 3)], [(value("W12"), 3, 3)]],
         piece,
         width,
-        value("partial"),
-        [(value("first"), 0)],
+        partial,
+        [(first, 0)],
     )
 
 

time: 53.4 us -> 53.2 us (level)
  Pallas kernels: 10.7 us -> 9.93 us
    pallas_call x10 -> x9, Pallas kernels: 10.7 us -> 9.93 us  [kernel_call(): pl.pallas_call(kernel, out_shape=out_shape, in_specs=[pl.BlockSpec(memory...]
  transfers between devices with their start and end apart: 13 -> 13, of which waited for: 6 -> 7; matrix products, arithmetic and copies ran while one was open for 0% -> 0% of each run, Pallas kernels for 14% -> 13%
where the time goes in v6:
time: 53.2 us; the launch traced here: 53.1 us
  starting transfers between devices  28.1 us (53%)
  waiting for transfers between devices  14.9 us (28%)
  Pallas kernels  9.93 us (19%)
    ppermute x13, starting transfers between devices, moved(): lax.ppermute(block, axis, [(i, target(i) % count) for i in range(count)])  28.1 us
    ppermute x13, waiting for transfers between devices, moved(): lax.ppermute(block, axis, [(i, target(i) % count) for i in range(count)])  14.9 us
    pallas_call x9, Pallas kernels, kernel_call(): pl.pallas_call(kernel, out_shape=out_shape, in_specs=[pl.BlockSpec(memory...  9.93 us
  transfers between devices with their start and end apart: 13, of which 7 were waited for; matrix products, arithmetic and copies ran while one was open for 0% of the time, Pallas kernels for 13%

profile of v6, /device:TPU:0, one launch (start us, length us, event | category | flops | bytes accessed | tf_op | source)
XLA Modules:
  0.0 53.1 jit_solution(680062539634770452)
XLA Ops:
  0.0 1.0 %mask_tile_1.1.refs_0_ = bf16[512,256]{1,0:T(8,128)(2,1)S(1)} custom-call(s32[2,4]{1,0:T(2,128)} %all_flags.4, bf16[512,1024]{1,0:T(8,128)(2,1)} %tile.2), custom_call_target="tpu_custom_call" | custom-call | bytes 1048592 | tf_op jit(solution)/shard_map/mask_tile_1/pallas_call | solution.py:38
  1.0 5.1 %collective-permute-start.3 = (bf16[512,256]{1,0:T(8,128)(2,1)S(1)}, bf16[512,256]{1,0:T(8,128)(2,1)S(1)}, u32[]{:S(2)}, u32[]{:S(2)}) collective-permute-start(bf16[512,256]{1,0:T(8,128)(2,1)S(1)} %mask_tile_1.1.refs_0_), channel_id=1, source_target_pairs={{0,6},{1,7},{2,0},{3,1},{4,2},{5,3},{6,4},{7,5},{8,14},{9,15},{10,... | collective-permute-start | bytes 786440 | tf_op jit(solution)/shard_map/send_Zb/ppermute | solution.py:282
  6.1 1.5 %collective-permute-start.5 = (bf16[512,256]{1,0:T(8,128)(2,1)S(1)}, bf16[512,256]{1,0:T(8,128)(2,1)S(1)}, u32[]{:S(2)}, u32[]{:S(2)}) collective-permute-start(bf16[512,256]{1,0:T(8,128)(2,1)S(1)} %mask_tile_1.1.refs_0_), channel_id=1, source_target_pairs={{0,1},{1,0},{2,3},{3,2},{4,5},{5,4},{6,7},{7,6},{8,9},{9,8},{10,11... | collective-permute-start | bytes 786440 | tf_op jit(solution)/shard_map/send_Db/ppermute | solution.py:282
  7.6 1.5 %collective-permute-start = (bf16[256,2048]{1,0:T(8,128)(2,1)}, bf16[256,2048]{1,0:T(8,128)(2,1)S(1)}, u32[]{:S(2)}, u32[]{:S(2)}) collective-permute-start(bf16[256,2048]{1,0:T(8,128)(2,1)} %refs_0_.1), channel_id=1, source_target_pairs={{0,16},{8,24},{16,0},{24,8},{1,17},{9,25},{17,1},{25,9},{2,18},{10... | collective-permute-start | bytes 3145736 | tf_op jit(solution)/shard_map/send_Ax/ppermute | solution.py:282
  9.1 1.2 %mask_tile_2.1 = (bf16[512,256]{1,0:T(8,128)(2,1)S(1)}, bf16[512,512]{1,0:T(8,128)(2,1)S(1)}) custom-call(s32[2,4]{1,0:T(2,128)} %all_flags.4, bf16[512,1024]{1,0:T(8,128)(2,1)} %tile.2), custom_call_target="tpu_custom_call" | custom-call | flops 6000000000 | bytes 1048592 | tf_op jit(solution)/shard_map/mask_tile_2/pallas_call | solution.py:38
  10.3 0.0 copy-start
  10.3 0.5 collective-permute-start.2
  10.8 2.0 %collective-permute-done.3.refs_1_ = bf16[512,256]{1,0:T(8,128)(2,1)S(1)} collective-permute-done((bf16[512,256]{1,0:T(8,128)(2,1)S(1)}, bf16[512,256]{1,0:T(8,128)(2,1)S(1)}, u32[]{:S(2)}, u32[]{:S(2)}) %collective-permute-start.3) | collective-permute-done | bytes 262176 | tf_op jit(solution)/shard_map/send_Zb/ppermute | solution.py:282
  12.8 1.1 %collective-permute-done.5.on_even = bf16[512,256]{1,0:T(8,128)(2,1)S(1)} collective-permute-done((bf16[512,256]{1,0:T(8,128)(2,1)S(1)}, bf16[512,256]{1,0:T(8,128)(2,1)S(1)}, u32[]{:S(2)}, u32[]{:S(2)}) %collective-permute-start.5) | collective-permute-done | bytes 262176 | tf_op jit(solution)/shard_map/send_Db/ppermute | solution.py:282
  13.9 1.5 %collective-permute-start.6 = (bf16[512,256]{1,0:T(8,128)(2,1)S(1)}, bf16[512,256]{1,0:T(8,128)(2,1)S(1)}, u32[]{:S(2)}, u32[]{:S(2)}) collective-permute-start(bf16[512,256]{1,0:T(8,128)(2,1)S(1)} %collective-permute-done.3.refs_1_), channel_id=1, source_target_pairs={{0,1},{1,0},{2,3},{3,2},{4,5},{5,4},{6,7},{7,6},{8,9},{9,8},{10,11... | collective-permute-start | bytes 786440 | tf_op jit(solution)/shard_map/send_Sb/ppermute | solution.py:282
  15.4 5.3 %collective-permute-done.6.on_odd.refs_2_ = bf16[512,256]{1,0:T(8,128)(2,1)S(1)} collective-permute-done((bf16[512,256]{1,0:T(8,128)(2,1)S(1)}, bf16[512,256]{1,0:T(8,128)(2,1)S(1)}, u32[]{:S(2)}, u32[]{:S(2)}) %collective-permute-start.6) | collective-permute-done | bytes 262176 | tf_op jit(solution)/shard_map/send_Sb/ppermute | solution.py:282
  20.7 2.7 %collective-permute-start.7 = (bf16[512,256]{1,0:T(8,128)(2,1)S(1)}, bf16[512,256]{1,0:T(8,128)(2,1)S(1)}, u32[]{:S(2)}, u32[]{:S(2)}) collective-permute-start(bf16[512,256]{1,0:T(8,128)(2,1)S(1)} %get-tuple-element.31.on_odd.refs_4_), channel_id=1, source_target_pairs={{0,6},{1,7},{2,0},{3,1},{4,2},{5,3},{6,4},{7,5},{8,14},{9,15},{10,... | collective-permute-start | bytes 786440 | tf_op jit(solution)/shard_map/send_Zc/ppermute | solution.py:282
  23.4 1.7 %collective-permute-done.2.on_even.refs_9_ = bf16[512,512]{1,0:T(8,128)(2,1)S(1)} collective-permute-done((bf16[512,512]{1,0:T(8,128)(2,1)S(1)}, bf16[512,512]{1,0:T(8,128)(2,1)S(1)}, u32[]{:S(2)}, u32[]{:S(2)}) %collective-permute-start.2) | collective-permute-done | bytes 524320 | tf_op jit(solution)/shard_map/send_Z12/ppermute | solution.py:282
  25.2 0.4 collective-permute-start.8
  25.6 3.1 %collective-permute-done.7.on_even.refs_5_ = bf16[512,256]{1,0:T(8,128)(2,1)S(1)} collective-permute-done((bf16[512,256]{1,0:T(8,128)(2,1)S(1)}, bf16[512,256]{1,0:T(8,128)(2,1)S(1)}, u32[]{:S(2)}, u32[]{:S(2)}) %collective-permute-start.7) | collective-permute-done | bytes 262176 | tf_op jit(solution)/shard_map/send_Zc/ppermute | solution.py:282
  28.8 4.1 %collective-permute-start.10 = (bf16[512,256]{1,0:T(8,128)(2,1)S(1)}, bf16[512,256]{1,0:T(8,128)(2,1)S(1)}, u32[]{:S(2)}, u32[]{:S(2)}) collective-permute-start(bf16[512,256]{1,0:T(8,128)(2,1)S(1)} %choose_X.1), channel_id=1, source_target_pairs={{0,6},{1,7},{2,0},{3,1},{4,2},{5,3},{6,4},{7,5},{8,14},{9,15},{10,... | collective-permute-start | bytes 786440 | tf_op jit(solution)/shard_map/send_X/ppermute | solution.py:282
  32.9 0.0 copy-done
  32.9 0.0 collective-permute-start.1
  32.9 0.0 collective-permute-done.refs_1_
  32.9 0.5 collective-permute-start.4
  33.4 1.5 %collective-permute-start.9 = (bf16[512,256]{1,0:T(8,128)(2,1)S(1)}, bf16[512,256]{1,0:T(8,128)(2,1)S(1)}, u32[]{:S(2)}, u32[]{:S(2)}) collective-permute-start(bf16[512,256]{1,0:T(8,128)(2,1)S(1)} %collective-permute-done.7.on_even.refs_5_), channel_id=1, source_target_pairs={{0,1},{1,0},{2,3},{3,2},{4,5},{5,4},{6,7},{7,6},{8,9},{9,8},{10,11... | collective-permute-start | bytes 786440 | tf_op jit(solution)/shard_map/send_Sc/ppermute | solution.py:282
  34.9 0.9 %collective-permute-done.8.refs_8_ = bf16[512,512]{1,0:T(8,128)(2,1)S(1)} collective-permute-done((bf16[512,512]{1,0:T(8,128)(2,1)S(1)}, bf16[512,512]{1,0:T(8,128)(2,1)S(1)}, u32[]{:S(2)}, u32[]{:S(2)}) %collective-permute-start.8) | collective-permute-done | bytes 524320 | tf_op jit(solution)/shard_map/send_Y12/ppermute | solution.py:282
  35.8 7.2 %collective-permute-start.12 = (bf16[512,512]{1,0:T(8,128)(2,1)S(1)}, bf16[512,512]{1,0:T(8,128)(2,1)S(1)}, u32[]{:S(2)}, u32[]{:S(2)}) collective-permute-start(bf16[512,512]{1,0:T(8,128)(2,1)S(1)} %collective-permute-done.8.refs_8_), channel_id=1, source_target_pairs={{0,6},{1,7},{2,0},{3,1},{4,2},{5,3},{6,4},{7,5},{8,14},{9,15},{10,... | collective-permute-start | bytes 1572872 | tf_op jit(solution)/shard_map/send_W12/ppermute | solution.py:282
  43.0 0.0 collective-permute-done.10.on_even.on_odd
  43.1 0.0 collective-permute-done.1.refs_2_
  43.1 0.0 collective-permute-done.4.refs_3_
  43.1 1.2 %stack_rows.1.left = bf16[1024,2048]{1,0:T(8,128)(2,1)S(1)} custom-call(s32[4,8]{1,0:T(4,128)} %all_flags.5, bf16[256,2048]{1,0:T(8,128)(2,1)S(1)} %copy-done, bf16[256,2048]{1,0:T(8,128)(2,1)S(1)} %collective-permute-done.refs_1_, bf16[256,2048]{1,0:T(8,128)(2,1)S(1)} %collective-permute-done.1.refs_2_, bf16[256,2048]{1,0:T(8,128)(2,1)S(1)} %collective-permute-done.4.refs_3_), custom_call_target="tpu_custom_call" | custom-call | flops 12000000000 | bytes 4194368 | tf_op jit(solution)/shard_map/stack_rows/pallas_call | solution.py:38
  44.3 1.5 %collective-permute-start.11 = (bf16[512,256]{1,0:T(8,128)(2,1)S(1)}, bf16[512,256]{1,0:T(8,128)(2,1)S(1)}, u32[]{:S(2)}, u32[]{:S(2)}) collective-permute-start(bf16[512,256]{1,0:T(8,128)(2,1)S(1)} %choose_Q.1), channel_id=1, source_target_pairs={{0,1},{1,0},{2,3},{3,2},{4,5},{5,4},{6,7},{7,6},{8,9},{9,8},{10,11... | collective-permute-start | bytes 786440 | tf_op jit(solution)/shard_map/send_Q/ppermute | solution.py:282
  45.8 0.0 collective-permute-done.9.refs_6_
  45.8 4.2 %sum_early.1 = (bf16[1024,256]{1,0:T(8,128)(2,1)S(1)}, f32[1024,768]{1,0:T(8,128)S(1)}) custom-call(bf16[1024,2048]{1,0:T(8,128)(2,1)S(1)} %stack_rows.1.left, bf16[512,256]{1,0:T(8,128)(2,1)S(1)} %mask_tile_1.1.refs_0_, bf16[512,256]{1,0:T(8,128)(2,1)S(1)} %collective-permute-done.3.refs_1_, bf16[512,256]{1,0:T(8,128)(2,1)S(1)} %collective-permute-done.6.on_odd.refs_2_, ...), custom_call_target="tpu_custom_call" | custom-call | flops 3000000000 | bytes 7602176 | tf_op jit(solution)/shard_map/sum_early/pallas_call | solution.py:38
  50.1 0.7 %collective-permute-done.11.refs_0_ = bf16[512,256]{1,0:T(8,128)(2,1)S(1)} collective-permute-done((bf16[512,256]{1,0:T(8,128)(2,1)S(1)}, bf16[512,256]{1,0:T(8,128)(2,1)S(1)}, u32[]{:S(2)}, u32[]{:S(2)}) %collective-permute-start.11) | collective-permute-done | bytes 262176 | tf_op jit(solution)/shard_map/send_Q/ppermute | solution.py:282
  50.8 0.0 collective-permute-done.12.refs_1_
  50.8 2.3 %sum_last.1 = bf16[1024,1024]{1,0:T(8,128)(2,1)} custom-call(bf16[1024,2048]{1,0:T(8,128)(2,1)S(1)} %stack_rows.1.left, bf16[512,256]{1,0:T(8,128)(2,1)S(1)} %collective-permute-done.11.refs_0_, bf16[512,512]{1,0:T(8,128)(2,1)S(1)} %collective-permute-done.12.refs_1_, f32[1024,768]{1,0:T(8,128)S(1)} %get-tuple-element.45.refs_2_, ...), custom_call_target="tpu_custom_call" | custom-call | flops 6000000000 | bytes 7077888 | tf_op jit(solution)/shard_map/sum_last/pallas_call | solution.py:38
  (4 shorter events, 0.1 us)
Async XLA Ops:
  1.0 11.8 %collective-permute-start.3 = (bf16[512,256]{1,0:T(8,128)(2,1)S(1)}, bf16[512,256]{1,0:T(8,128)(2,1)S(1)}, u32[]{:S(2)}, u32[]{:S(2)}) collective-permute-start(bf16[512,256]{1,0:T(8,128)(2,1)S(1)} %mask_tile_1.1.refs_0_), channel_id=1, source_target_pairs={{0,6},{1,7},{2,0},{3,1},{4,2},{5,3},{6,4},{7,5},{8,14},{9,15},{10,... | collective-permute-start | bytes 786440 | tf_op jit(solution)/shard_map/send_Zb/ppermute | solution.py:282
  6.1 7.8 %collective-permute-start.5 = (bf16[512,256]{1,0:T(8,128)(2,1)S(1)}, bf16[512,256]{1,0:T(8,128)(2,1)S(1)}, u32[]{:S(2)}, u32[]{:S(2)}) collective-permute-start(bf16[512,256]{1,0:T(8,128)(2,1)S(1)} %mask_tile_1.1.refs_0_), channel_id=1, source_target_pairs={{0,1},{1,0},{2,3},{3,2},{4,5},{5,4},{6,7},{7,6},{8,9},{9,8},{10,11... | collective-permute-start | bytes 786440 | tf_op jit(solution)/shard_map/send_Db/ppermute | solution.py:282
  7.6 25.3 %collective-permute-start = (bf16[256,2048]{1,0:T(8,128)(2,1)}, bf16[256,2048]{1,0:T(8,128)(2,1)S(1)}, u32[]{:S(2)}, u32[]{:S(2)}) collective-permute-start(bf16[256,2048]{1,0:T(8,128)(2,1)} %refs_0_.1), channel_id=1, source_target_pairs={{0,16},{8,24},{16,0},{24,8},{1,17},{9,25},{17,1},{25,9},{2,18},{10... | collective-permute-start | bytes 3145736 | tf_op jit(solution)/shard_map/send_Ax/ppermute | solution.py:282
  10.3 22.6 %copy-start = (bf16[256,2048]{1,0:T(8,128)(2,1)S(1)}, bf16[256,2048]{1,0:T(8,128)(2,1)}, u32[]{:S(2)}) copy-start(bf16[256,2048]{1,0:T(8,128)(2,1)} %refs_0_.1) | copy-start | bytes 3145732
  10.3 14.9 %collective-permute-start.2 = (bf16[512,512]{1,0:T(8,128)(2,1)S(1)}, bf16[512,512]{1,0:T(8,128)(2,1)S(1)}, u32[]{:S(2)}, u32[]{:S(2)}) collective-permute-start(bf16[512,512]{1,0:T(8,128)(2,1)S(1)} %get-tuple-element.27.on_odd.refs_7_), channel_id=1, source_target_pairs={{0,6},{1,7},{2,0},{3,1},{4,2},{5,3},{6,4},{7,5},{8,14},{9,15},{10,... | collective-permute-start | bytes 1572872 | tf_op jit(solution)/shard_map/send_Z12/ppermute | solution.py:282
  13.9 6.9 %collective-permute-start.6 = (bf16[512,256]{1,0:T(8,128)(2,1)S(1)}, bf16[512,256]{1,0:T(8,128)(2,1)S(1)}, u32[]{:S(2)}, u32[]{:S(2)}) collective-permute-start(bf16[512,256]{1,0:T(8,128)(2,1)S(1)} %collective-permute-done.3.refs_1_), channel_id=1, source_target_pairs={{0,1},{1,0},{2,3},{3,2},{4,5},{5,4},{6,7},{7,6},{8,9},{9,8},{10,11... | collective-permute-start | bytes 786440 | tf_op jit(solution)/shard_map/send_Sb/ppermute | solution.py:282
  20.7 8.0 %collective-permute-start.7 = (bf16[512,256]{1,0:T(8,128)(2,1)S(1)}, bf16[512,256]{1,0:T(8,128)(2,1)S(1)}, u32[]{:S(2)}, u32[]{:S(2)}) collective-permute-start(bf16[512,256]{1,0:T(8,128)(2,1)S(1)} %get-tuple-element.31.on_odd.refs_4_), channel_id=1, source_target_pairs={{0,6},{1,7},{2,0},{3,1},{4,2},{5,3},{6,4},{7,5},{8,14},{9,15},{10,... | collective-permute-start | bytes 786440 | tf_op jit(solution)/shard_map/send_Zc/ppermute | solution.py:282
  25.2 10.6 %collective-permute-start.8 = (bf16[512,512]{1,0:T(8,128)(2,1)S(1)}, bf16[512,512]{1,0:T(8,128)(2,1)S(1)}, u32[]{:S(2)}, u32[]{:S(2)}) collective-permute-start(bf16[512,512]{1,0:T(8,128)(2,1)S(1)} %choose_Y12.1), channel_id=1, source_target_pairs={{0,1},{1,0},{2,3},{3,2},{4,5},{5,4},{6,7},{7,6},{8,9},{9,8},{10,11... | collective-permute-start | bytes 1572872 | tf_op jit(solution)/shard_map/send_Y12/ppermute | solution.py:282
  28.8 14.3 %collective-permute-start.10 = (bf16[512,256]{1,0:T(8,128)(2,1)S(1)}, bf16[512,256]{1,0:T(8,128)(2,1)S(1)}, u32[]{:S(2)}, u32[]{:S(2)}) collective-permute-start(bf16[512,256]{1,0:T(8,128)(2,1)S(1)} %choose_X.1), channel_id=1, source_target_pairs={{0,6},{1,7},{2,0},{3,1},{4,2},{5,3},{6,4},{7,5},{8,14},{9,15},{10,... | collective-permute-start | bytes 786440 | tf_op jit(solution)/shard_map/send_X/ppermute | solution.py:282
  32.9 10.3 %collective-permute-start.1 = (bf16[256,2048]{1,0:T(8,128)(2,1)S(1)}, bf16[256,2048]{1,0:T(8,128)(2,1)S(1)}, u32[]{:S(2)}, u32[]{:S(2)}) collective-permute-start(bf16[256,2048]{1,0:T(8,128)(2,1)S(1)} %copy-done), channel_id=1, source_target_pairs={{0,8},{8,0},{16,24},{24,16},{1,9},{9,1},{17,25},{25,17},{2,10},{10... | collective-permute-start | bytes 3145736 | tf_op jit(solution)/shard_map/send_Af/ppermute | solution.py:282
  32.9 10.3 %collective-permute-start.4 = (bf16[256,2048]{1,0:T(8,128)(2,1)S(1)}, bf16[256,2048]{1,0:T(8,128)(2,1)S(1)}, u32[]{:S(2)}, u32[]{:S(2)}) collective-permute-start(bf16[256,2048]{1,0:T(8,128)(2,1)S(1)} %collective-permute-done.refs_1_), channel_id=1, source_target_pairs={{0,8},{8,0},{16,24},{24,16},{1,9},{9,1},{17,25},{25,17},{2,10},{10... | collective-permute-start | bytes 3145736 | tf_op jit(solution)/shard_map/send_Ar/ppermute | solution.py:282
  33.4 12.5 %collective-permute-start.9 = (bf16[512,256]{1,0:T(8,128)(2,1)S(1)}, bf16[512,256]{1,0:T(8,128)(2,1)S(1)}, u32[]{:S(2)}, u32[]{:S(2)}) collective-permute-start(bf16[512,256]{1,0:T(8,128)(2,1)S(1)} %collective-permute-done.7.on_even.refs_5_), channel_id=1, source_target_pairs={{0,1},{1,0},{2,3},{3,2},{4,5},{5,4},{6,7},{7,6},{8,9},{9,8},{10,11... | collective-permute-start | bytes 786440 | tf_op jit(solution)/shard_map/send_Sc/ppermute | solution.py:282
  35.8 15.0 %collective-permute-start.12 = (bf16[512,512]{1,0:T(8,128)(2,1)S(1)}, bf16[512,512]{1,0:T(8,128)(2,1)S(1)}, u32[]{:S(2)}, u32[]{:S(2)}) collective-permute-start(bf16[512,512]{1,0:T(8,128)(2,1)S(1)} %collective-permute-done.8.refs_8_), channel_id=1, source_target_pairs={{0,6},{1,7},{2,0},{3,1},{4,2},{5,3},{6,4},{7,5},{8,14},{9,15},{10,... | collective-permute-start | bytes 1572872 | tf_op jit(solution)/shard_map/send_W12/ppermute | solution.py:282
  44.3 6.4 %collective-permute-start.11 = (bf16[512,256]{1,0:T(8,128)(2,1)S(1)}, bf16[512,256]{1,0:T(8,128)(2,1)S(1)}, u32[]{:S(2)}, u32[]{:S(2)}) collective-permute-start(bf16[512,256]{1,0:T(8,128)(2,1)S(1)} %choose_Q.1), channel_id=1, source_target_pairs={{0,1},{1,0},{2,3},{3,2},{4,5},{5,4},{6,7},{7,6},{8,9},{9,8},{10,11... | collective-permute-start | bytes 786440 | tf_op jit(solution)/shard_map/send_Q/ppermute | solution.py:282

commit v7 on v6

--- a/solution.py
+++ b/solution.py
@@ -165,7 +165,7 @@
 
 
 def chunks_of(left):
-    chunk = min(BS, left.shape[0])
+    chunk = min(2 * BS, left.shape[0])
     return chunk, left.shape[0] // chunk
 
 

time: 53.2 us -> 53 us (level)
  Pallas kernels: 9.93 us -> 9.27 us
    pallas_call x9, Pallas kernels: 9.93 us -> 9.27 us  [kernel_call(): pl.pallas_call(kernel, out_shape=out_shape, in_specs=[pl.BlockSpec(memory...]
  transfers between devices with their start and end apart: 13 -> 13, of which waited for: 7 -> 7; matrix products, arithmetic and copies ran while one was open for 0% -> 0% of each run, Pallas kernels for 13% -> 12%
where the time goes in v7:
time: 53 us; the launch traced here: 52.8 us
  starting transfers between devices  28.2 us (53%)
  waiting for transfers between devices  15.1 us (28%)
  Pallas kernels  9.27 us (17%)
    ppermute x13, starting transfers between devices, moved(): lax.ppermute(block, axis, [(i, target(i) % count) for i in range(count)])  28.2 us
    ppermute x13, waiting for transfers between devices, moved(): lax.ppermute(block, axis, [(i, target(i) % count) for i in range(count)])  15.1 us
    pallas_call x9, Pallas kernels, kernel_call(): pl.pallas_call(kernel, out_shape=out_shape, in_specs=[pl.BlockSpec(memory...  9.27 us
  transfers between devices with their start and end apart: 13, of which 7 were waited for; matrix products, arithmetic and copies ran while one was open for 0% of the time, Pallas kernels for 12%

profile of v7, /device:TPU:0, one launch (start us, length us, event | category | flops | bytes accessed | tf_op | source)
XLA Modules:
  0.0 52.8 jit_solution(17487168955847140669)
XLA Ops:
  0.0 1.0 %mask_tile_1.1.refs_0_ = bf16[512,256]{1,0:T(8,128)(2,1)S(1)} custom-call(s32[2,4]{1,0:T(2,128)} %all_flags.4, bf16[512,1024]{1,0:T(8,128)(2,1)} %tile.2), custom_call_target="tpu_custom_call" | custom-call | bytes 1048592 | tf_op jit(solution)/shard_map/mask_tile_1/pallas_call | solution.py:38
  1.0 5.1 %collective-permute-start.3 = (bf16[512,256]{1,0:T(8,128)(2,1)S(1)}, bf16[512,256]{1,0:T(8,128)(2,1)S(1)}, u32[]{:S(2)}, u32[]{:S(2)}) collective-permute-start(bf16[512,256]{1,0:T(8,128)(2,1)S(1)} %mask_tile_1.1.refs_0_), channel_id=1, source_target_pairs={{0,6},{1,7},{2,0},{3,1},{4,2},{5,3},{6,4},{7,5},{8,14},{9,15},{10,... | collective-permute-start | bytes 786440 | tf_op jit(solution)/shard_map/send_Zb/ppermute | solution.py:282
  6.1 1.5 %collective-permute-start.5 = (bf16[512,256]{1,0:T(8,128)(2,1)S(1)}, bf16[512,256]{1,0:T(8,128)(2,1)S(1)}, u32[]{:S(2)}, u32[]{:S(2)}) collective-permute-start(bf16[512,256]{1,0:T(8,128)(2,1)S(1)} %mask_tile_1.1.refs_0_), channel_id=1, source_target_pairs={{0,1},{1,0},{2,3},{3,2},{4,5},{5,4},{6,7},{7,6},{8,9},{9,8},{10,11... | collective-permute-start | bytes 786440 | tf_op jit(solution)/shard_map/send_Db/ppermute | solution.py:282
  7.6 1.5 %collective-permute-start = (bf16[256,2048]{1,0:T(8,128)(2,1)}, bf16[256,2048]{1,0:T(8,128)(2,1)S(1)}, u32[]{:S(2)}, u32[]{:S(2)}) collective-permute-start(bf16[256,2048]{1,0:T(8,128)(2,1)} %refs_0_.1), channel_id=1, source_target_pairs={{0,16},{8,24},{16,0},{24,8},{1,17},{9,25},{17,1},{25,9},{2,18},{10... | collective-permute-start | bytes 3145736 | tf_op jit(solution)/shard_map/send_Ax/ppermute | solution.py:282
  9.1 1.2 %mask_tile_2.1 = (bf16[512,256]{1,0:T(8,128)(2,1)S(1)}, bf16[512,512]{1,0:T(8,128)(2,1)S(1)}) custom-call(s32[2,4]{1,0:T(2,128)} %all_flags.4, bf16[512,1024]{1,0:T(8,128)(2,1)} %tile.2), custom_call_target="tpu_custom_call" | custom-call | flops 6000000000 | bytes 1048592 | tf_op jit(solution)/shard_map/mask_tile_2/pallas_call | solution.py:38
  10.3 0.0 copy-start
  10.3 0.5 collective-permute-start.2
  10.8 2.0 %collective-permute-done.3.refs_1_ = bf16[512,256]{1,0:T(8,128)(2,1)S(1)} collective-permute-done((bf16[512,256]{1,0:T(8,128)(2,1)S(1)}, bf16[512,256]{1,0:T(8,128)(2,1)S(1)}, u32[]{:S(2)}, u32[]{:S(2)}) %collective-permute-start.3) | collective-permute-done | bytes 262176 | tf_op jit(solution)/shard_map/send_Zb/ppermute | solution.py:282
  12.8 1.1 %collective-permute-done.5.on_even = bf16[512,256]{1,0:T(8,128)(2,1)S(1)} collective-permute-done((bf16[512,256]{1,0:T(8,128)(2,1)S(1)}, bf16[512,256]{1,0:T(8,128)(2,1)S(1)}, u32[]{:S(2)}, u32[]{:S(2)}) %collective-permute-start.5) | collective-permute-done | bytes 262176 | tf_op jit(solution)/shard_map/send_Db/ppermute | solution.py:282
  13.9 1.5 %collective-permute-start.6 = (bf16[512,256]{1,0:T(8,128)(2,1)S(1)}, bf16[512,256]{1,0:T(8,128)(2,1)S(1)}, u32[]{:S(2)}, u32[]{:S(2)}) collective-permute-start(bf16[512,256]{1,0:T(8,128)(2,1)S(1)} %collective-permute-done.3.refs_1_), channel_id=1, source_target_pairs={{0,1},{1,0},{2,3},{3,2},{4,5},{5,4},{6,7},{7,6},{8,9},{9,8},{10,11... | collective-permute-start | bytes 786440 | tf_op jit(solution)/shard_map/send_Sb/ppermute | solution.py:282
  15.4 5.3 %collective-permute-done.6.on_odd.refs_2_ = bf16[512,256]{1,0:T(8,128)(2,1)S(1)} collective-permute-done((bf16[512,256]{1,0:T(8,128)(2,1)S(1)}, bf16[512,256]{1,0:T(8,128)(2,1)S(1)}, u32[]{:S(2)}, u32[]{:S(2)}) %collective-permute-start.6) | collective-permute-done | bytes 262176 | tf_op jit(solution)/shard_map/send_Sb/ppermute | solution.py:282
  20.7 2.7 %collective-permute-start.7 = (bf16[512,256]{1,0:T(8,128)(2,1)S(1)}, bf16[512,256]{1,0:T(8,128)(2,1)S(1)}, u32[]{:S(2)}, u32[]{:S(2)}) collective-permute-start(bf16[512,256]{1,0:T(8,128)(2,1)S(1)} %get-tuple-element.31.on_odd.refs_4_), channel_id=1, source_target_pairs={{0,6},{1,7},{2,0},{3,1},{4,2},{5,3},{6,4},{7,5},{8,14},{9,15},{10,... | collective-permute-start | bytes 786440 | tf_op jit(solution)/shard_map/send_Zc/ppermute | solution.py:282
  23.5 1.8 %collective-permute-done.2.on_even.refs_9_ = bf16[512,512]{1,0:T(8,128)(2,1)S(1)} collective-permute-done((bf16[512,512]{1,0:T(8,128)(2,1)S(1)}, bf16[512,512]{1,0:T(8,128)(2,1)S(1)}, u32[]{:S(2)}, u32[]{:S(2)}) %collective-permute-start.2) | collective-permute-done | bytes 524320 | tf_op jit(solution)/shard_map/send_Z12/ppermute | solution.py:282
  25.3 0.4 collective-permute-start.8
  25.6 3.1 %collective-permute-done.7.on_even.refs_5_ = bf16[512,256]{1,0:T(8,128)(2,1)S(1)} collective-permute-done((bf16[512,256]{1,0:T(8,128)(2,1)S(1)}, bf16[512,256]{1,0:T(8,128)(2,1)S(1)}, u32[]{:S(2)}, u32[]{:S(2)}) %collective-permute-start.7) | collective-permute-done | bytes 262176 | tf_op jit(solution)/shard_map/send_Zc/ppermute | solution.py:282
  28.8 4.1 %collective-permute-start.10 = (bf16[512,256]{1,0:T(8,128)(2,1)S(1)}, bf16[512,256]{1,0:T(8,128)(2,1)S(1)}, u32[]{:S(2)}, u32[]{:S(2)}) collective-permute-start(bf16[512,256]{1,0:T(8,128)(2,1)S(1)} %choose_X.1), channel_id=1, source_target_pairs={{0,6},{1,7},{2,0},{3,1},{4,2},{5,3},{6,4},{7,5},{8,14},{9,15},{10,... | collective-permute-start | bytes 786440 | tf_op jit(solution)/shard_map/send_X/ppermute | solution.py:282
  32.9 0.0 copy-done
  32.9 0.0 collective-permute-start.1
  32.9 0.0 collective-permute-done.refs_1_
  32.9 0.5 collective-permute-start.4
  33.4 1.5 %collective-permute-start.9 = (bf16[512,256]{1,0:T(8,128)(2,1)S(1)}, bf16[512,256]{1,0:T(8,128)(2,1)S(1)}, u32[]{:S(2)}, u32[]{:S(2)}) collective-permute-start(bf16[512,256]{1,0:T(8,128)(2,1)S(1)} %collective-permute-done.7.on_even.refs_5_), channel_id=1, source_target_pairs={{0,1},{1,0},{2,3},{3,2},{4,5},{5,4},{6,7},{7,6},{8,9},{9,8},{10,11... | collective-permute-start | bytes 786440 | tf_op jit(solution)/shard_map/send_Sc/ppermute | solution.py:282
  34.9 0.9 %collective-permute-done.8.refs_8_ = bf16[512,512]{1,0:T(8,128)(2,1)S(1)} collective-permute-done((bf16[512,512]{1,0:T(8,128)(2,1)S(1)}, bf16[512,512]{1,0:T(8,128)(2,1)S(1)}, u32[]{:S(2)}, u32[]{:S(2)}) %collective-permute-start.8) | collective-permute-done | bytes 524320 | tf_op jit(solution)/shard_map/send_Y12/ppermute | solution.py:282
  35.8 7.3 %collective-permute-start.12 = (bf16[512,512]{1,0:T(8,128)(2,1)S(1)}, bf16[512,512]{1,0:T(8,128)(2,1)S(1)}, u32[]{:S(2)}, u32[]{:S(2)}) collective-permute-start(bf16[512,512]{1,0:T(8,128)(2,1)S(1)} %collective-permute-done.8.refs_8_), channel_id=1, source_target_pairs={{0,6},{1,7},{2,0},{3,1},{4,2},{5,3},{6,4},{7,5},{8,14},{9,15},{10,... | collective-permute-start | bytes 1572872 | tf_op jit(solution)/shard_map/send_W12/ppermute | solution.py:282
  43.1 0.0 collective-permute-done.10.on_even.on_odd
  43.2 0.0 collective-permute-done.1.refs_2_
  43.2 0.0 collective-permute-done.4.refs_3_
  43.2 1.1 %stack_rows.1.left = bf16[1024,2048]{1,0:T(8,128)(2,1)S(1)} custom-call(s32[4,8]{1,0:T(4,128)} %all_flags.5, bf16[256,2048]{1,0:T(8,128)(2,1)S(1)} %copy-done, bf16[256,2048]{1,0:T(8,128)(2,1)S(1)} %collective-permute-done.refs_1_, bf16[256,2048]{1,0:T(8,128)(2,1)S(1)} %collective-permute-done.1.refs_2_, bf16[256,2048]{1,0:T(8,128)(2,1)S(1)} %collective-permute-done.4.refs_3_), custom_call_target="tpu_custom_call" | custom-call | flops 12000000000 | bytes 4194368 | tf_op jit(solution)/shard_map/stack_rows/pallas_call | solution.py:38
  44.3 1.6 %collective-permute-start.11 = (bf16[512,256]{1,0:T(8,128)(2,1)S(1)}, bf16[512,256]{1,0:T(8,128)(2,1)S(1)}, u32[]{:S(2)}, u32[]{:S(2)}) collective-permute-start(bf16[512,256]{1,0:T(8,128)(2,1)S(1)} %choose_Q.1), channel_id=1, source_target_pairs={{0,1},{1,0},{2,3},{3,2},{4,5},{5,4},{6,7},{7,6},{8,9},{9,8},{10,11... | collective-permute-start | bytes 786440 | tf_op jit(solution)/shard_map/send_Q/ppermute | solution.py:282
  45.9 0.0 collective-permute-done.9.refs_6_
  45.9 3.9 %sum_early.1 = (bf16[1024,256]{1,0:T(8,128)(2,1)S(1)}, f32[1024,768]{1,0:T(8,128)S(1)}) custom-call(bf16[1024,2048]{1,0:T(8,128)(2,1)S(1)} %stack_rows.1.left, bf16[512,256]{1,0:T(8,128)(2,1)S(1)} %mask_tile_1.1.refs_0_, bf16[512,256]{1,0:T(8,128)(2,1)S(1)} %collective-permute-done.3.refs_1_, bf16[512,256]{1,0:T(8,128)(2,1)S(1)} %collective-permute-done.6.on_odd.refs_2_, ...), custom_call_target="tpu_custom_call" | custom-call | flops 3000000000 | bytes 7602176 | tf_op jit(solution)/shard_map/sum_early/pallas_call | solution.py:38
  49.8 0.9 %collective-permute-done.11.refs_0_ = bf16[512,256]{1,0:T(8,128)(2,1)S(1)} collective-permute-done((bf16[512,256]{1,0:T(8,128)(2,1)S(1)}, bf16[512,256]{1,0:T(8,128)(2,1)S(1)}, u32[]{:S(2)}, u32[]{:S(2)}) %collective-permute-start.11) | collective-permute-done | bytes 262176 | tf_op jit(solution)/shard_map/send_Q/ppermute | solution.py:282
  50.7 0.0 collective-permute-done.12.refs_1_
  50.7 2.1 %sum_last.1 = bf16[1024,1024]{1,0:T(8,128)(2,1)} custom-call(bf16[1024,2048]{1,0:T(8,128)(2,1)S(1)} %stack_rows.1.left, bf16[512,256]{1,0:T(8,128)(2,1)S(1)} %collective-permute-done.11.refs_0_, bf16[512,512]{1,0:T(8,128)(2,1)S(1)} %collective-permute-done.12.refs_1_, f32[1024,768]{1,0:T(8,128)S(1)} %get-tuple-element.45.refs_2_, ...), custom_call_target="tpu_custom_call" | custom-call | flops 6000000000 | bytes 7077888 | tf_op jit(solution)/shard_map/sum_last/pallas_call | solution.py:38
  (4 shorter events, 0.1 us)
Async XLA Ops:
  1.0 11.8 %collective-permute-start.3 = (bf16[512,256]{1,0:T(8,128)(2,1)S(1)}, bf16[512,256]{1,0:T(8,128)(2,1)S(1)}, u32[]{:S(2)}, u32[]{:S(2)}) collective-permute-start(bf16[512,256]{1,0:T(8,128)(2,1)S(1)} %mask_tile_1.1.refs_0_), channel_id=1, source_target_pairs={{0,6},{1,7},{2,0},{3,1},{4,2},{5,3},{6,4},{7,5},{8,14},{9,15},{10,... | collective-permute-start | bytes 786440 | tf_op jit(solution)/shard_map/send_Zb/ppermute | solution.py:282
  6.1 7.8 %collective-permute-start.5 = (bf16[512,256]{1,0:T(8,128)(2,1)S(1)}, bf16[512,256]{1,0:T(8,128)(2,1)S(1)}, u32[]{:S(2)}, u32[]{:S(2)}) collective-permute-start(bf16[512,256]{1,0:T(8,128)(2,1)S(1)} %mask_tile_1.1.refs_0_), channel_id=1, source_target_pairs={{0,1},{1,0},{2,3},{3,2},{4,5},{5,4},{6,7},{7,6},{8,9},{9,8},{10,11... | collective-permute-start | bytes 786440 | tf_op jit(solution)/shard_map/send_Db/ppermute | solution.py:282
  7.6 25.3 %collective-permute-start = (bf16[256,2048]{1,0:T(8,128)(2,1)}, bf16[256,2048]{1,0:T(8,128)(2,1)S(1)}, u32[]{:S(2)}, u32[]{:S(2)}) collective-permute-start(bf16[256,2048]{1,0:T(8,128)(2,1)} %refs_0_.1), channel_id=1, source_target_pairs={{0,16},{8,24},{16,0},{24,8},{1,17},{9,25},{17,1},{25,9},{2,18},{10... | collective-permute-start | bytes 3145736 | tf_op jit(solution)/shard_map/send_Ax/ppermute | solution.py:282
  10.3 22.6 %copy-start = (bf16[256,2048]{1,0:T(8,128)(2,1)S(1)}, bf16[256,2048]{1,0:T(8,128)(2,1)}, u32[]{:S(2)}) copy-start(bf16[256,2048]{1,0:T(8,128)(2,1)} %refs_0_.1) | copy-start | bytes 3145732
  10.3 14.9 %collective-permute-start.2 = (bf16[512,512]{1,0:T(8,128)(2,1)S(1)}, bf16[512,512]{1,0:T(8,128)(2,1)S(1)}, u32[]{:S(2)}, u32[]{:S(2)}) collective-permute-start(bf16[512,512]{1,0:T(8,128)(2,1)S(1)} %get-tuple-element.27.on_odd.refs_7_), channel_id=1, source_target_pairs={{0,6},{1,7},{2,0},{3,1},{4,2},{5,3},{6,4},{7,5},{8,14},{9,15},{10,... | collective-permute-start | bytes 1572872 | tf_op jit(solution)/shard_map/send_Z12/ppermute | solution.py:282
  13.9 6.9 %collective-permute-start.6 = (bf16[512,256]{1,0:T(8,128)(2,1)S(1)}, bf16[512,256]{1,0:T(8,128)(2,1)S(1)}, u32[]{:S(2)}, u32[]{:S(2)}) collective-permute-start(bf16[512,256]{1,0:T(8,128)(2,1)S(1)} %collective-permute-done.3.refs_1_), channel_id=1, source_target_pairs={{0,1},{1,0},{2,3},{3,2},{4,5},{5,4},{6,7},{7,6},{8,9},{9,8},{10,11... | collective-permute-start | bytes 786440 | tf_op jit(solution)/shard_map/send_Sb/ppermute | solution.py:282
  20.7 8.1 %collective-permute-start.7 = (bf16[512,256]{1,0:T(8,128)(2,1)S(1)}, bf16[512,256]{1,0:T(8,128)(2,1)S(1)}, u32[]{:S(2)}, u32[]{:S(2)}) collective-permute-start(bf16[512,256]{1,0:T(8,128)(2,1)S(1)} %get-tuple-element.31.on_odd.refs_4_), channel_id=1, source_target_pairs={{0,6},{1,7},{2,0},{3,1},{4,2},{5,3},{6,4},{7,5},{8,14},{9,15},{10,... | collective-permute-start | bytes 786440 | tf_op jit(solution)/shard_map/send_Zc/ppermute | solution.py:282
  25.3 10.5 %collective-permute-start.8 = (bf16[512,512]{1,0:T(8,128)(2,1)S(1)}, bf16[512,512]{1,0:T(8,128)(2,1)S(1)}, u32[]{:S(2)}, u32[]{:S(2)}) collective-permute-start(bf16[512,512]{1,0:T(8,128)(2,1)S(1)} %choose_Y12.1), channel_id=1, source_target_pairs={{0,1},{1,0},{2,3},{3,2},{4,5},{5,4},{6,7},{7,6},{8,9},{9,8},{10,11... | collective-permute-start | bytes 1572872 | tf_op jit(solution)/shard_map/send_Y12/ppermute | solution.py:282
  28.8 14.3 %collective-permute-start.10 = (bf16[512,256]{1,0:T(8,128)(2,1)S(1)}, bf16[512,256]{1,0:T(8,128)(2,1)S(1)}, u32[]{:S(2)}, u32[]{:S(2)}) collective-permute-start(bf16[512,256]{1,0:T(8,128)(2,1)S(1)} %choose_X.1), channel_id=1, source_target_pairs={{0,6},{1,7},{2,0},{3,1},{4,2},{5,3},{6,4},{7,5},{8,14},{9,15},{10,... | collective-permute-start | bytes 786440 | tf_op jit(solution)/shard_map/send_X/ppermute | solution.py:282
  32.9 10.3 %collective-permute-start.1 = (bf16[256,2048]{1,0:T(8,128)(2,1)S(1)}, bf16[256,2048]{1,0:T(8,128)(2,1)S(1)}, u32[]{:S(2)}, u32[]{:S(2)}) collective-permute-start(bf16[256,2048]{1,0:T(8,128)(2,1)S(1)} %copy-done), channel_id=1, source_target_pairs={{0,8},{8,0},{16,24},{24,16},{1,9},{9,1},{17,25},{25,17},{2,10},{10... | collective-permute-start | bytes 3145736 | tf_op jit(solution)/shard_map/send_Af/ppermute | solution.py:282
  32.9 10.3 %collective-permute-start.4 = (bf16[256,2048]{1,0:T(8,128)(2,1)S(1)}, bf16[256,2048]{1,0:T(8,128)(2,1)S(1)}, u32[]{:S(2)}, u32[]{:S(2)}) collective-permute-start(bf16[256,2048]{1,0:T(8,128)(2,1)S(1)} %collective-permute-done.refs_1_), channel_id=1, source_target_pairs={{0,8},{8,0},{16,24},{24,16},{1,9},{9,1},{17,25},{25,17},{2,10},{10... | collective-permute-start | bytes 3145736 | tf_op jit(solution)/shard_map/send_Ar/ppermute | solution.py:282
  33.4 12.5 %collective-permute-start.9 = (bf16[512,256]{1,0:T(8,128)(2,1)S(1)}, bf16[512,256]{1,0:T(8,128)(2,1)S(1)}, u32[]{:S(2)}, u32[]{:S(2)}) collective-permute-start(bf16[512,256]{1,0:T(8,128)(2,1)S(1)} %collective-permute-done.7.on_even.refs_5_), channel_id=1, source_target_pairs={{0,1},{1,0},{2,3},{3,2},{4,5},{5,4},{6,7},{7,6},{8,9},{9,8},{10,11... | collective-permute-start | bytes 786440 | tf_op jit(solution)/shard_map/send_Sc/ppermute | solution.py:282
  35.8 14.9 %collective-permute-start.12 = (bf16[512,512]{1,0:T(8,128)(2,1)S(1)}, bf16[512,512]{1,0:T(8,128)(2,1)S(1)}, u32[]{:S(2)}, u32[]{:S(2)}) collective-permute-start(bf16[512,512]{1,0:T(8,128)(2,1)S(1)} %collective-permute-done.8.refs_8_), channel_id=1, source_target_pairs={{0,6},{1,7},{2,0},{3,1},{4,2},{5,3},{6,4},{7,5},{8,14},{9,15},{10,... | collective-permute-start | bytes 1572872 | tf_op jit(solution)/shard_map/send_W12/ppermute | solution.py:282
  44.3 6.4 %collective-permute-start.11 = (bf16[512,256]{1,0:T(8,128)(2,1)S(1)}, bf16[512,256]{1,0:T(8,128)(2,1)S(1)}, u32[]{:S(2)}, u32[]{:S(2)}) collective-permute-start(bf16[512,256]{1,0:T(8,128)(2,1)S(1)} %choose_Q.1), channel_id=1, source_target_pairs={{0,1},{1,0},{2,3},{3,2},{4,5},{5,4},{6,7},{7,6},{8,9},{9,8},{10,11... | collective-permute-start | bytes 786440 | tf_op jit(solution)/shard_map/send_Q/ppermute | solution.py:282
